TPU v7x, 32 devices: a whole 2x2x4 slice. The times are simulated.
32 devices in a mesh: ctx: 4 (over y, x), fsdp: 8 (over z, core).
Axes of the slice: x: 2, y: 2, z: 4, core: 2. Of those that a mesh axis runs over, the one named last changes fastest.
Arguments:
- tokens: bfloat16 [2, 8, 1024, 1024], P(None, 'fsdp', 'ctx'), may hold values from -6 to 6
- doc_lengths: int32 [2, 8, 4], P(None, 'fsdp'), may hold values from 1 to 512, 1024 in all within a row
- w_query: bfloat16 [1024, 1024], P(('ctx', 'fsdp')), may hold values from -0.1875 to 0.1875
- b_query: bfloat16 [1024], P(('ctx', 'fsdp')), may hold values from -1.75 to 1.75
- w_key: bfloat16 [1024, 1024], P(('ctx', 'fsdp')), may hold values from -0.1875 to 0.1875
- w_value: bfloat16 [1024, 1024], P(('ctx', 'fsdp')), may hold values from -0.1875 to 0.1875
- b_value: bfloat16 [1024], P(('ctx', 'fsdp')), may hold values from -0.3125 to 0.3125
- w_out: bfloat16 [1024, 1024], P(('ctx', 'fsdp')), may hold values from -1.5 to 1.5
- b_out: bfloat16 [1024], P(('ctx', 'fsdp')), may hold values from -1.75 to 1.75
- ln1_gain: bfloat16 [1024], P(('ctx', 'fsdp')), may hold values from 0.5 to 1.5
- ln1_bias: bfloat16 [1024], P(('ctx', 'fsdp')), may hold values from -1.75 to 1.75
- w_up: bfloat16 [1024, 4096], P(('ctx', 'fsdp')), may hold values from -0.1875 to 0.1875
- b_up: bfloat16 [4096], P(('ctx', 'fsdp')), may hold values from -1.75 to 1.75
- w_down: bfloat16 [4096, 1024], P(('ctx', 'fsdp')), may hold values from -0.09375 to 0.09375
- b_down: bfloat16 [1024], P(('ctx', 'fsdp')), may hold values from -1.75 to 1.75
- ln2_gain: bfloat16 [1024], P(('ctx', 'fsdp')), may hold values from 0.5 to 1.5
- ln2_bias: bfloat16 [1024], P(('ctx', 'fsdp')), may hold values from -1.75 to 1.75
- cotangent: bfloat16 [2, 8, 1024, 1024], P(None, 'fsdp', 'ctx'), may hold values from -6 to 6
Outputs:
- output: bfloat16 [2, 8, 1024, 1024], P(None, 'fsdp', 'ctx')
- grad_tokens: float32 [2, 8, 1024, 1024], P(None, 'fsdp', 'ctx')
- grad_w_query: float32 [1024, 1024], P(('ctx', 'fsdp'))
- grad_b_query: float32 [1024], P(('ctx', 'fsdp'))
- grad_w_key: float32 [1024, 1024], P(('ctx', 'fsdp'))
- grad_w_value: float32 [1024, 1024], P(('ctx', 'fsdp'))
- grad_b_value: float32 [1024], P(('ctx', 'fsdp'))
- grad_w_out: float32 [1024, 1024], P(('ctx', 'fsdp'))
- grad_b_out: float32 [1024], P(('ctx', 'fsdp'))
- grad_ln1_gain: float32 [1024], P(('ctx', 'fsdp'))
- grad_ln1_bias: float32 [1024], P(('ctx', 'fsdp'))
- grad_w_up: float32 [1024, 4096], P(('ctx', 'fsdp'))
- grad_b_up: float32 [4096], P(('ctx', 'fsdp'))
- grad_w_down: float32 [4096, 1024], P(('ctx', 'fsdp'))
- grad_b_down: float32 [1024], P(('ctx', 'fsdp'))
- grad_ln2_gain: float32 [1024], P(('ctx', 'fsdp'))
- grad_ln2_bias: float32 [1024], P(('ctx', 'fsdp'))
Inputs may be any that keep to these rules, and one draw needn't show every extreme that they name: `doc_lengths`: in each stream the 4 documents fill the 1024 positions in order, and the longest is exactly 512.
All inputs are finite; a program needn't handle non-finite values.
Results may differ from a plain program's by a relative error of at most 0.014.
Values may be sent and summed in bfloat16 or wider, within the bound.
No kernel may reach another device: no remote copies, remote signals or barrier semaphores. Data moves between devices by JAX's collectives and lax.ppermute only.
A program may use at most 256 MiB of HBM per device.

v0:
```python
import jax
import jax.numpy as jnp
from jax import lax
from jax.sharding import PartitionSpec as P

H = 16
HD = 64


EPSILON = 1e-12
SCORE_SCALE = 0.125
MASKED_SCORE = -1e30


def exact_gelu(values_in):
    return jax.nn.gelu(values_in, approximate=False)


def norm_forward(values_in, gain_vec, bias_vec):
    center = values_in - jnp.mean(values_in, axis=-1, keepdims=True)
    inverse = lax.rsqrt(jnp.mean(center * center, axis=-1, keepdims=True) + EPSILON)
    normed = center * inverse
    return (normed * gain_vec + bias_vec, normed, inverse)


def norm_backward(upstream, normed, inverse, gain_vec):
    scaled = upstream * gain_vec
    inner_sum = (
        scaled
        - jnp.mean(scaled, axis=-1, keepdims=True)
        - normed * jnp.mean(scaled * normed, axis=-1, keepdims=True)
    )
    return (inverse * inner_sum, jnp.sum(upstream * normed, axis=0), jnp.sum(upstream, axis=0))


def segment_ids(lengths, positions):
    starts = jnp.cumsum(lengths) - lengths
    return jnp.sum((positions[:, None] >= starts[None, :]).astype(jnp.int32), axis=1) - 1


def to_blocks(stacked):
    streams, row_count, _ = stacked.shape
    pieces = stacked.reshape(streams, row_count, H // 4, 4, HD)
    return jnp.moveaxis(pieces, 2, 1).reshape(streams * (H // 4), row_count, 4, HD)


def from_blocks(stacked, streams):
    _, row_count, heads_block, head_size = stacked.shape
    pieces = stacked.reshape(streams, H // 4, row_count, heads_block, head_size)
    return jnp.moveaxis(pieces, 1, 2).reshape(streams, row_count, H * HD)


def masked_scores(queries, keys_all, seg_rows, seg_cols):
    scores = (
        jnp.einsum("qgd,kgd->gqk", queries, keys_all, preferred_element_type=jnp.float32)
        * SCORE_SCALE
    )
    return jnp.where((seg_rows[:, None] == seg_cols[None, :])[None], scores, MASKED_SCORE)


def attend(operands):
    queries, keys_all, values_all, seg_rows, seg_cols = operands
    scores = masked_scores(queries, keys_all, seg_rows, seg_cols)
    top_score = jnp.max(scores, axis=-1, keepdims=True)
    exponent_terms = jnp.exp(scores - top_score)
    totals = jnp.sum(exponent_terms, axis=-1, keepdims=True)
    probs = exponent_terms / totals
    mixed = jnp.einsum(
        "gqk,kgd->qgd", probs.astype(jnp.bfloat16), values_all, preferred_element_type=jnp.float32
    )
    return (mixed, top_score + jnp.log(totals))


def attend_back(operands):
    queries, keys_all, values_all, seg_rows, seg_cols, log_totals, grad_mixed = operands
    scores = masked_scores(queries, keys_all, seg_rows, seg_cols)
    probs = jnp.exp(scores - log_totals)
    grad_values = jnp.einsum(
        "gqk,qgd->kgd", probs.astype(jnp.bfloat16), grad_mixed, preferred_element_type=jnp.float32
    )
    grad_probs = jnp.einsum(
        "qgd,kgd->gqk", grad_mixed, values_all, preferred_element_type=jnp.float32
    )
    central = jnp.sum(probs * grad_probs, axis=-1, keepdims=True)
    grad_scores = (probs * (grad_probs - central)).astype(jnp.bfloat16)
    grad_queries = (
        jnp.einsum("gqk,kgd->qgd", grad_scores, keys_all, preferred_element_type=jnp.float32)
        * SCORE_SCALE
    )
    grad_keys = (
        jnp.einsum("gqk,qgd->kgd", grad_scores, queries, preferred_element_type=jnp.float32)
        * SCORE_SCALE
    )
    return (grad_queries, grad_keys, grad_values)


def left_product(left, right):
    return jnp.einsum("ta,tb->ab", left, right, preferred_element_type=jnp.float32)


def right_transpose(left, right):
    return jnp.einsum("tb,ab->ta", left, right, preferred_element_type=jnp.float32)


def body(
    tokens,
    doc_lengths,
    w_query,
    b_query,
    w_key,
    w_value,
    b_value,
    w_out,
    b_out,
    ln1_gain,
    ln1_bias,
    w_up,
    b_up,
    w_down,
    b_down,
    ln2_gain,
    ln2_bias,
    cotangent,
):
    micro, per_device, ctx_rows, width = tokens.shape
    stream_len = ctx_rows * lax.axis_size("ctx")
    row_pos = lax.axis_index("ctx") * ctx_rows + jnp.arange(ctx_rows, dtype=jnp.int32)
    key_pos = jnp.arange(stream_len, dtype=jnp.int32)
    blocks_per = H // 4
    flat_rows = per_device * ctx_rows
    outputs = []
    input_grads = []
    accumulated = None
    for batch_index in range(micro):
        full = (
            lax.all_gather(w_query, ("ctx", "fsdp"), axis=0, tiled=True),
            lax.all_gather(b_query, ("ctx", "fsdp"), axis=0, tiled=True),
            lax.all_gather(w_key, ("ctx", "fsdp"), axis=0, tiled=True),
            lax.all_gather(w_value, ("ctx", "fsdp"), axis=0, tiled=True),
            lax.all_gather(b_value, ("ctx", "fsdp"), axis=0, tiled=True),
            lax.all_gather(w_out, ("ctx", "fsdp"), axis=0, tiled=True),
            lax.all_gather(b_out, ("ctx", "fsdp"), axis=0, tiled=True),
            lax.all_gather(ln1_gain, ("ctx", "fsdp"), axis=0, tiled=True),
            lax.all_gather(ln1_bias, ("ctx", "fsdp"), axis=0, tiled=True),
            lax.all_gather(w_up, ("ctx", "fsdp"), axis=0, tiled=True),
            lax.all_gather(b_up, ("ctx", "fsdp"), axis=0, tiled=True),
            lax.all_gather(w_down, ("ctx", "fsdp"), axis=0, tiled=True),
            lax.all_gather(b_down, ("ctx", "fsdp"), axis=0, tiled=True),
            lax.all_gather(ln2_gain, ("ctx", "fsdp"), axis=0, tiled=True),
            lax.all_gather(ln2_bias, ("ctx", "fsdp"), axis=0, tiled=True),
        )
        (
            query_mat,
            query_bias,
            key_mat,
            value_mat,
            value_bias,
            out_mat,
            out_bias,
            gain_one,
            bias_one,
            up_mat,
            up_bias,
            down_mat,
            down_bias,
            gain_two,
            bias_two,
        ) = full
        inputs = tokens[batch_index].reshape(flat_rows, width)
        queries = (
            jnp.dot(inputs, query_mat, preferred_element_type=jnp.float32) + query_bias
        ).astype(jnp.bfloat16)
        keys_mine = jnp.dot(inputs, key_mat, preferred_element_type=jnp.float32).astype(
            jnp.bfloat16
        )
        values_mine = (
            jnp.dot(inputs, value_mat, preferred_element_type=jnp.float32) + value_bias
        ).astype(jnp.bfloat16)
        keys_all, values_all = (
            lax.all_gather(
                keys_mine.reshape(per_device, ctx_rows, width), "ctx", axis=1, tiled=True
            ),
            lax.all_gather(
                values_mine.reshape(per_device, ctx_rows, width), "ctx", axis=1, tiled=True
            ),
        )
        lengths_now = doc_lengths[batch_index]
        seg_rows = jax.vmap(segment_ids, (0, None))(lengths_now, row_pos)
        seg_cols = jax.vmap(segment_ids, (0, None))(lengths_now, key_pos)
        rows_rep = jnp.repeat(seg_rows, blocks_per, axis=0)
        cols_rep = jnp.repeat(seg_cols, blocks_per, axis=0)
        query_blocks = to_blocks(queries.reshape(per_device, ctx_rows, width))
        key_blocks = to_blocks(keys_all)
        value_blocks = to_blocks(values_all)
        mixed_blocks, log_totals = lax.map(
            attend, (query_blocks, key_blocks, value_blocks, rows_rep, cols_rep)
        )
        mixed = from_blocks(mixed_blocks, per_device).reshape(flat_rows, width).astype(jnp.bfloat16)
        attended = jnp.dot(mixed, out_mat, preferred_element_type=jnp.float32) + out_bias
        first, normed_one, inverse_one = norm_forward(
            inputs.astype(jnp.float32) + attended, gain_one, bias_one
        )
        first_low = first.astype(jnp.bfloat16)
        hidden = jnp.dot(first_low, up_mat, preferred_element_type=jnp.float32) + up_bias
        activated_full, gelu_pull = jax.vjp(exact_gelu, hidden)
        activated = activated_full.astype(jnp.bfloat16)
        branch = jnp.dot(activated, down_mat, preferred_element_type=jnp.float32) + down_bias
        result, normed_two, inverse_two = norm_forward(first + branch, gain_two, bias_two)
        outputs.append(result.astype(jnp.bfloat16).reshape(per_device, ctx_rows, width))
        full = (
            lax.all_gather(w_query, ("ctx", "fsdp"), axis=0, tiled=True),
            lax.all_gather(b_query, ("ctx", "fsdp"), axis=0, tiled=True),
            lax.all_gather(w_key, ("ctx", "fsdp"), axis=0, tiled=True),
            lax.all_gather(w_value, ("ctx", "fsdp"), axis=0, tiled=True),
            lax.all_gather(b_value, ("ctx", "fsdp"), axis=0, tiled=True),
            lax.all_gather(w_out, ("ctx", "fsdp"), axis=0, tiled=True),
            lax.all_gather(b_out, ("ctx", "fsdp"), axis=0, tiled=True),
            lax.all_gather(ln1_gain, ("ctx", "fsdp"), axis=0, tiled=True),
            lax.all_gather(ln1_bias, ("ctx", "fsdp"), axis=0, tiled=True),
            lax.all_gather(w_up, ("ctx", "fsdp"), axis=0, tiled=True),
            lax.all_gather(b_up, ("ctx", "fsdp"), axis=0, tiled=True),
            lax.all_gather(w_down, ("ctx", "fsdp"), axis=0, tiled=True),
            lax.all_gather(b_down, ("ctx", "fsdp"), axis=0, tiled=True),
            lax.all_gather(ln2_gain, ("ctx", "fsdp"), axis=0, tiled=True),
            lax.all_gather(ln2_bias, ("ctx", "fsdp"), axis=0, tiled=True),
        )
        (
            query_mat,
            query_bias,
            key_mat,
            value_mat,
            value_bias,
            out_mat,
            out_bias,
            gain_one,
            bias_one,
            up_mat,
            up_bias,
            down_mat,
            down_bias,
            gain_two,
            bias_two,
        ) = full
        upstream = cotangent[batch_index].reshape(flat_rows, width).astype(jnp.float32)
        grad_h2, grad_gain_two, grad_bias_two = norm_backward(
            upstream, normed_two, inverse_two, gain_two
        )
        grad_branch = grad_h2.astype(jnp.bfloat16)
        grad_down_bias = jnp.sum(grad_branch.astype(jnp.float32), axis=0)
        grad_down_mat = left_product(activated, grad_branch)
        grad_activated = right_transpose(grad_branch, down_mat)
        grad_hidden = gelu_pull(grad_activated)[0].astype(jnp.bfloat16)
        grad_up_bias = jnp.sum(grad_hidden.astype(jnp.float32), axis=0)
        grad_up_mat = left_product(first_low, grad_hidden)
        grad_first = right_transpose(grad_hidden, up_mat) + grad_h2
        grad_h1, grad_gain_one, grad_bias_one = norm_backward(
            grad_first, normed_one, inverse_one, gain_one
        )
        grad_attended = grad_h1.astype(jnp.bfloat16)
        grad_out_bias = jnp.sum(grad_attended.astype(jnp.float32), axis=0)
        grad_out_mat = left_product(mixed, grad_attended)
        grad_mixed = right_transpose(grad_attended, out_mat).astype(jnp.bfloat16)
        grad_mixed_blocks = to_blocks(grad_mixed.reshape(per_device, ctx_rows, width))
        grad_query_blocks, grad_key_blocks, grad_value_blocks = lax.map(
            attend_back,
            (
                query_blocks,
                key_blocks,
                value_blocks,
                rows_rep,
                cols_rep,
                log_totals,
                grad_mixed_blocks,
            ),
        )
        grad_keys_all = from_blocks(grad_key_blocks, per_device)
        grad_values_all = from_blocks(grad_value_blocks, per_device)
        grad_keys_mine, grad_values_mine = (
            lax.psum_scatter(
                grad_keys_all.astype(jnp.bfloat16), "ctx", scatter_dimension=1, tiled=True
            ).astype(jnp.float32),
            lax.psum_scatter(
                grad_values_all.astype(jnp.bfloat16), "ctx", scatter_dimension=1, tiled=True
            ).astype(jnp.float32),
        )
        grad_queries = (
            from_blocks(grad_query_blocks, per_device)
            .reshape(flat_rows, width)
            .astype(jnp.bfloat16)
        )
        grad_keys = grad_keys_mine.reshape(flat_rows, width).astype(jnp.bfloat16)
        grad_values = grad_values_mine.reshape(flat_rows, width).astype(jnp.bfloat16)
        grad_query_bias = jnp.sum(grad_queries.astype(jnp.float32), axis=0)
        grad_value_bias = jnp.sum(grad_values.astype(jnp.float32), axis=0)
        grad_query_mat = left_product(inputs, grad_queries)
        grad_key_mat = left_product(inputs, grad_keys)
        grad_value_mat = left_product(inputs, grad_values)
        grad_inputs = (
            grad_h1
            + right_transpose(grad_queries, query_mat)
            + right_transpose(grad_keys, key_mat)
            + right_transpose(grad_values, value_mat)
        )
        input_grads.append(grad_inputs.reshape(per_device, ctx_rows, width))
        owned = (
            lax.psum_scatter(grad_query_mat, ("ctx", "fsdp"), scatter_dimension=0, tiled=True),
            lax.psum_scatter(grad_query_bias, ("ctx", "fsdp"), scatter_dimension=0, tiled=True),
            lax.psum_scatter(grad_key_mat, ("ctx", "fsdp"), scatter_dimension=0, tiled=True),
            lax.psum_scatter(grad_value_mat, ("ctx", "fsdp"), scatter_dimension=0, tiled=True),
            lax.psum_scatter(grad_value_bias, ("ctx", "fsdp"), scatter_dimension=0, tiled=True),
            lax.psum_scatter(grad_out_mat, ("ctx", "fsdp"), scatter_dimension=0, tiled=True),
            lax.psum_scatter(grad_out_bias, ("ctx", "fsdp"), scatter_dimension=0, tiled=True),
            lax.psum_scatter(grad_gain_one, ("ctx", "fsdp"), scatter_dimension=0, tiled=True),
            lax.psum_scatter(grad_bias_one, ("ctx", "fsdp"), scatter_dimension=0, tiled=True),
            lax.psum_scatter(grad_up_mat, ("ctx", "fsdp"), scatter_dimension=0, tiled=True),
            lax.psum_scatter(grad_up_bias, ("ctx", "fsdp"), scatter_dimension=0, tiled=True),
            lax.psum_scatter(grad_down_mat, ("ctx", "fsdp"), scatter_dimension=0, tiled=True),
            lax.psum_scatter(grad_down_bias, ("ctx", "fsdp"), scatter_dimension=0, tiled=True),
            lax.psum_scatter(grad_gain_two, ("ctx", "fsdp"), scatter_dimension=0, tiled=True),
            lax.psum_scatter(grad_bias_two, ("ctx", "fsdp"), scatter_dimension=0, tiled=True),
        )
        accumulated = owned if accumulated is None else jax.tree.map(jnp.add, accumulated, owned)
    stacked_out = jnp.stack(outputs)
    stacked_grads = jnp.stack(input_grads)
    return (
        stacked_out,
        stacked_grads,
        accumulated[0],
        accumulated[1],
        accumulated[2],
        accumulated[3],
        accumulated[4],
        accumulated[5],
        accumulated[6],
        accumulated[7],
        accumulated[8],
        accumulated[9],
        accumulated[10],
        accumulated[11],
        accumulated[12],
        accumulated[13],
        accumulated[14],
    )


def solution(mesh):
    placed = (
        P(None, "fsdp", "ctx", None),
        P(None, "fsdp", None),
        P(("ctx", "fsdp"), None),
        P(("ctx", "fsdp")),
        P(("ctx", "fsdp"), None),
        P(("ctx", "fsdp"), None),
        P(("ctx", "fsdp")),
        P(("ctx", "fsdp"), None),
        P(("ctx", "fsdp")),
        P(("ctx", "fsdp")),
        P(("ctx", "fsdp")),
        P(("ctx", "fsdp"), None),
        P(("ctx", "fsdp")),
        P(("ctx", "fsdp"), None),
        P(("ctx", "fsdp")),
        P(("ctx", "fsdp")),
        P(("ctx", "fsdp")),
        P(None, "fsdp", "ctx", None),
    )
    return jax.shard_map(
        body,
        mesh=mesh,
        in_specs=placed,
        out_specs=(
            P(None, "fsdp", "ctx", None),
            P(None, "fsdp", "ctx", None),
            P(("ctx", "fsdp"), None),
            P(("ctx", "fsdp")),
            P(("ctx", "fsdp"), None),
            P(("ctx", "fsdp"), None),
            P(("ctx", "fsdp")),
            P(("ctx", "fsdp"), None),
            P(("ctx", "fsdp")),
            P(("ctx", "fsdp")),
            P(("ctx", "fsdp")),
            P(("ctx", "fsdp"), None),
            P(("ctx", "fsdp")),
            P(("ctx", "fsdp"), None),
            P(("ctx", "fsdp")),
            P(("ctx", "fsdp")),
            P(("ctx", "fsdp")),
        ),
        check_vma=False,
    )
```

profile of v0, /device:TPU:1, one launch (start us, length us, event | category | flops | bytes accessed | tf_op | source)
XLA Modules:
  0.0 1786.9 jit_solution(13232261122871129861)
XLA Ops:
  16.2 40.9 %all-reduce.18 = (bf16[1024]{0:T(1024)(128)(2,1)S(1)}, bf16[1024]{0:T(1024)(128)(2,1)S(1)}, bf16[1024]{0:T(1024)(128)(2,1)S(1)}, bf16[1024]{0:T(1024)(128)(2,1)S...) all-reduce(bf16[1024]{0:T(1024)(128)(2,1)S(1)} %dynamic-update-slic, ...), channel_id=1, replica_groups=mesh['ctx'=4,'fsdp'=8] {'ctx','fsdp'}, use_global_device_ids=true, to_apply=%add | all-reduce | flops 8192 | bytes 32768
  57.1 13.0 all-gather.16.cloned.1.call-done
  73.5 55.0 %all-gather.20.cloned.1.call-done = bf16[1024,1024]{1,0:T(8,128)(2,1)} async-done(((bf16[32,1024]{1,0:T(8,128)(2,1)}), bf16[1024,1024]{1,0:T(8,128)(2,1)}) %all-gather.20.cloned.1.call-update) | async-done | bytes 2097168 | tf_op jit(solution)/shard_map/all_gather | solution.py:138
  138.6 39.3 %all-gather.4 = bf16[32,1,128]{2,1,0:T(2,128)(2,1)S(1)} all-gather(bf16[1,1,128]{2,1,0:T(2,128)(2,1)S(1)} %bitcast.493), channel_id=1, replica_groups=mesh['ctx'=4,'fsdp'=8] {'ctx','fsdp'}, dimensions={0}, use_global_device_ids=true | all-gather | bytes 8448 | tf_op jit(solution)/shard_map/all_gather | solution.py:146
  195.8 27.2 %all-gather.28.cloned.1.call-done = bf16[1024,1024]{1,0:T(8,128)(2,1)} async-done(((bf16[256,1024]{1,0:T(8,128)(2,1)}), bf16[1024,1024]{1,0:T(8,128)(2,1)}) %all-gather.28.cloned.1.call-update) | async-done | bytes 2097168 | tf_op jit(solution)/shard_map/all_gather | solution.py:183
  227.1 33.5 %all-gather.30.cloned.1.call-done = bf16[1024,1024]{1,0:T(8,128)(2,1)} async-done(((bf16[256,1024]{1,0:T(8,128)(2,1)}), bf16[1024,1024]{1,0:T(8,128)(2,1)}) %all-gather.30.cloned.1.call-update) | async-done | bytes 2097168 | tf_op jit(solution)/shard_map/all_gather | solution.py:180
  264.4 26.7 %while.52 = (s32[]{:T(128)}, bf16[4,256,4,64]{1,3,2,0:T(8,128)(2,1)}, f32[4,4,256,1]{2,1,3,0:T(4,128)S(1)}, bf16[4,1024,4,64]{1,3,2,0:T(8,128)(2,1)}, s32[4,256]...) while((s32[]{:T(128)}, ...), condition=%wide.region_6.7_spmd, body=%wide.region_3.6_spmd.sunk | while | flops 281279488 | bytes 19317928 | solution.py:195
  301.6 33.2 %all-gather.34.cloned.1.call-done = bf16[1024,1024]{1,0:T(8,128)(2,1)} async-done(((bf16[256,1024]{1,0:T(8,128)(2,1)}), bf16[1024,1024]{1,0:T(8,128)(2,1)}) %all-gather.34.cloned.1.call-update) | async-done | bytes 2097168 | tf_op jit(solution)/shard_map/all_gather | solution.py:180
  337.8 57.0 %all-gather.22.cloned.1.call-done = bf16[1024,1024]{1,0:T(8,128)(2,1)} async-done(((bf16[32,1024]{1,0:T(8,128)(2,1)}), bf16[1024,1024]{1,0:T(8,128)(2,1)}) %all-gather.22.cloned.1.call-update) | async-done | bytes 2097168 | tf_op jit(solution)/shard_map/all_gather | solution.py:141
  398.7 23.4 %while.53 = (s32[]{:T(128)}, bf16[4,256,4,64]{1,3,2,0:T(8,128)(2,1)S(1)}, f32[4,4,256,1]{2,1,3,0:T(4,128)S(1)}, bf16[4,1024,4,64]{1,3,2,0:T(8,128)(2,1)}, s32[4,...) while((s32[]{:T(128)}, ...), condition=%wide.region_17.18_spmd, body=%wide.region_14.17_spmd.sunk | while | flops 281279488 | bytes 15123569 | solution.py:195
  426.2 47.9 %all-gather.24.cloned.1.call-done = bf16[1024,4096]{1,0:T(8,128)(2,1)} async-done(((bf16[32,4096]{1,0:T(8,128)(2,1)}), bf16[1024,4096]{1,0:T(8,128)(2,1)}) %all-gather.24.cloned.1.call-update) | async-done | bytes 8388624 | tf_op jit(solution)/shard_map/all_gather | solution.py:145
  474.1 16.5 multiply_convert_fusion.3
  490.6 62.4 %all-gather.26.cloned.1.call-done = bf16[4096,1024]{1,0:T(8,128)(2,1)} async-done(((bf16[128,1024]{1,0:T(8,128)(2,1)}), bf16[4096,1024]{1,0:T(8,128)(2,1)}) %all-gather.26.cloned.1.call-update) | async-done | bytes 8388624 | tf_op jit(solution)/shard_map/all_gather | solution.py:147
  560.0 13.4 multiply_convert_fusion.2
  580.3 13.1 convert_reduce_fusion.1
  593.4 7.4 multiply_reduce_fusion.3
  600.9 11.6 convert_reduce_fusion
  612.5 8.6 convert_reduce_fusion.7
  632.0 45.7 %while.54 = (s32[]{:T(128)}, bf16[4,256,4,64]{1,3,2,0:T(8,128)(2,1)S(1)}, bf16[4,1024,4,64]{1,3,2,0:T(8,128)(2,1)}, bf16[4,1024,4,64]{1,3,2,0:T(8,128)(2,1)}, bf...) while((s32[]{:T(128)}, ...), condition=%wide.region_28.29_spmd, body=%wide.region_26.28_spmd.sunk | while | flops 687406080 | bytes 72663312 | solution.py:264
  681.7 46.2 %while.55 = (s32[]{:T(128)}, bf16[4,256,4,64]{1,3,2,0:T(8,128)(2,1)}, bf16[4,1024,4,64]{1,3,2,0:T(8,128)(2,1)}, bf16[4,1024,4,64]{1,3,2,0:T(8,128)(2,1)}, bf16[4...) while((s32[]{:T(128)}, ...), condition=%wide.region_37.38_spmd, body=%wide.region_35.37_spmd.sunk | while | flops 687406080 | bytes 76857680 | solution.py:264
  747.4 14.1 reduce-scatter.21.cloned.1.call-done
  771.9 27.8 %reduce-scatter.19.cloned.1.call-done = bf16[1,256,1024]{1,2,0:T(8,128)(2,1)} async-done(((bf16[1,1024,1024]{1,2,0:T(8,128)(2,1)}), bf16[1,256,1024]{1,2,0:T(8,128)(2,1)}) %reduce-scatter.19.cloned.1.call-update) | async-done | bytes 524304 | tf_op jit(solution)/shard_map/reduce_scatter | solution.py:282
  803.4 34.6 %reduce-scatter.23.cloned.1.call-done = bf16[1,256,1024]{1,2,0:T(8,128)(2,1)} async-done(((bf16[1,1024,1024]{1,2,0:T(8,128)(2,1)}), bf16[1,256,1024]{1,2,0:T(8,128)(2,1)}) %reduce-scatter.23.cloned.1.call-update) | async-done | bytes 524304 | tf_op jit(solution)/shard_map/reduce_scatter | solution.py:282
  853.5 9.9 convolution_add_fusion.1
  868.7 10.1 convolution_add_fusion
  891.8 40.8 %all-reduce.17 = (f32[1024]{0:T(1024)S(1)}, f32[1024]{0:T(1024)S(1)}, f32[1024]{0:T(1024)S(1)}, f32[1024]{0:T(1024)S(1)}, f32[1024]{0:T(1024)S(1)}, /*index=5*/f...) all-reduce(f32[1024]{0:T(1024)S(1)} %reshape.711, ...), channel_id=26, replica_groups=mesh['ctx'=4,'fsdp'=8] {'ctx','fsdp'}, use_global_device_ids=true, to_apply=%region_43.44.clone | all-reduce | flops 12288 | bytes 98304
  944.6 34.5 %reduce-scatter.31.cloned.1.call-done = f32[32,1024]{1,0:T(8,128)} async-done(((f32[1024,1024]{1,0:T(8,128)}), f32[32,1024]{1,0:T(8,128)}) %reduce-scatter.31.cloned.1.call-update) | async-done | bytes 131088
  979.1 142.0 %reduce-scatter.25.cloned.1.call-done = f32[32,1024]{1,0:T(8,128)} async-done(((f32[1024,1024]{1,0:T(8,128)}), f32[32,1024]{1,0:T(8,128)}) %reduce-scatter.25.cloned.1.call-update) | async-done | bytes 131088 | tf_op jit(solution)/shard_map/reduce_scatter | solution.py:311
  1121.1 142.1 %reduce-scatter.33.cloned.1.call-done = f32[32,1024]{1,0:T(8,128)} async-done(((f32[1024,1024]{1,0:T(8,128)}), f32[32,1024]{1,0:T(8,128)}) %reduce-scatter.33.cloned.1.call-update) | async-done | bytes 131088
  1263.2 142.6 %reduce-scatter.35.cloned.1.call-done = f32[32,1024]{1,0:T(8,128)} async-done(((f32[1024,1024]{1,0:T(8,128)}), f32[32,1024]{1,0:T(8,128)}) %reduce-scatter.35.cloned.1.call-update) | async-done | bytes 131088
  1405.9 186.9 %reduce-scatter.27.cloned.1.call-done = f32[32,4096]{1,0:T(8,128)} async-done(((f32[1024,4096]{1,0:T(8,128)}), f32[32,4096]{1,0:T(8,128)}) %reduce-scatter.27.cloned.1.call-update) | async-done | bytes 524304 | tf_op jit(solution)/shard_map/reduce_scatter | solution.py:315
  1592.8 187.1 %reduce-scatter.29.cloned.1.call-done = f32[128,1024]{1,0:T(8,128)} async-done(((f32[4096,1024]{1,0:T(8,128)}), f32[128,1024]{1,0:T(8,128)}) %reduce-scatter.29.cloned.1.call-update) | async-done | bytes 524304 | tf_op jit(solution)/shard_map/reduce_scatter | solution.py:317
  (580 shorter events, 317.1 us)
Async XLA Ops:
  7.2 121.4 %copy-start.7 = (bf16[2,1,256,1024]{3,2,1,0:T(8,128)(2,1)S(1)}, bf16[2,1,256,1024]{3,2,1,0:T(8,128)(2,1)}, u32[]{:S(2)}) copy-start(bf16[2,1,256,1024]{3,2,1,0:T(8,128)(2,1)} %param.26) | copy-start | bytes 3145732
  7.2 62.8 %all-gather.16.cloned.1.call-start = ((), (), s32[]{:S(2)}) async-start(), calls=%async_computation.10 | async-start | bytes 2162688 | tf_op jit(solution)/shard_map/all_gather | solution.py:139
  7.9 120.6 %all-gather.20.cloned.1.call-start = ((), (), s32[]{:S(2)}) async-start(), calls=%async_computation.12 | async-start | bytes 2162688 | tf_op jit(solution)/shard_map/all_gather | solution.py:138
  8.7 178.3 %all-gather.18.cloned.1.call-start = ((), (), s32[]{:S(2)}) async-start(), calls=%async_computation.11 | async-start | bytes 2162688 | tf_op jit(solution)/shard_map/all_gather | solution.py:136
  9.4 213.6 %all-gather.28.cloned.1.call-start = ((), (), s32[]{:S(2)}) async-start(), calls=%async_computation.20 | async-start | bytes 2621440 | tf_op jit(solution)/shard_map/all_gather | solution.py:183
  70.0 61.7 %copy-start.22 = (bf16[1024,1024]{1,0:T(8,128)(2,1)S(1)}, bf16[1024,1024]{1,0:T(8,128)(2,1)}, u32[]{:S(2)}) copy-start(bf16[1024,1024]{1,0:T(8,128)(2,1)} %all-gather.16.cloned.1.call-done) | copy-start | bytes 6291460
  73.5 187.2 %all-gather.30.cloned.1.call-start = ((), (), s32[]{:S(2)}) async-start(), calls=%async_computation.21 | async-start | bytes 2621440 | tf_op jit(solution)/shard_map/all_gather | solution.py:180
  131.7 166.0 %all-gather.32.cloned.1.call-start = ((), (), s32[]{:S(2)}) async-start(), calls=%async_computation.22 | async-start | bytes 2621440 | tf_op jit(solution)/shard_map/all_gather | solution.py:183
  133.3 201.6 %all-gather.34.cloned.1.call-start = ((), (), s32[]{:S(2)}) async-start(), calls=%async_computation.23 | async-start | bytes 2621440 | tf_op jit(solution)/shard_map/all_gather | solution.py:180
  136.5 258.3 %all-gather.22.cloned.1.call-start = ((), (), s32[]{:S(2)}) async-start(), calls=%async_computation.13 | async-start | bytes 2162688 | tf_op jit(solution)/shard_map/all_gather | solution.py:141
  137.2 336.9 %all-gather.24.cloned.1.call-start = ((), (), s32[]{:S(2)}) async-start(), calls=%async_computation.14 | async-start | bytes 8650752 | tf_op jit(solution)/shard_map/all_gather | solution.py:145
  137.9 415.0 %all-gather.26.cloned.1.call-start = ((), (), s32[]{:S(2)}) async-start(), calls=%async_computation.15 | async-start | bytes 8650752 | tf_op jit(solution)/shard_map/all_gather | solution.py:147
  138.5 605.2 %reduce-scatter.17.cloned.1.call-start = ((), (), s32[]{:S(2)}) async-start(), calls=%async_computation.16 | async-start | bytes 2621440 | tf_op jit(solution)/shard_map/reduce_scatter | solution.py:279
  178.5 394.9 %copy-start.53 = (f32[1024]{0:T(1024)}, f32[1024]{0:T(1024)S(1)}, u32[]{:S(2)}) copy-start(f32[1024]{0:T(1024)S(1)} %convert_element_type.386) | copy-start | bytes 12292
  422.1 68.4 %copy-start = (bf16[4,1024,4,64]{1,3,2,0:T(8,128)(2,1)}, bf16[4,1024,4,64]{1,3,2,0:T(8,128)(2,1)S(1)}, u32[]{:S(2)}) copy-start(bf16[4,1024,4,64]{1,3,2,0:T(8,128)(2,1)S(1)} %get-tuple-element.861) | copy-start | bytes 6291460
  422.1 68.4 %copy-start.55 = (s32[4,1024]{1,0:T(4,128)}, s32[4,1024]{1,0:T(4,128)S(1)}, u32[]{:S(2)}) copy-start(s32[4,1024]{1,0:T(4,128)S(1)} %get-tuple-element.907) | copy-start | bytes 49156
  422.1 68.4 %copy-start.58 = (f32[4,4,256,1]{2,1,3,0:T(4,128)}, f32[4,4,256,1]{2,1,3,0:T(4,128)S(1)}, u32[]{:S(2)}) copy-start(f32[4,4,256,1]{2,1,3,0:T(4,128)S(1)} %get-tuple-element.773) | copy-start | bytes 49156
  422.1 68.4 %copy-start.59 = (s32[4,256]{1,0:T(4,128)}, s32[4,256]{1,0:T(4,128)S(1)}, u32[]{:S(2)}) copy-start(s32[4,256]{1,0:T(4,128)S(1)} %get-tuple-element.917) | copy-start | bytes 12292
  425.9 195.3 %copy-start.5 = (f32[256,1024]{1,0:T(8,128)}, f32[256,1024]{1,0:T(8,128)S(1)}, u32[]{:S(2)}) copy-start(f32[256,1024]{1,0:T(8,128)S(1)} %get-tuple-element.451) | copy-start | bytes 3145732
  425.9 195.3 %copy-start.62 = (f32[256]{0:T(256)}, f32[256]{0:T(256)S(1)}, u32[]{:S(2)}) copy-start(f32[256]{0:T(256)S(1)} %broadcast_multiply_fusion.9) | copy-start | bytes 3076
  426.2 195.0 %copy-start.64 = (f32[256]{0:T(256)}, f32[256]{0:T(256)S(1)}, u32[]{:S(2)}) copy-start(f32[256]{0:T(256)S(1)} %add_rsqrt_fusion.1) | copy-start | bytes 3076
  677.7 83.9 %reduce-scatter.21.cloned.1.call-start = ((), (), s32[]{:S(2)}) async-start(), calls=%async_computation.18 | async-start | bytes 2621440 | tf_op jit(solution)/shard_map/reduce_scatter | solution.py:279
  728.0 71.7 %reduce-scatter.19.cloned.1.call-start = ((), (), s32[]{:S(2)}) async-start(), calls=%async_computation.17 | async-start | bytes 2621440 | tf_op jit(solution)/shard_map/reduce_scatter | solution.py:282
  728.8 109.3 %reduce-scatter.23.cloned.1.call-start = ((), (), s32[]{:S(2)}) async-start(), calls=%async_computation.19 | async-start | bytes 2621440 | tf_op jit(solution)/shard_map/reduce_scatter | solution.py:282
  729.3 249.8 %reduce-scatter.31.cloned.1.call-start = ((), (), s32[]{:S(2)}) async-start(), calls=%async_computation.27 | async-start | bytes 4325376
  738.6 382.5 %reduce-scatter.25.cloned.1.call-start = ((), (), s32[]{:S(2)}) async-start(), calls=%async_computation.24 | async-start | bytes 4325376 | tf_op jit(solution)/shard_map/reduce_scatter | solution.py:311
  743.7 519.5 %reduce-scatter.33.cloned.1.call-start = ((), (), s32[]{:S(2)}) async-start(), calls=%async_computation.28 | async-start | bytes 4325376
  771.9 634.0 %reduce-scatter.35.cloned.1.call-start = ((), (), s32[]{:S(2)}) async-start(), calls=%async_computation.29 | async-start | bytes 4325376
  848.4 744.3 %reduce-scatter.27.cloned.1.call-start = ((), (), s32[]{:S(2)}) async-start(), calls=%async_computation.25 | async-start | bytes 17301504 | tf_op jit(solution)/shard_map/reduce_scatter | solution.py:315
  863.5 916.4 %reduce-scatter.29.cloned.1.call-start = ((), (), s32[]{:S(2)}) async-start(), calls=%async_computation.26 | async-start | bytes 17301504 | tf_op jit(solution)/shard_map/reduce_scatter | solution.py:317
  889.5 51.2 %copy-start.39 = (bf16[1,256,1024]{1,2,0:T(8,128)(2,1)S(1)}, bf16[1,256,1024]{1,2,0:T(8,128)(2,1)}, u32[]{:S(2)}) copy-start(bf16[1,256,1024]{1,2,0:T(8,128)(2,1)} %reduce-scatter.23.cloned.1.call-done) | copy-start | bytes 1572868
  891.3 49.5 %copy-start.23 = (bf16[1024,1024]{1,0:T(8,128)(2,1)S(1)}, bf16[1024,1024]{1,0:T(8,128)(2,1)}, u32[]{:S(2)}) copy-start(bf16[1024,1024]{1,0:T(8,128)(2,1)} %all-gather.16.cloned.1.call-done) | copy-start | bytes 6291460
  (119 other events, 599.0 us)
Sparse Core Ops, SparseCore 0:
  11.0 58.9 all-gather.15
  73.0 55.4 all-gather.19
  131.5 55.3 all-gather.17
  189.2 33.7 all-gather.27
  225.3 35.2 all-gather.29
  262.3 35.2 all-gather.31
  299.5 35.2 all-gather.33
  337.9 56.8 all-gather.21
  397.8 76.2 all-gather.23
  476.9 75.9 all-gather.25
  677.8 33.3 reduce-scatter.16
  728.1 33.3 reduce-scatter.20
  764.5 35.1 reduce-scatter.18
  802.8 35.1 reduce-scatter.22
  840.7 138.3 reduce-scatter.30
  981.8 139.2 reduce-scatter.24
  1123.8 139.3 reduce-scatter.32
  1265.9 139.8 reduce-scatter.34
  1408.7 183.9 reduce-scatter.26
  1595.5 184.3 reduce-scatter.28
where the time goes:
time: 1800 us; the launch traced here: 1790 us
  waiting for transfers between devices  1260 us (70%)
  matrix products  252 us (14%)
  blocking collectives  121 us (7%)
  local copies, waits for them, and re-layouts  96.1 us (5%)
  other arithmetic  39.1 us (2%)
    unnamed x23, waiting for transfers between devices  325 us
    reduce_scatter x1, waiting for transfers between devices, body(): lax.psum_scatter(grad_down_mat, ('ctx', 'fsdp'), scatter_dimension=0, til...  187 us
    reduce_scatter x1, waiting for transfers between devices, body(): lax.psum_scatter(grad_up_mat, ('ctx', 'fsdp'), scatter_dimension=0, tiled...  187 us
    reduce_scatter x1, waiting for transfers between devices, body(): lax.psum_scatter(grad_out_mat, ('ctx', 'fsdp'), scatter_dimension=0, tile...  142 us
    unnamed x2, blocking collectives  81.6 us
    all_gather x2, waiting for transfers between devices, body(): lax.all_gather(keys_mine.reshape(per_device, ctx_rows, width), 'ctx', axi...  66.8 us
    reduce_scatter x2, waiting for transfers between devices, body(): lax.psum_scatter(grad_values_all.astype(jnp.bfloat16), 'ctx', scatter_dim...  62.4 us
    all_gather x1, waiting for transfers between devices, body(): lax.all_gather(w_down, ('ctx', 'fsdp'), axis=0, tiled=True)  62.4 us
  transfers between devices with their start and end apart: 20, of which 19 were waited for; matrix products, arithmetic and copies ran while one was open for 14% of the time, Pallas kernels for 0%

commit v1 on v0

v1 whole, which is shorter than its diff:
```python
import functools

import jax
import jax.numpy as jnp
from jax import lax
from jax.experimental import pallas as pl
from jax.experimental.pallas import tpu as pltpu
from jax.sharding import PartitionSpec as P

H = 16
HD = 64
EPSILON = 1e-12
SCORE_SCALE = 0.125
MASKED = -1e30
BF = jnp.bfloat16
F32 = jnp.float32
BOTH = ("ctx", "fsdp")
VMEM_LIMIT = 48 << 20


def dot(a, b, ca, cb):
    return lax.dot_general(a, b, (((ca,), (cb,)), ((), ())), preferred_element_type=F32)


def swap(x, axis, r):
    n = lax.axis_size(axis)
    return lax.ppermute(x, axis, [(i, i ^ r) for i in range(n)])


def bits_of(n):
    return [1 << b for b in range(n.bit_length() - 1)]


def place(pieces, me):
    n = len(pieces)
    out = jnp.zeros((n,) + pieces[0].shape, pieces[0].dtype)
    for r in range(n):
        out = lax.dynamic_update_index_in_dim(out, pieces[r], me ^ r, 0)
    return out


def gather_z(x):
    n = lax.axis_size("fsdp") // 2
    z = lax.axis_index("fsdp") // 2
    pieces = [x] + [swap(x, "fsdp", 2 * r) for r in range(1, n)]
    return place(pieces, z)


def gather_ctx(x, order):
    n = lax.axis_size("ctx")
    pieces = {0: x}
    for b in order:
        for r in list(pieces):
            pieces[r ^ b] = swap(pieces[r], "ctx", b)
    return place([pieces[r] for r in range(n)], lax.axis_index("ctx"))


def scatter_ctx(x, order):
    n = lax.axis_size("ctx")
    me = lax.axis_index("ctx")
    pieces = {r: lax.dynamic_index_in_dim(x, me ^ r, 0, False) for r in range(n)}
    for b in order:
        for r in [r for r in pieces if r & b]:
            got = swap(pieces.pop(r).astype(BF), "ctx", b)
            pieces[r ^ b] = pieces[r ^ b].astype(F32) + got.astype(F32)
    return pieces[0]


def scatter_z(x):
    n = lax.axis_size("fsdp") // 2
    z = lax.axis_index("fsdp") // 2
    x = x.astype(BF)
    total = lax.dynamic_index_in_dim(x, z, 0, False).astype(F32)
    for r in range(1, n):
        got = swap(lax.dynamic_index_in_dim(x, z ^ r, 0, False), "fsdp", 2 * r)
        total = total + got.astype(F32)
    return total


def exchange_ctx(x):
    n = lax.axis_size("ctx")
    me = lax.axis_index("ctx")
    pieces = [lax.dynamic_index_in_dim(x, me, 0, False)]
    for r in range(1, n):
        pieces.append(swap(lax.dynamic_index_in_dim(x, me ^ r, 0, False), "ctx", r))
    return place(pieces, me)


def core_swap(x):
    return swap(x, "fsdp", 1)


def attend_kernel(q_ref, k_ref, v_ref, srow_ref, scol_ref, o_ref, lse_ref):
    q = q_ref[...] * jnp.asarray(SCORE_SCALE, BF)
    s = dot(k_ref[...], q, 0, 0)
    s = jnp.where(scol_ref[...] == srow_ref[...], s, MASKED)
    top = jnp.max(s, axis=0, keepdims=True)
    p = jnp.exp(s - top)
    total = jnp.sum(p, axis=0, keepdims=True)
    o = dot(v_ref[...], p.astype(BF), 1, 0)
    o_ref[...] = (o / total).astype(BF)[None]
    lse_ref[...] = (top + jnp.log(total))[None]


def attend(qkv, seg, block):
    rows, length = qkv.shape
    heads = rows // (3 * HD)
    nq = length // block
    whole = lambda part: pl.BlockSpec((HD, length), lambda h, i: (part * heads + h, 0))
    return pl.pallas_call(
        attend_kernel,
        grid=(heads, nq),
        in_specs=[
            pl.BlockSpec((HD, block), lambda h, i: (h, i)),
            whole(1),
            whole(2),
            pl.BlockSpec((1, block), lambda h, i: (0, i)),
            pl.BlockSpec((length, 1), lambda h, i: (0, 0)),
        ],
        out_specs=[
            pl.BlockSpec((1, HD, block), lambda h, i: (i, h, 0)),
            pl.BlockSpec((1, 1, block), lambda h, i: (h, 0, i)),
        ],
        out_shape=[
            jax.ShapeDtypeStruct((nq, heads * HD, block), BF),
            jax.ShapeDtypeStruct((heads, 1, length), F32),
        ],
        compiler_params=pltpu.CompilerParams(vmem_limit_bytes=VMEM_LIMIT),
        cost_estimate=pl.CostEstimate(
            flops=4 * heads * HD * length * length,
            transcendentals=heads * length * length,
            bytes_accessed=4 * rows * length,
        ),
        name="attend",
    )(qkv, qkv, qkv, seg[None, :], seg[:, None])


def attend_back_kernel(
    heads, nq, block, q_ref, k_ref, v_ref, do_ref, lse_ref, srow_ref, scol_ref, out_ref, dk_ref, dv_ref
):
    h = pl.program_id(0)
    i = pl.program_id(1)
    q = q_ref[...] * jnp.asarray(SCORE_SCALE, BF)
    k = k_ref[...]
    do = do_ref[0]
    s = dot(k, q, 0, 0)
    p = jnp.exp(s - lse_ref[0])
    p = jnp.where(scol_ref[...] == srow_ref[...], p, 0.0)
    dp = dot(v_ref[...], do, 0, 0)
    central = jnp.sum(p * dp, axis=0, keepdims=True)
    ds = (p * (dp - central)).astype(BF)
    dq = dot(k, ds, 1, 0) * SCORE_SCALE
    dk = dot(q, ds, 1, 1)
    dv = dot(do, p.astype(BF), 1, 1)
    out_ref[pl.ds(pl.multiple_of(h * HD, HD), HD), pl.ds(pl.multiple_of(i * block, block), block)] = dq.astype(BF)

    @pl.when(i == 0)
    def _():
        dk_ref[...] = dk
        dv_ref[...] = dv

    @pl.when(i > 0)
    def _():
        dk_ref[...] += dk
        dv_ref[...] += dv

    @pl.when(i == nq - 1)
    def _():
        out_ref[pl.ds(pl.multiple_of((heads + h) * HD, HD), HD), :] = dk_ref[...].astype(BF)
        out_ref[pl.ds(pl.multiple_of((2 * heads + h) * HD, HD), HD), :] = dv_ref[...].astype(BF)


def attend_back(qkv, do, lse, seg, block):
    rows, length = qkv.shape
    heads = rows // (3 * HD)
    nq = length // block
    whole = lambda part: pl.BlockSpec((HD, length), lambda h, i: (part * heads + h, 0))
    return pl.pallas_call(
        functools.partial(attend_back_kernel, heads, nq, block),
        grid=(heads, nq),
        in_specs=[
            pl.BlockSpec((HD, block), lambda h, i: (h, i)),
            whole(1),
            whole(2),
            pl.BlockSpec((1, HD, block), lambda h, i: (i, h, 0)),
            pl.BlockSpec((1, 1, block), lambda h, i: (h, 0, i)),
            pl.BlockSpec((1, block), lambda h, i: (0, i)),
            pl.BlockSpec((length, 1), lambda h, i: (0, 0)),
        ],
        out_specs=pl.BlockSpec((rows, length), lambda h, i: (0, 0)),
        out_shape=jax.ShapeDtypeStruct((rows, length), BF),
        scratch_shapes=[pltpu.VMEM((HD, length), F32), pltpu.VMEM((HD, length), F32)],
        compiler_params=pltpu.CompilerParams(vmem_limit_bytes=VMEM_LIMIT),
        cost_estimate=pl.CostEstimate(
            flops=10 * heads * HD * length * length,
            transcendentals=heads * length * length,
            bytes_accessed=6 * rows * length,
        ),
        name="attend_back",
    )(qkv, qkv, qkv, do, lse, seg[None, :], seg[:, None])


def norm_forward(values_in, gain_vec, bias_vec):
    center = values_in - jnp.mean(values_in, axis=-1, keepdims=True)
    inverse = lax.rsqrt(jnp.mean(center * center, axis=-1, keepdims=True) + EPSILON)
    normed = center * inverse
    return (normed * gain_vec + bias_vec, normed, inverse)


def norm_backward(upstream, normed, inverse, gain_vec):
    scaled = upstream * gain_vec
    inner_sum = (
        scaled
        - jnp.mean(scaled, axis=-1, keepdims=True)
        - normed * jnp.mean(scaled * normed, axis=-1, keepdims=True)
    )
    return (inverse * inner_sum, jnp.sum(upstream * normed, axis=0), jnp.sum(upstream, axis=0))


def segment_ids(lengths, positions):
    starts = jnp.cumsum(lengths) - lengths
    return jnp.sum((positions[:, None] >= starts[None, :]).astype(jnp.int32), axis=1) - 1


def body(
    tokens,
    doc_lengths,
    w_query,
    b_query,
    w_key,
    w_value,
    b_value,
    w_out,
    b_out,
    ln1_gain,
    ln1_bias,
    w_up,
    b_up,
    w_down,
    b_down,
    ln2_gain,
    ln2_bias,
    cotangent,
):
    micro, per_device, ctx_rows, width = tokens.shape
    nc = lax.axis_size("ctx")
    nf = lax.axis_size("fsdp")
    nz = nf // 2
    me = lax.axis_index("ctx")
    fi = lax.axis_index("fsdp")
    core = fi % 2
    rows_w = w_query.shape[0]
    ff_w = w_down.shape[0]
    ff = w_up.shape[1]
    half = ff // 2
    cols = width // nc
    length = ctx_rows * nc
    flat_rows = micro * per_device * ctx_rows
    groups = micro * per_device
    order_a = bits_of(nc)
    order_b = order_a[::-1]

    mine = tokens.reshape(groups, ctx_rows, width)
    inputs_all = [
        gather_ctx(mine[g], order_a if g % 2 == 0 else order_b).reshape(length, width) for g in range(groups)
    ]

    w_qkv = jnp.stack([w_query, w_key, w_value], axis=1).reshape(rows_w, 3, nc, cols)
    w_qkv = exchange_ctx(jnp.moveaxis(w_qkv, 2, 0).reshape(nc, rows_w, 3 * cols))
    w_qkv = gather_z(w_qkv)
    other = core_swap(w_qkv)
    w_qkv = jnp.where(core == 0, jnp.stack([w_qkv, other], axis=2), jnp.stack([other, w_qkv], axis=2))
    w_qkv = jnp.moveaxis(w_qkv.reshape(nz, nc, 2, rows_w, 3 * cols), 0, 1)
    w_qkv = w_qkv.reshape(nc, nz, 2, rows_w, 3 * cols).reshape(width, 3 * cols)

    vectors = (b_query, b_value, b_out, ln1_gain, ln1_bias, b_down, ln2_gain, ln2_bias, b_up)
    packed = jnp.concatenate(vectors)
    packed = lax.all_to_all(
        jnp.broadcast_to(packed[None], (nc * nf,) + packed.shape), BOTH, 0, 0
    ).reshape(nc * nf, packed.shape[0])
    full = [packed[:, j * rows_w : (j + 1) * rows_w].reshape(width) for j in range(8)]
    query_bias, value_bias, out_bias, gain_one, bias_one, down_bias, gain_two, bias_two = full
    up_bias = packed[:, 8 * rows_w :].reshape(nc * nz, 2, ff_w)
    up_bias = lax.dynamic_index_in_dim(up_bias, core, 1, False).reshape(half)

    out_mat = gather_ctx(gather_z(w_out), order_a)
    out_other = core_swap(out_mat)
    out_mat = jnp.where(core == 0, jnp.stack([out_mat, out_other], axis=2), jnp.stack([out_other, out_mat], axis=2))
    out_mat = out_mat.reshape(width, width)

    split = w_up.reshape(rows_w, half // ff_w, 2, ff_w)
    keep = lax.dynamic_index_in_dim(split, core, 2, False).reshape(rows_w, half)
    give = lax.dynamic_index_in_dim(split, 1 - core, 2, False).reshape(rows_w, half)
    got = core_swap(give)
    up_mine = jnp.where(core == 0, jnp.stack([keep, got]), jnp.stack([got, keep])).reshape(2 * rows_w, half)
    up_mat = gather_ctx(gather_z(up_mine), order_a).reshape(width, half)
    down_mat = gather_ctx(gather_z(w_down), order_b).reshape(half, width)

    key_pos = jnp.arange(length, dtype=jnp.int32)
    lengths = doc_lengths.reshape(groups, -1)
    zero_bias = jnp.zeros((cols,), BF)
    qkv_bias = jnp.concatenate(
        [
            lax.dynamic_slice_in_dim(query_bias, me * cols, cols),
            zero_bias,
            lax.dynamic_slice_in_dim(value_bias, me * cols, cols),
        ]
    ).astype(F32)[:, None]
    segs, qkvs, lses, mixed = [], [], [], []
    for g in range(groups):
        seg = segment_ids(lengths[g], key_pos)
        qkv = (dot(w_qkv, inputs_all[g], 0, 1) + qkv_bias).astype(BF)
        o, lse = attend(qkv, seg, ctx_rows)
        mixed.append(exchange_ctx(o).reshape(width, ctx_rows))
        segs.append(seg)
        qkvs.append(qkv)
        lses.append(lse)
    mixed = jnp.concatenate(mixed, axis=1)

    inputs = mine.reshape(flat_rows, width).astype(F32)
    attended = dot(mixed, out_mat, 0, 0) + out_bias
    first, normed_one, inverse_one = norm_forward(inputs + attended, gain_one, bias_one)
    first_low = first.astype(BF)
    both_first = jnp.concatenate([first_low, core_swap(first_low)])
    hidden = dot(both_first, up_mat, 1, 0) + up_bias
    cdf = 0.5 * (1.0 + lax.erf(hidden * 0.7071067811865476))
    slope = (cdf + hidden * jnp.exp(-0.5 * hidden * hidden) * 0.3989422804014327).astype(BF)
    activated = (hidden * cdf).astype(BF)
    part = dot(activated, down_mat, 1, 0)
    branch = part[:flat_rows] + core_swap(part[flat_rows:]) + down_bias
    result, normed_two, inverse_two = norm_forward(first + branch, gain_two, bias_two)
    output = result.astype(BF).reshape(micro, per_device, ctx_rows, width)

    upstream = cotangent.reshape(flat_rows, width).astype(F32)
    grad_h2, grad_gain_two, grad_bias_two = norm_backward(upstream, normed_two, inverse_two, gain_two)
    grad_branch = grad_h2.astype(BF)
    grad_down_bias = jnp.sum(grad_branch.astype(F32), axis=0)
    both_branch = jnp.concatenate([grad_branch, core_swap(grad_branch)])
    grad_down = dot(activated, both_branch, 0, 0).astype(BF).reshape(nc, nz, ff_w, width)
    grad_down = scatter_z(scatter_ctx(grad_down, order_a))
    grad_hidden = (dot(both_branch, down_mat, 1, 1) * slope.astype(F32)).astype(BF)
    grad_up_bias = jnp.sum(grad_hidden.astype(F32), axis=0)
    grad_up = dot(both_first, grad_hidden, 0, 0).astype(BF).reshape(nc, nz, 2, rows_w, half)
    grad_up = scatter_z(scatter_ctx(grad_up, order_b))
    grad_up_mine = lax.dynamic_index_in_dim(grad_up, core, 0, False)
    grad_up_got = core_swap(lax.dynamic_index_in_dim(grad_up, 1 - core, 0, False))
    pair = [t.reshape(rows_w, half // ff_w, ff_w) for t in (grad_up_mine, grad_up_got)]
    grad_up = jnp.where(core == 0, jnp.stack(pair, axis=2), jnp.stack(pair[::-1], axis=2)).reshape(rows_w, ff)
    part = dot(grad_hidden, up_mat, 1, 1)
    grad_first = part[:flat_rows] + core_swap(part[flat_rows:]) + grad_h2
    grad_h1, grad_gain_one, grad_bias_one = norm_backward(grad_first, normed_one, inverse_one, gain_one)
    grad_attended = grad_h1.astype(BF)
    grad_out_bias = jnp.sum(grad_attended.astype(F32), axis=0)
    grad_mixed = dot(out_mat, grad_attended, 1, 1).astype(BF)
    grad_mixed = grad_mixed.reshape(nc, cols, groups, ctx_rows)
    grad_out = dot(mixed, grad_attended, 1, 0).astype(BF).reshape(nc, nz, 2, rows_w, width)
    grad_out_got = core_swap(lax.dynamic_index_in_dim(grad_out, 1 - core, 2, False))
    grad_out = lax.dynamic_index_in_dim(grad_out, core, 2, False).astype(F32) + grad_out_got.astype(F32)
    grad_out = scatter_z(scatter_ctx(grad_out.astype(BF), order_a))

    grad_qkv = None
    grad_bias_parts = []
    input_grads = []
    for g in range(groups):
        do = exchange_ctx(grad_mixed[:, :, g])
        dqkv = attend_back(qkvs[g], do, lses[g], segs[g], ctx_rows)
        grad_bias_parts.append(jnp.sum(dqkv.astype(F32), axis=1))
        now = dot(inputs_all[g], dqkv, 0, 1)
        grad_qkv = now if grad_qkv is None else grad_qkv + now
        back = dot(dqkv, w_qkv, 0, 1).astype(BF).reshape(nc, ctx_rows, width)
        input_grads.append(scatter_ctx(back, order_a if g % 2 == 0 else order_b))
    grad_tokens = grad_h1.reshape(groups, ctx_rows, width) + jnp.stack(input_grads)
    grad_tokens = grad_tokens.reshape(micro, per_device, ctx_rows, width)

    grad_qkv = grad_qkv.astype(BF).reshape(nc, nz, 2, rows_w, 3 * cols)
    grad_qkv_got = core_swap(lax.dynamic_index_in_dim(grad_qkv, 1 - core, 2, False))
    grad_qkv = lax.dynamic_index_in_dim(grad_qkv, core, 2, False).astype(F32) + grad_qkv_got.astype(F32)
    grad_qkv = scatter_z(jnp.moveaxis(grad_qkv.astype(BF), 1, 0))
    grad_qkv = exchange_ctx(grad_qkv).reshape(nc, rows_w, 3, cols)
    grad_qkv = jnp.moveaxis(grad_qkv, 0, 2).reshape(rows_w, 3, width)

    grad_bias = sum(grad_bias_parts).reshape(3, cols)
    spread = lambda v: lax.dynamic_update_slice_in_dim(jnp.zeros((width,), F32), v, me * cols, 0)
    small = [
        spread(grad_bias[0]),
        spread(grad_bias[2]),
        grad_out_bias,
        grad_gain_one,
        grad_bias_one,
        grad_down_bias,
        grad_gain_two,
        grad_bias_two,
    ]
    small = [t.reshape(nc * nf, rows_w) for t in small]
    grad_up_bias = grad_up_bias.reshape(nc * nz, ff_w)
    pair = [jnp.where(core == j, grad_up_bias, 0.0) for j in range(2)]
    small.append(jnp.stack(pair, axis=1).reshape(nc * nf, ff_w))
    small = jnp.concatenate(small, axis=1)
    small = jnp.sum(lax.all_to_all(small, BOTH, 0, 0), axis=0)
    small_out = [small[j * rows_w : (j + 1) * rows_w] for j in range(8)]
    g_bq, g_bv, g_bo, g_g1, g_b1, g_bd, g_g2, g_b2 = small_out
    g_bu = small[8 * rows_w :]

    return (
        output,
        grad_tokens,
        grad_qkv[:, 0],
        g_bq,
        grad_qkv[:, 1],
        grad_qkv[:, 2],
        g_bv,
        grad_out,
        g_bo,
        g_g1,
        g_b1,
        grad_up,
        g_bu,
        grad_down,
        g_bd,
        g_g2,
        g_b2,
    )


def solution(mesh):
    stream = P(None, "fsdp", "ctx", None)
    mat = P(BOTH, None)
    vec = P(BOTH)
    return jax.shard_map(
        body,
        mesh=mesh,
        in_specs=(
            stream,
            P(None, "fsdp", None),
            mat,
            vec,
            mat,
            mat,
            vec,
            mat,
            vec,
            vec,
            vec,
            mat,
            vec,
            mat,
            vec,
            vec,
            vec,
            stream,
        ),
        out_specs=(
            stream,
            stream,
            mat,
            vec,
            mat,
            mat,
            vec,
            mat,
            vec,
            vec,
            vec,
            mat,
            vec,
            mat,
            vec,
            vec,
            vec,
        ),
        check_vma=False,
    )
```

time: 1800 us -> 592 us (0.33)
  the two profiles are of different devices: /device:TPU:1 before, /device:TPU:0 now
where the time goes in v1:
time: 592 us; the launch traced here: 582 us
  waiting for transfers between devices  211 us (36%)
  starting transfers between devices  105 us (18%)
  local copies, waits for them, and re-layouts  88.8 us (15%)
  matrix products  65.4 us (11%)
  Pallas kernels  65.2 us (11%)
  other arithmetic  44 us (7%)
    ppermute x82, waiting for transfers between devices, swap(): return lax.ppermute(x, axis, [(i, i ^ r) for i in range(n)])  208 us
    ppermute x82, starting transfers between devices, swap(): return lax.ppermute(x, axis, [(i, i ^ r) for i in range(n)])  96 us
    dot_general x15, matrix products, dot(): lax.dot_general(a, b, (((ca,), (cb,)), ((), ())), preferred_element_type=...  65.4 us
    pallas_call x2, Pallas kernels, attend_back(): pl.pallas_call(functools.partial(attend_back_kernel, heads, nq, block), g...  40.7 us
    pallas_call x2, Pallas kernels, attend(): pl.pallas_call(attend_kernel, grid=(heads, nq), in_specs=[pl.BlockSpec((H...  24.6 us
    dynamic_update_slice x56, local copies, waits for them, and re-layouts, place(): out = lax.dynamic_update_index_in_dim(out, pieces[r], me ^ r, 0)  20.9 us
    unnamed x125, local copies, waits for them, and re-layouts  18.8 us
  transfers between devices with their start and end apart: 84, of which 36 were waited for; matrix products, arithmetic and copies ran while one was open for 24% of the time, Pallas kernels for 11%

profile of v1, /device:TPU:0, one launch (start us, length us, event | category | flops | bytes accessed | tf_op | source)
XLA Modules:
  0.0 582.4 jit_solution(9238671821311209452)
XLA Ops:
  6.4 6.1 %concatenate.30 = bf16[384]{0:T(512)(128)(2,1)S(1)} concatenate(bf16[32]{0:T(256)(128)(2,1)} %param.21, bf16[32]{0:T(256)(128)(2,1)} %param.24, bf16[32]{0:T(256)(128)(2,1)} %param.26, bf16[32]{0:T(256)(128)(2,1)} %param.27, bf16[32]{0:T(256)(128)(2,1)} %param.28, bf16[32]{0:T(256)(128)(2,1)} %param.32, bf16[32]{0:T(256)(128)(2,1)} %param.33, bf16[32]{0:T(256)(128)(2,1)} %param.34, ...), dimensions={0} | concatenate | bytes 1536 | tf_op jit(solution)/shard_map/concatenate | solution.py:277
  14.5 6.1 %all-to-all-start = ((bf16[32,2,192]{2,1,0:T(2,128)(2,1)}), bf16[32,2,192]{2,1,0:T(2,128)(2,1)S(1)}, u32[]{:S(2)}, u32[]{:S(2)}) async-start(bf16[32,2,192]{2,1,0:T(2,128)(2,1)} %reshape.626), calls=%async_computation | async-start | bytes 65536 | tf_op jit(solution)/shard_map/all_to_all | solution.py:278
  54.4 8.3 %collective-permute-done.3 = bf16[4,32,768]{2,1,0:T(8,128)(2,1)S(1)} collective-permute-done((bf16[4,32,768]{2,1,0:T(8,128)(2,1)S(1)}, bf16[4,32,768]{2,1,0:T(8,128)(2,1)S(1)}, u32[]{:S(2)}, u32[]{:S(2)}) %collective-permute-start.3) | collective-permute-done | bytes 196640 | tf_op jit(solution)/shard_map/ppermute | solution.py:27
  64.9 8.6 %collective-permute-done.4 = bf16[4,32,768]{2,1,0:T(8,128)(2,1)S(1)} collective-permute-done((bf16[4,32,768]{2,1,0:T(8,128)(2,1)S(1)}, bf16[4,32,768]{2,1,0:T(8,128)(2,1)S(1)}, u32[]{:S(2)}, u32[]{:S(2)}) %collective-permute-start.4) | collective-permute-done | bytes 196640 | tf_op jit(solution)/shard_map/ppermute | solution.py:27
  75.8 6.5 %collective-permute-done.5 = bf16[4,32,768]{2,1,0:T(8,128)(2,1)S(1)} collective-permute-done((bf16[4,32,768]{2,1,0:T(8,128)(2,1)S(1)}, bf16[4,32,768]{2,1,0:T(8,128)(2,1)S(1)}, u32[]{:S(2)}, u32[]{:S(2)}) %collective-permute-start.5) | collective-permute-done | bytes 196640 | tf_op jit(solution)/shard_map/ppermute | solution.py:27
  87.2 4.3 collective-permute-done.36
  95.6 5.5 collective-permute-done.22
  109.4 9.9 %collective-permute-done.29 = bf16[64,2048]{1,0:T(8,128)(2,1)S(1)} collective-permute-done((bf16[64,2048]{1,0:T(8,128)(2,1)S(1)}, bf16[64,2048]{1,0:T(8,128)(2,1)S(1)}, u32[]{:S(2)}, u32[]{:S(2)}) %collective-permute-start.29) | collective-permute-done | bytes 262176 | tf_op jit(solution)/shard_map/ppermute | solution.py:27
  122.8 5.4 collective-permute-done.30
  136.4 26.1 %collective-permute-done.24 = bf16[4,32,1024]{2,1,0:T(8,128)(2,1)S(1)} collective-permute-done((bf16[4,32,1024]{2,1,0:T(8,128)(2,1)S(1)}, bf16[4,32,1024]{2,1,0:T(8,128)(2,1)S(1)}, u32[]{:S(2)}, u32[]{:S(2)}) %collective-permute-start.24) | collective-permute-done | bytes 262176 | tf_op jit(solution)/shard_map/ppermute | solution.py:27
  172.2 12.4 %attend.3 = (bf16[4,256,256]{2,1,0:T(8,128)(2,1)S(1)}, f32[4,1,1024]{2,1,0:T(1,128)S(1)}) custom-call(bf16[768,1024]{1,0:T(8,128)(2,1)S(1)} %add_convert_fusion.1.q_ref.k_ref.v_ref, bf16[768,1024]{1,0:T(8,128)(2,1)S(1)} %add_convert_fusion.1.q_ref.k_ref.v_ref, bf16[768,1024]{1,0:T(8,128)(2,1)S(1)} %add_convert_fusion.1.q_ref.k_ref.v_ref, ...), custom_call_target="tpu_custom_call" | custom-call | flops 1073741824 | bytes 3145728 | tf_op jit(solution)/shard_map/attend/pallas_call | solution.py:110
  184.7 13.8 %collective-permute-done.9 = bf16[256,1024]{1,0:T(8,128)(2,1)S(1)} collective-permute-done((bf16[256,1024]{1,0:T(8,128)(2,1)S(1)}, bf16[256,1024]{1,0:T(8,128)(2,1)S(1)}, u32[]{:S(2)}, u32[]{:S(2)}) %collective-permute-start.9) | collective-permute-done | bytes 524320 | tf_op jit(solution)/shard_map/ppermute | solution.py:27
  204.4 12.2 %attend.2 = (bf16[4,256,256]{2,1,0:T(8,128)(2,1)S(1)}, f32[4,1,1024]{2,1,0:T(1,128)S(1)}) custom-call(bf16[768,1024]{1,0:T(8,128)(2,1)S(1)} %add_convert_fusion.2.q_ref.k_ref.v_ref, bf16[768,1024]{1,0:T(8,128)(2,1)S(1)} %add_convert_fusion.2.q_ref.k_ref.v_ref, bf16[768,1024]{1,0:T(8,128)(2,1)S(1)} %add_convert_fusion.2.q_ref.k_ref.v_ref, ...), custom_call_target="tpu_custom_call" | custom-call | flops 1073741824 | bytes 3145728 | tf_op jit(solution)/shard_map/attend/pallas_call | solution.py:110
  223.1 5.9 %collective-permute-done.18 = bf16[256,256]{1,0:T(8,128)(2,1)S(1)} collective-permute-done((bf16[256,256]{1,0:T(8,128)(2,1)S(1)}, bf16[256,256]{1,0:T(8,128)(2,1)S(1)}, u32[]{:S(2)}, u32[]{:S(2)}) %collective-permute-start.18) | collective-permute-done | bytes 131104 | tf_op jit(solution)/shard_map/ppermute | solution.py:27
  229.1 4.9 collective-permute-done.10
  240.0 5.0 collective-permute-done.12
  256.6 14.2 %collective-permute-done.39 = bf16[4,128,1024]{2,1,0:T(8,128)(2,1)S(1)} collective-permute-done((bf16[4,128,1024]{2,1,0:T(8,128)(2,1)}, bf16[4,128,1024]{2,1,0:T(8,128)(2,1)S(1)}, u32[]{:S(2)}, u32[]{:S(2)}) %collective-permute-start.39) | collective-permute-done | bytes 1048608 | tf_op jit(solution)/shard_map/ppermute | solution.py:27
  273.9 8.8 %multiply_convert_fusion.1 = (bf16[1024,2048]{1,0:T(8,128)(2,1)S(1)}, f32[1024,2048]{1,0:T(8,128)}) fusion(f32[2048]{0:T(1024)S(1)} %bitcast.457, bf16[1024,2048]{1,0:T(8,128)(2,1)S(1)} %bitcast.410, bf16[512,1024]{1,0:T(8,128)(2,1)S(1)} %collective-permute-done.26, bf16[512,1024]{1,0:T(8,128)(2,1)S(1)} %fusion.22), kind=kOutput, calls=%fused_computation.8 | convolution fusion | flops 4311744512 | bytes 18882560 | tf_op jit(solution)/shard_map/dot_general | solution.py:22
  282.7 4.5 fusion.61
  304.4 11.8 %convert_reduce_fusion = (f32[2048]{0:T(1024)S(1)}, bf16[1024,2048]{1,0:T(8,128)(2,1)}) fusion(f32[1024,2048]{1,0:T(8,128)} %get-tuple-element.210, f32[2048]{0:T(1024)S(1)} %bitcast.458, bf16[2048,1024]{1,0:T(8,128)(2,1)S(1)} %bitcast.409, bf16[512,1024]{1,0:T(8,128)(2,1)S(1)} %collective-permute-done.41, bf16[512,1024]{1,0:T(8,128)(2,1)S(1)} %get-tuple-element.121), kind=kOutput, calls=%fused_computation.6 | convolution fusion | flops 4330616832 | bytes 18890752 | tf_op jit(solution)/shard_map/dot_general | solution.py:22
  316.1 6.8 %fusion.62 = f32[1024,1024]{1,0:T(8,128)S(1)} fusion(bf16[1024,2048]{1,0:T(8,128)(2,1)} %get-tuple-element.212, bf16[1024,2048]{1,0:T(8,128)(2,1)S(1)} %bitcast.411), kind=kOutput, calls=%fused_computation.274 | convolution fusion | flops 4294967296 | bytes 12582912 | tf_op jit(solution)/shard_map/dot_general | solution.py:22
  326.0 5.0 convolution_convert_fusion.1
  335.5 4.8 convolution_convert_fusion
  347.0 13.5 %collective-permute-done.70 = bf16[4,2,32,2048]{3,2,1,0:T(8,128)(2,1)} collective-permute-done((bf16[4,2,32,2048]{3,2,1,0:T(8,128)(2,1)}, bf16[4,2,32,2048]{3,2,1,0:T(8,128)(2,1)}, u32[]{:S(2)}, u32[]{:S(2)}) %collective-permute-start.70) | collective-permute-done | bytes 1048608 | tf_op jit(solution)/shard_map/ppermute | solution.py:27
  373.4 4.7 multiply_reduce_fusion
  401.1 13.2 %collective-permute-done.71 = bf16[4,2,32,2048]{3,2,1,0:T(8,128)(2,1)} collective-permute-done((bf16[4,2,32,2048]{3,2,1,0:T(8,128)(2,1)}, bf16[4,2,32,2048]{3,2,1,0:T(8,128)(2,1)}, u32[]{:S(2)}, u32[]{:S(2)}) %collective-permute-start.71) | collective-permute-done | bytes 1048608 | tf_op jit(solution)/shard_map/ppermute | solution.py:27
  432.6 20.2 %attend_back.3 = bf16[768,1024]{1,0:T(8,128)(2,1)S(1)} custom-call(bf16[768,1024]{1,0:T(8,128)(2,1)S(1)} %copy-done.1, bf16[768,1024]{1,0:T(8,128)(2,1)S(1)} %copy-done.1, bf16[768,1024]{1,0:T(8,128)(2,1)S(1)} %copy-done.1, bf16[4,256,256]{2,1,0:T(8,128)(2,1)S(1)} %bitcast_dynamic-update-slice_fusion.32.do_ref, f32[4,1,1024]{2,1,0:T(1,128)S(1)} %get-tuple-element.24.lse_ref, ...), custom_call_target="tpu_custom_call" | custom-call | flops 2684354560 | bytes 4718592 | tf_op jit(solution)/shard_map/attend_back/pallas_call | solution.py:178
  463.3 20.4 %attend_back.2 = bf16[768,1024]{1,0:T(8,128)(2,1)S(1)} custom-call(bf16[768,1024]{1,0:T(8,128)(2,1)S(1)} %add_convert_fusion.2.q_ref.k_ref.v_ref, bf16[768,1024]{1,0:T(8,128)(2,1)S(1)} %add_convert_fusion.2.q_ref.k_ref.v_ref, bf16[768,1024]{1,0:T(8,128)(2,1)S(1)} %add_convert_fusion.2.q_ref.k_ref.v_ref, ...), custom_call_target="tpu_custom_call" | custom-call | flops 2684354560 | bytes 4718592 | tf_op jit(solution)/shard_map/attend_back/pallas_call | solution.py:178
  536.7 8.3 %collective-permute-done.57 = bf16[4,32,768]{2,1,0:T(8,128)(2,1)S(1)} collective-permute-done((bf16[4,32,768]{2,1,0:T(8,128)(2,1)S(1)}, bf16[4,32,768]{2,1,0:T(8,128)(2,1)S(1)}, u32[]{:S(2)}, u32[]{:S(2)}) %collective-permute-start.57) | collective-permute-done | bytes 196640 | tf_op jit(solution)/shard_map/ppermute | solution.py:27
  551.5 7.6 %collective-permute-done.48 = bf16[256,1024]{1,0:T(8,128)(2,1)S(1)} collective-permute-done((bf16[256,1024]{1,0:T(8,128)(2,1)S(1)}, bf16[256,1024]{1,0:T(8,128)(2,1)S(1)}, u32[]{:S(2)}, u32[]{:S(2)}) %collective-permute-start.48) | collective-permute-done | bytes 524320 | tf_op jit(solution)/shard_map/ppermute | solution.py:27
  565.4 4.6 collective-permute-done.65
  571.9 5.1 collective-permute-start.67
  (481 shorter events, 285.0 us)
Async XLA Ops:
  0.7 45.9 %collective-permute-start.19 = (bf16[32,1024]{1,0:T(8,128)(2,1)}, bf16[32,1024]{1,0:T(8,128)(2,1)}, u32[]{:S(2)}, u32[]{:S(2)}) collective-permute-start(bf16[32,1024]{1,0:T(8,128)(2,1)} %param.25), channel_id=1, source_target_pairs={{0,2},{1,3},{2,0},{3,1},{4,6},{5,7},{6,4},{7,5},{8,10},{9,11},{10,... | collective-permute-start | bytes 196616 | tf_op jit(solution)/shard_map/ppermute | solution.py:27
  3.8 45.2 %collective-permute-start.20 = (bf16[32,1024]{1,0:T(8,128)(2,1)}, bf16[32,1024]{1,0:T(8,128)(2,1)}, u32[]{:S(2)}, u32[]{:S(2)}) collective-permute-start(bf16[32,1024]{1,0:T(8,128)(2,1)} %param.25), channel_id=1, source_target_pairs={{0,4},{1,5},{2,6},{3,7},{4,0},{5,1},{6,2},{7,3},{8,12},{9,13},{10,... | collective-permute-start | bytes 196616 | tf_op jit(solution)/shard_map/ppermute | solution.py:27
  6.3 46.0 %collective-permute-start.21 = (bf16[32,1024]{1,0:T(8,128)(2,1)}, bf16[32,1024]{1,0:T(8,128)(2,1)S(1)}, u32[]{:S(2)}, u32[]{:S(2)}) collective-permute-start(bf16[32,1024]{1,0:T(8,128)(2,1)} %param.25), channel_id=1, source_target_pairs={{0,6},{1,7},{2,4},{3,5},{4,2},{5,3},{6,0},{7,1},{8,14},{9,15},{10,... | collective-permute-start | bytes 196616 | tf_op jit(solution)/shard_map/ppermute | solution.py:27
  41.4 87.4 %collective-permute-start.13 = (bf16[256,1024]{1,0:T(8,128)(2,1)}, bf16[256,1024]{1,0:T(8,128)(2,1)S(1)}, u32[]{:S(2)}, u32[]{:S(2)}) collective-permute-start(bf16[256,1024]{1,0:T(8,128)(2,1)} %get-tuple-element.157), channel_id=1, source_target_pairs={{0,8},{8,0},{16,24},{24,16},{1,9},{9,1},{17,25},{25,17},{2,10},{10... | collective-permute-start | bytes 1572872 | tf_op jit(solution)/shard_map/ppermute | solution.py:27
  45.9 85.5 %collective-permute-start.14 = (bf16[256,1024]{1,0:T(8,128)(2,1)}, bf16[256,1024]{1,0:T(8,128)(2,1)S(1)}, u32[]{:S(2)}, u32[]{:S(2)}) collective-permute-start(bf16[256,1024]{1,0:T(8,128)(2,1)} %get-tuple-element.157), channel_id=1, source_target_pairs={{0,16},{8,24},{16,0},{24,8},{1,17},{9,25},{17,1},{25,9},{2,18},{10... | collective-permute-start | bytes 1572872 | tf_op jit(solution)/shard_map/ppermute | solution.py:27
  46.6 37.1 %collective-permute-start.34 = (bf16[128,1024]{1,0:T(8,128)(2,1)S(1)}, bf16[128,1024]{1,0:T(8,128)(2,1)S(1)}, u32[]{:S(2)}, u32[]{:S(2)}) collective-permute-start(bf16[128,1024]{1,0:T(8,128)(2,1)S(1)} %copy-done.40), channel_id=1, source_target_pairs={{0,2},{1,3},{2,0},{3,1},{4,6},{5,7},{6,4},{7,5},{8,10},{9,11},{10,... | collective-permute-start | bytes 786440 | tf_op jit(solution)/shard_map/ppermute | solution.py:27
  49.0 35.5 %collective-permute-start.35 = (bf16[128,1024]{1,0:T(8,128)(2,1)S(1)}, bf16[128,1024]{1,0:T(8,128)(2,1)S(1)}, u32[]{:S(2)}, u32[]{:S(2)}) collective-permute-start(bf16[128,1024]{1,0:T(8,128)(2,1)S(1)} %copy-done.40), channel_id=1, source_target_pairs={{0,4},{1,5},{2,6},{3,7},{4,0},{5,1},{6,2},{7,3},{8,12},{9,13},{10,... | collective-permute-start | bytes 786440 | tf_op jit(solution)/shard_map/ppermute | solution.py:27
  83.6 49.6 %collective-permute-start.7 = (bf16[256,1024]{1,0:T(8,128)(2,1)S(1)}, bf16[256,1024]{1,0:T(8,128)(2,1)S(1)}, u32[]{:S(2)}, u32[]{:S(2)}) collective-permute-start(bf16[256,1024]{1,0:T(8,128)(2,1)S(1)} %get-tuple-element.156), channel_id=1, source_target_pairs={{0,8},{8,0},{16,24},{24,16},{1,9},{9,1},{17,25},{25,17},{2,10},{10... | collective-permute-start | bytes 1572872 | tf_op jit(solution)/shard_map/ppermute | solution.py:27
  103.2 31.9 %collective-permute-start.8 = (bf16[256,1024]{1,0:T(8,128)(2,1)S(1)}, bf16[256,1024]{1,0:T(8,128)(2,1)S(1)}, u32[]{:S(2)}, u32[]{:S(2)}) collective-permute-start(bf16[256,1024]{1,0:T(8,128)(2,1)S(1)} %get-tuple-element.156), channel_id=1, source_target_pairs={{0,16},{8,24},{16,0},{24,8},{1,17},{9,25},{17,1},{25,9},{2,18},{10... | collective-permute-start | bytes 1572872 | tf_op jit(solution)/shard_map/ppermute | solution.py:27
  128.2 34.8 %collective-permute-start.6 = (bf16[4,4,32,768]{3,2,0,1:T(8,128)(2,1)S(1)}, bf16[4,4,32,768]{3,2,0,1:T(8,128)(2,1)S(1)}, u32[]{:S(2)}, u32[]{:S(2)}) collective-permute-start(bf16[4,4,32,768]{3,2,0,1:T(8,128)(2,1)S(1)} %bitcast_dynamic-update-slice_fusion.31), channel_id=1, source_target_pairs={{0,1},{1,0},{2,3},{3,2},{4,5},{5,4},{6,7},{7,6},{8,9},{9,8},{10,11... | collective-permute-start | bytes 2359304 | tf_op jit(solution)/shard_map/ppermute | solution.py:27
  128.9 116.4 %collective-permute-start.37 = (bf16[4,128,1024]{2,1,0:T(8,128)(2,1)}, bf16[4,128,1024]{2,1,0:T(8,128)(2,1)}, u32[]{:S(2)}, u32[]{:S(2)}) collective-permute-start(bf16[4,128,1024]{2,1,0:T(8,128)(2,1)} %bitcast_dynamic-update-slice_fusion.16), channel_id=1, source_target_pairs={{0,8},{8,0},{16,24},{24,16},{1,9},{9,1},{17,25},{25,17},{2,10},{10... | collective-permute-start | bytes 3145736 | tf_op jit(solution)/shard_map/ppermute | solution.py:27
  131.4 113.6 %collective-permute-start.38 = (bf16[4,128,1024]{2,1,0:T(8,128)(2,1)}, bf16[4,128,1024]{2,1,0:T(8,128)(2,1)}, u32[]{:S(2)}, u32[]{:S(2)}) collective-permute-start(bf16[4,128,1024]{2,1,0:T(8,128)(2,1)} %bitcast_dynamic-update-slice_fusion.16), channel_id=1, source_target_pairs={{0,16},{8,24},{16,0},{24,8},{1,17},{9,25},{17,1},{25,9},{2,18},{10... | collective-permute-start | bytes 3145736 | tf_op jit(solution)/shard_map/ppermute | solution.py:27
  135.1 31.2 %collective-permute-start.15 = (bf16[256,1024]{1,0:T(8,128)(2,1)S(1)}, bf16[256,1024]{1,0:T(8,128)(2,1)S(1)}, u32[]{:S(2)}, u32[]{:S(2)}) collective-permute-start(bf16[256,1024]{1,0:T(8,128)(2,1)S(1)} %collective-permute-done.14), channel_id=1, source_target_pairs={{0,8},{8,0},{16,24},{24,16},{1,9},{9,1},{17,25},{25,17},{2,10},{10... | collective-permute-start | bytes 1572872 | tf_op jit(solution)/shard_map/ppermute | solution.py:27
  162.5 85.5 %collective-permute-start.31 = (bf16[4,64,2048]{2,1,0:T(8,128)(2,1)S(1)}, bf16[4,64,2048]{2,1,0:T(8,128)(2,1)}, u32[]{:S(2)}, u32[]{:S(2)}) collective-permute-start(bf16[4,64,2048]{2,1,0:T(8,128)(2,1)S(1)} %bitcast_dynamic-update-slice_fusion.20), channel_id=1, source_target_pairs={{0,8},{8,0},{16,24},{24,16},{1,9},{9,1},{17,25},{25,17},{2,10},{10... | collective-permute-start | bytes 3145736 | tf_op jit(solution)/shard_map/ppermute | solution.py:27
  163.0 91.9 %collective-permute-start.32 = (bf16[4,64,2048]{2,1,0:T(8,128)(2,1)S(1)}, bf16[4,64,2048]{2,1,0:T(8,128)(2,1)}, u32[]{:S(2)}, u32[]{:S(2)}) collective-permute-start(bf16[4,64,2048]{2,1,0:T(8,128)(2,1)S(1)} %bitcast_dynamic-update-slice_fusion.20), channel_id=1, source_target_pairs={{0,16},{8,24},{16,0},{24,8},{1,17},{9,25},{17,1},{25,9},{2,18},{10... | collective-permute-start | bytes 3145736 | tf_op jit(solution)/shard_map/ppermute | solution.py:27
  166.3 32.1 %collective-permute-start.9 = (bf16[256,1024]{1,0:T(8,128)(2,1)S(1)}, bf16[256,1024]{1,0:T(8,128)(2,1)S(1)}, u32[]{:S(2)}, u32[]{:S(2)}) collective-permute-start(bf16[256,1024]{1,0:T(8,128)(2,1)S(1)} %collective-permute-done.7), channel_id=1, source_target_pairs={{0,16},{8,24},{16,0},{24,8},{1,17},{9,25},{17,1},{25,9},{2,18},{10... | collective-permute-start | bytes 1572872 | tf_op jit(solution)/shard_map/ppermute | solution.py:27
  325.8 47.6 %collective-permute-start.42 = (f32[512,1024]{1,0:T(8,128)}, f32[512,1024]{1,0:T(8,128)}, u32[]{:S(2)}, u32[]{:S(2)}) collective-permute-start(f32[512,1024]{1,0:T(8,128)} %slice.156), channel_id=1, source_target_pairs={{0,1},{1,0},{2,3},{3,2},{4,5},{5,4},{6,7},{7,6},{8,9},{9,8},{10,11... | collective-permute-start | bytes 6291464 | tf_op jit(solution)/shard_map/ppermute | solution.py:27
  344.9 55.1 %collective-permute-start.69 = (bf16[4,2,32,2048]{3,2,1,0:T(8,128)(2,1)}, bf16[4,2,32,2048]{3,2,1,0:T(8,128)(2,1)}, u32[]{:S(2)}, u32[]{:S(2)}) collective-permute-start(bf16[4,2,32,2048]{3,2,1,0:T(8,128)(2,1)} %get-tuple-element.129), channel_id=1, source_target_pairs={{0,16},{8,24},{16,0},{24,8},{1,17},{9,25},{17,1},{25,9},{2,18},{10... | collective-permute-start | bytes 3145736 | tf_op jit(solution)/shard_map/ppermute | solution.py:27
  346.0 73.9 %collective-permute-start.76 = (bf16[4,128,1024]{2,1,0:T(8,128)(2,1)}, bf16[4,128,1024]{2,1,0:T(8,128)(2,1)}, u32[]{:S(2)}, u32[]{:S(2)}) collective-permute-start(bf16[4,128,1024]{2,1,0:T(8,128)(2,1)} %get-tuple-element.127), channel_id=1, source_target_pairs={{0,8},{8,0},{16,24},{24,16},{1,9},{9,1},{17,25},{25,17},{2,10},{10... | collective-permute-start | bytes 3145736 | tf_op jit(solution)/shard_map/ppermute | solution.py:27
  363.6 50.7 %collective-permute-start.71 = (bf16[4,2,32,2048]{3,2,1,0:T(8,128)(2,1)}, bf16[4,2,32,2048]{3,2,1,0:T(8,128)(2,1)}, u32[]{:S(2)}, u32[]{:S(2)}) collective-permute-start(bf16[4,2,32,2048]{3,2,1,0:T(8,128)(2,1)} %fusion.11), channel_id=1, source_target_pairs={{0,8},{8,0},{16,24},{24,16},{1,9},{9,1},{17,25},{25,17},{2,10},{10... | collective-permute-start | bytes 3145736 | tf_op jit(solution)/shard_map/ppermute | solution.py:27
  372.3 48.0 %collective-permute-start.78 = (bf16[4,128,1024]{2,1,0:T(8,128)(2,1)}, bf16[4,128,1024]{2,1,0:T(8,128)(2,1)}, u32[]{:S(2)}, u32[]{:S(2)}) collective-permute-start(bf16[4,128,1024]{2,1,0:T(8,128)(2,1)} %fusion.8), channel_id=1, source_target_pairs={{0,16},{8,24},{16,0},{24,8},{1,17},{9,25},{17,1},{25,9},{2,18},{10... | collective-permute-start | bytes 3145736 | tf_op jit(solution)/shard_map/ppermute | solution.py:27
  389.9 34.8 %collective-permute-start.49 = (bf16[256,256]{1,0:T(8,128)(2,1)}, bf16[256,256]{1,0:T(8,128)(2,1)}, u32[]{:S(2)}, u32[]{:S(2)}) collective-permute-start(bf16[256,256]{1,0:T(8,128)(2,1)} %bitcast.385), channel_id=1, source_target_pairs={{0,8},{8,0},{16,24},{24,16},{1,9},{9,1},{17,25},{25,17},{2,10},{10... | collective-permute-start | bytes 393224 | tf_op jit(solution)/shard_map/ppermute | solution.py:27
  419.8 39.8 %collective-permute-start.43 = (bf16[256,256]{1,0:T(8,128)(2,1)S(1)}, bf16[256,256]{1,0:T(8,128)(2,1)S(1)}, u32[]{:S(2)}, u32[]{:S(2)}) collective-permute-start(bf16[256,256]{1,0:T(8,128)(2,1)S(1)} %bitcast.446), channel_id=1, source_target_pairs={{0,8},{8,0},{16,24},{24,16},{1,9},{9,1},{17,25},{25,17},{2,10},{10... | collective-permute-start | bytes 393224 | tf_op jit(solution)/shard_map/ppermute | solution.py:27
  420.3 39.4 %collective-permute-start.44 = (bf16[256,256]{1,0:T(8,128)(2,1)S(1)}, bf16[256,256]{1,0:T(8,128)(2,1)S(1)}, u32[]{:S(2)}, u32[]{:S(2)}) collective-permute-start(bf16[256,256]{1,0:T(8,128)(2,1)S(1)} %bitcast.445), channel_id=1, source_target_pairs={{0,16},{8,24},{16,0},{24,8},{1,17},{9,25},{17,1},{25,9},{2,18},{10... | collective-permute-start | bytes 393224 | tf_op jit(solution)/shard_map/ppermute | solution.py:27
  424.8 37.0 %collective-permute-start.45 = (bf16[256,256]{1,0:T(8,128)(2,1)S(1)}, bf16[256,256]{1,0:T(8,128)(2,1)S(1)}, u32[]{:S(2)}, u32[]{:S(2)}) collective-permute-start(bf16[256,256]{1,0:T(8,128)(2,1)S(1)} %bitcast.444), channel_id=1, source_target_pairs={{0,24},{8,16},{16,8},{24,0},{1,25},{9,17},{17,9},{25,1},{2,26},{10... | collective-permute-start | bytes 393224 | tf_op jit(solution)/shard_map/ppermute | solution.py:27
  427.8 75.3 %collective-permute-start.74 = (bf16[2,32,2048]{2,1,0:T(8,128)(2,1)}, bf16[2,32,2048]{2,1,0:T(8,128)(2,1)}, u32[]{:S(2)}, u32[]{:S(2)}) collective-permute-start(bf16[2,32,2048]{2,1,0:T(8,128)(2,1)} %get-tuple-element.142), channel_id=1, source_target_pairs={{0,6},{1,7},{2,4},{3,5},{4,2},{5,3},{6,0},{7,1},{8,14},{9,15},{10,... | collective-permute-start | bytes 786440 | tf_op jit(solution)/shard_map/ppermute | solution.py:27
  430.1 73.5 %collective-permute-start.73 = (bf16[2,32,2048]{2,1,0:T(8,128)(2,1)S(1)}, bf16[2,32,2048]{2,1,0:T(8,128)(2,1)}, u32[]{:S(2)}, u32[]{:S(2)}) collective-permute-start(bf16[2,32,2048]{2,1,0:T(8,128)(2,1)S(1)} %get-tuple-element.143), channel_id=1, source_target_pairs={{0,4},{1,5},{2,6},{3,7},{4,0},{5,1},{6,2},{7,3},{8,12},{9,13},{10,... | collective-permute-start | bytes 786440 | tf_op jit(solution)/shard_map/ppermute | solution.py:27
  459.6 44.7 %collective-permute-start.72 = (bf16[2,32,2048]{2,1,0:T(8,128)(2,1)}, bf16[2,32,2048]{2,1,0:T(8,128)(2,1)}, u32[]{:S(2)}, u32[]{:S(2)}) collective-permute-start(bf16[2,32,2048]{2,1,0:T(8,128)(2,1)} %get-tuple-element.141), channel_id=1, source_target_pairs={{0,2},{1,3},{2,0},{3,1},{4,6},{5,7},{6,4},{7,5},{8,10},{9,11},{10,... | collective-permute-start | bytes 786440 | tf_op jit(solution)/shard_map/ppermute | solution.py:27
  459.7 47.8 %collective-permute-start.81 = (bf16[128,1024]{1,0:T(8,128)(2,1)}, bf16[128,1024]{1,0:T(8,128)(2,1)S(1)}, u32[]{:S(2)}, u32[]{:S(2)}) collective-permute-start(bf16[128,1024]{1,0:T(8,128)(2,1)} %get-tuple-element.139), channel_id=1, source_target_pairs={{0,6},{1,7},{2,4},{3,5},{4,2},{5,3},{6,0},{7,1},{8,14},{9,15},{10,... | collective-permute-start | bytes 786440 | tf_op jit(solution)/shard_map/ppermute | solution.py:27
  461.8 46.2 %collective-permute-start.80 = (bf16[128,1024]{1,0:T(8,128)(2,1)}, bf16[128,1024]{1,0:T(8,128)(2,1)}, u32[]{:S(2)}, u32[]{:S(2)}) collective-permute-start(bf16[128,1024]{1,0:T(8,128)(2,1)} %get-tuple-element.140), channel_id=1, source_target_pairs={{0,4},{1,5},{2,6},{3,7},{4,0},{5,1},{6,2},{7,3},{8,12},{9,13},{10,... | collective-permute-start | bytes 786440 | tf_op jit(solution)/shard_map/ppermute | solution.py:27
  514.0 33.2 %collective-permute-start.52 = (bf16[256,1024]{1,0:T(8,128)(2,1)}, bf16[256,1024]{1,0:T(8,128)(2,1)}, u32[]{:S(2)}, u32[]{:S(2)}) collective-permute-start(bf16[256,1024]{1,0:T(8,128)(2,1)} %get-tuple-element.134), channel_id=1, source_target_pairs={{0,16},{8,24},{16,0},{24,8},{1,17},{9,25},{17,1},{25,9},{2,18},{10... | collective-permute-start | bytes 1572872 | tf_op jit(solution)/shard_map/ppermute | solution.py:27
  518.9 29.8 %collective-permute-start.54 = (bf16[256,1024]{1,0:T(8,128)(2,1)S(1)}, bf16[256,1024]{1,0:T(8,128)(2,1)S(1)}, u32[]{:S(2)}, u32[]{:S(2)}) collective-permute-start(bf16[256,1024]{1,0:T(8,128)(2,1)S(1)} %fusion.25), channel_id=1, source_target_pairs={{0,8},{8,0},{16,24},{24,16},{1,9},{9,1},{17,25},{25,17},{2,10},{10... | collective-permute-start | bytes 1572872 | tf_op jit(solution)/shard_map/ppermute | solution.py:27
  (109 other events, 1032.6 us)

commit v2 on v1

--- a/solution.py
+++ b/solution.py
@@ -27,8 +27,25 @@
     return lax.ppermute(x, axis, [(i, i ^ r) for i in range(n)])
 
 
+def core_swap(x):
+    return swap(x, "fsdp", 1)
+
+
+def after(x, *first):
+    return lax.optimization_barrier((x, first))[0]
+
+
 def bits_of(n):
     return [1 << b for b in range(n.bit_length() - 1)]
+
+
+def in_order(mine, got, bit, dim):
+    return jnp.where(bit == 0, jnp.stack([mine, got], axis=dim), jnp.stack([got, mine], axis=dim))
+
+
+def core_groups():
+    n = lax.axis_size("fsdp") * lax.axis_size("ctx")
+    return [list(range(k, n, 2)) for k in range(2)]
 
 
 def place(pieces, me):
@@ -39,55 +56,57 @@
     return out
 
 
+def pick(x, i):
+    return lax.dynamic_index_in_dim(x, i, 0, False)
+
+
 def gather_z(x):
     n = lax.axis_size("fsdp") // 2
-    z = lax.axis_index("fsdp") // 2
-    pieces = [x] + [swap(x, "fsdp", 2 * r) for r in range(1, n)]
-    return place(pieces, z)
+    return [x] + [swap(x, "fsdp", 2 * r) for r in range(1, n)]
 
 
 def gather_ctx(x, order):
-    n = lax.axis_size("ctx")
     pieces = {0: x}
     for b in order:
         for r in list(pieces):
             pieces[r ^ b] = swap(pieces[r], "ctx", b)
-    return place([pieces[r] for r in range(n)], lax.axis_index("ctx"))
-
-
-def scatter_ctx(x, order):
-    n = lax.axis_size("ctx")
-    me = lax.axis_index("ctx")
-    pieces = {r: lax.dynamic_index_in_dim(x, me ^ r, 0, False) for r in range(n)}
-    for b in order:
-        for r in [r for r in pieces if r & b]:
-            got = swap(pieces.pop(r).astype(BF), "ctx", b)
-            pieces[r ^ b] = pieces[r ^ b].astype(F32) + got.astype(F32)
-    return pieces[0]
-
-
-def scatter_z(x):
+    return [pieces[r] for r in range(len(pieces))]
+
+
+def exchange_ctx(x):
+    return lax.all_to_all(x, "ctx", 0, 0)
+
+
+def send_ctx(chunks):
+    return [chunks[0]] + [swap(c, "ctx", r) for r, c in enumerate(chunks) if r]
+
+
+def total_of(pieces):
+    out = pieces[0].astype(F32)
+    for p in pieces[1:]:
+        out = out + p.astype(F32)
+    return out
+
+
+def add_up(x):
+    return jnp.sum(x.astype(F32), axis=0).astype(BF)
+
+
+def z_send(x):
     n = lax.axis_size("fsdp") // 2
     z = lax.axis_index("fsdp") // 2
-    x = x.astype(BF)
-    total = lax.dynamic_index_in_dim(x, z, 0, False).astype(F32)
-    for r in range(1, n):
-        got = swap(lax.dynamic_index_in_dim(x, z ^ r, 0, False), "fsdp", 2 * r)
-        total = total + got.astype(F32)
+    return [swap(lax.dynamic_index_in_dim(x, z ^ r, 0, False), "fsdp", 2 * r) for r in range(1, n)]
+
+
+def z_sum(x, got):
+    total = lax.dynamic_index_in_dim(x, lax.axis_index("fsdp") // 2, 0, False).astype(F32)
+    for g in got:
+        total = total + g.astype(F32)
     return total
 
 
 def exchange_ctx(x):
-    n = lax.axis_size("ctx")
-    me = lax.axis_index("ctx")
-    pieces = [lax.dynamic_index_in_dim(x, me, 0, False)]
-    for r in range(1, n):
-        pieces.append(swap(lax.dynamic_index_in_dim(x, me ^ r, 0, False), "ctx", r))
-    return place(pieces, me)
-
-
-def core_swap(x):
-    return swap(x, "fsdp", 1)
+    return lax.all_to_all(x, "ctx", 0, 0)
 
 
 def attend_kernel(q_ref, k_ref, v_ref, srow_ref, scol_ref, o_ref, lse_ref):
@@ -127,9 +146,9 @@
         ],
         compiler_params=pltpu.CompilerParams(vmem_limit_bytes=VMEM_LIMIT),
         cost_estimate=pl.CostEstimate(
-            flops=4 * heads * HD * length * length,
-            transcendentals=heads * length * length,
-            bytes_accessed=4 * rows * length,
+            flops=1 << 20,
+            transcendentals=1 << 10,
+            bytes_accessed=1 << 20,
         ),
         name="attend",
     )(qkv, qkv, qkv, seg[None, :], seg[:, None])
@@ -170,7 +189,7 @@
         out_ref[pl.ds(pl.multiple_of((2 * heads + h) * HD, HD), HD), :] = dv_ref[...].astype(BF)
 
 
-def attend_back(qkv, do, lse, seg, block):
+def attend_back(qkv, do, group, lse, seg, block):
     rows, length = qkv.shape
     heads = rows // (3 * HD)
     nq = length // block
@@ -182,7 +201,7 @@
             pl.BlockSpec((HD, block), lambda h, i: (h, i)),
             whole(1),
             whole(2),
-            pl.BlockSpec((1, HD, block), lambda h, i: (i, h, 0)),
+            pl.BlockSpec((1, HD, block), lambda h, i: (i, h, group)),
             pl.BlockSpec((1, 1, block), lambda h, i: (h, 0, i)),
             pl.BlockSpec((1, block), lambda h, i: (0, i)),
             pl.BlockSpec((length, 1), lambda h, i: (0, 0)),
@@ -192,9 +211,9 @@
         scratch_shapes=[pltpu.VMEM((HD, length), F32), pltpu.VMEM((HD, length), F32)],
         compiler_params=pltpu.CompilerParams(vmem_limit_bytes=VMEM_LIMIT),
         cost_estimate=pl.CostEstimate(
-            flops=10 * heads * HD * length * length,
-            transcendentals=heads * length * length,
-            bytes_accessed=6 * rows * length,
+            flops=1 << 20,
+            transcendentals=1 << 10,
+            bytes_accessed=1 << 20,
         ),
         name="attend_back",
     )(qkv, qkv, qkv, do, lse, seg[None, :], seg[:, None])
@@ -259,42 +278,39 @@
     groups = micro * per_device
     order_a = bits_of(nc)
     order_b = order_a[::-1]
-
-    mine = tokens.reshape(groups, ctx_rows, width)
-    inputs_all = [
-        gather_ctx(mine[g], order_a if g % 2 == 0 else order_b).reshape(length, width) for g in range(groups)
-    ]
+    me_c, me_z = me, fi // 2
 
     w_qkv = jnp.stack([w_query, w_key, w_value], axis=1).reshape(rows_w, 3, nc, cols)
-    w_qkv = exchange_ctx(jnp.moveaxis(w_qkv, 2, 0).reshape(nc, rows_w, 3 * cols))
-    w_qkv = gather_z(w_qkv)
-    other = core_swap(w_qkv)
-    w_qkv = jnp.where(core == 0, jnp.stack([w_qkv, other], axis=2), jnp.stack([other, w_qkv], axis=2))
-    w_qkv = jnp.moveaxis(w_qkv.reshape(nz, nc, 2, rows_w, 3 * cols), 0, 1)
-    w_qkv = w_qkv.reshape(nc, nz, 2, rows_w, 3 * cols).reshape(width, 3 * cols)
-
+    w_qkv = jnp.moveaxis(w_qkv, 2, 0).reshape(nc, rows_w, 3 * cols)
     vectors = (b_query, b_value, b_out, ln1_gain, ln1_bias, b_down, ln2_gain, ln2_bias, b_up)
     packed = jnp.concatenate(vectors)
-    packed = lax.all_to_all(
-        jnp.broadcast_to(packed[None], (nc * nf,) + packed.shape), BOTH, 0, 0
-    ).reshape(nc * nf, packed.shape[0])
+    packed = jnp.pad(packed, (0, 8 * 3 * cols - packed.shape[0])).reshape(1, 8, 3 * cols)
+    sent = jnp.concatenate([w_qkv, jnp.broadcast_to(packed, (nc, 8, 3 * cols))], axis=1)
+    sent_c = send_ctx([pick(sent, me ^ r) for r in range(nc)])
+    sent_z = gather_z(place(sent_c, me_c))
+    mine = tokens.reshape(groups, ctx_rows, width)
+    inputs_all = []
+    for g in range(groups):
+        rows_now = after(mine[g], sent_c) if g == 0 else after(mine[g], inputs_all[g - 1])
+        inputs_all.append(exchange_ctx(jnp.broadcast_to(rows_now[None], (nc, ctx_rows, width))))
+    inputs_all = [t.reshape(length, width) for t in inputs_all]
+    sent = place(sent_z, me_z)
+    sent = in_order(sent, core_swap(sent), core, 2)
+    sent = jnp.moveaxis(sent, 0, 1)
+    w_qkv = sent[:, :, :, :rows_w].reshape(width, 3 * cols)
+    packed = sent[:, :, :, rows_w:].reshape(nc * nf, 8 * 3 * cols)
     full = [packed[:, j * rows_w : (j + 1) * rows_w].reshape(width) for j in range(8)]
     query_bias, value_bias, out_bias, gain_one, bias_one, down_bias, gain_two, bias_two = full
-    up_bias = packed[:, 8 * rows_w :].reshape(nc * nz, 2, ff_w)
+    up_bias = packed[:, 8 * rows_w : 8 * rows_w + ff_w].reshape(nc * nz, 2, ff_w)
     up_bias = lax.dynamic_index_in_dim(up_bias, core, 1, False).reshape(half)
-
-    out_mat = gather_ctx(gather_z(w_out), order_a)
-    out_other = core_swap(out_mat)
-    out_mat = jnp.where(core == 0, jnp.stack([out_mat, out_other], axis=2), jnp.stack([out_other, out_mat], axis=2))
-    out_mat = out_mat.reshape(width, width)
 
     split = w_up.reshape(rows_w, half // ff_w, 2, ff_w)
     keep = lax.dynamic_index_in_dim(split, core, 2, False).reshape(rows_w, half)
     give = lax.dynamic_index_in_dim(split, 1 - core, 2, False).reshape(rows_w, half)
-    got = core_swap(give)
-    up_mine = jnp.where(core == 0, jnp.stack([keep, got]), jnp.stack([got, keep])).reshape(2 * rows_w, half)
-    up_mat = gather_ctx(gather_z(up_mine), order_a).reshape(width, half)
-    down_mat = gather_ctx(gather_z(w_down), order_b).reshape(half, width)
+    up_mine = in_order(keep, core_swap(give), core, 0).reshape(2 * rows_w, half)
+    parts = half // width
+    own = jnp.concatenate([up_mine[:, j * width : (j + 1) * width] for j in range(parts)] + [w_down, w_out])
+    own = lax.all_gather(own, BOTH, axis=0, axis_index_groups=core_groups())
 
     key_pos = jnp.arange(length, dtype=jnp.int32)
     lengths = doc_lengths.reshape(groups, -1)
@@ -307,15 +323,24 @@
         ]
     ).astype(F32)[:, None]
     segs, qkvs, lses, mixed = [], [], [], []
+    outs = []
     for g in range(groups):
-        seg = segment_ids(lengths[g], key_pos)
-        qkv = (dot(w_qkv, inputs_all[g], 0, 1) + qkv_bias).astype(BF)
-        o, lse = attend(qkv, seg, ctx_rows)
-        mixed.append(exchange_ctx(o).reshape(width, ctx_rows))
-        segs.append(seg)
-        qkvs.append(qkv)
+        segs.append(segment_ids(lengths[g], key_pos))
+        rows_now = inputs_all[g] if g == 0 else after(inputs_all[g], outs[0])
+        qkvs.append((dot(w_qkv, rows_now, 0, 1) + qkv_bias).astype(BF))
+        o, lse = attend(qkvs[g], segs[g], ctx_rows)
+        outs.append(o)
         lses.append(lse)
-    mixed = jnp.concatenate(mixed, axis=1)
+        mixed.append(exchange_ctx(o if g == 0 else after(o, mixed[-1])))
+    own = after(own, mixed[-1])
+    mixed = jnp.concatenate([t.reshape(width, ctx_rows) for t in mixed], axis=1)
+    n_up = 2 * rows_w * parts
+    up_mat = jnp.concatenate(
+        [own[:, j * 2 * rows_w : (j + 1) * 2 * rows_w].reshape(width, width) for j in range(parts)], axis=1
+    )
+    down_mat = own[:, n_up : n_up + ff_w].reshape(half, width)
+    out_mine = own[:, n_up + ff_w :]
+    out_mat = in_order(out_mine, core_swap(out_mine), core, 1).reshape(width, width)
 
     inputs = mine.reshape(flat_rows, width).astype(F32)
     attended = dot(mixed, out_mat, 0, 0) + out_bias
@@ -336,16 +361,17 @@
     grad_branch = grad_h2.astype(BF)
     grad_down_bias = jnp.sum(grad_branch.astype(F32), axis=0)
     both_branch = jnp.concatenate([grad_branch, core_swap(grad_branch)])
-    grad_down = dot(activated, both_branch, 0, 0).astype(BF).reshape(nc, nz, ff_w, width)
-    grad_down = scatter_z(scatter_ctx(grad_down, order_a))
+    grad_down = dot(activated, both_branch, 0, 0).astype(BF)
     grad_hidden = (dot(both_branch, down_mat, 1, 1) * slope.astype(F32)).astype(BF)
     grad_up_bias = jnp.sum(grad_hidden.astype(F32), axis=0)
-    grad_up = dot(both_first, grad_hidden, 0, 0).astype(BF).reshape(nc, nz, 2, rows_w, half)
-    grad_up = scatter_z(scatter_ctx(grad_up, order_b))
-    grad_up_mine = lax.dynamic_index_in_dim(grad_up, core, 0, False)
-    grad_up_got = core_swap(lax.dynamic_index_in_dim(grad_up, 1 - core, 0, False))
-    pair = [t.reshape(rows_w, half // ff_w, ff_w) for t in (grad_up_mine, grad_up_got)]
-    grad_up = jnp.where(core == 0, jnp.stack(pair, axis=2), jnp.stack(pair[::-1], axis=2)).reshape(rows_w, ff)
+    grad_ups = [
+        dot(both_first, grad_hidden[:, j * width : (j + 1) * width], 0, 0).astype(BF) for j in range(parts)
+    ]
+    grad_ffn = jnp.concatenate(
+        [t.reshape(nc * nz, 2 * rows_w, width) for t in grad_ups] + [grad_down.reshape(nc * nz, ff_w, width)], axis=1
+    )
+    grad_ffn = lax.psum_scatter(grad_ffn, BOTH, scatter_dimension=0, axis_index_groups=core_groups()).astype(F32)
+    grad_down = grad_ffn[n_up:]
     part = dot(grad_hidden, up_mat, 1, 1)
     grad_first = part[:flat_rows] + core_swap(part[flat_rows:]) + grad_h2
     grad_h1, grad_gain_one, grad_bias_one = norm_backward(grad_first, normed_one, inverse_one, gain_one)
@@ -353,32 +379,30 @@
     grad_out_bias = jnp.sum(grad_attended.astype(F32), axis=0)
     grad_mixed = dot(out_mat, grad_attended, 1, 1).astype(BF)
     grad_mixed = grad_mixed.reshape(nc, cols, groups, ctx_rows)
+    dos = []
+    for g in range(groups):
+        do = grad_mixed[:, :, g]
+        dos.append(exchange_ctx(do if g == 0 else after(do, dos[0])))
     grad_out = dot(mixed, grad_attended, 1, 0).astype(BF).reshape(nc, nz, 2, rows_w, width)
     grad_out_got = core_swap(lax.dynamic_index_in_dim(grad_out, 1 - core, 2, False))
     grad_out = lax.dynamic_index_in_dim(grad_out, core, 2, False).astype(F32) + grad_out_got.astype(F32)
-    grad_out = scatter_z(scatter_ctx(grad_out.astype(BF), order_a))
-
+    grad_out = after(grad_out.astype(BF), dos[0])
+    out_raw = send_ctx([pick(grad_out, me ^ r) for r in range(nc)])
+
+    backs = []
     grad_qkv = None
     grad_bias_parts = []
-    input_grads = []
     for g in range(groups):
-        do = exchange_ctx(grad_mixed[:, :, g])
-        dqkv = attend_back(qkvs[g], do, lses[g], segs[g], ctx_rows)
+        dqkv = attend_back(qkvs[g], dos[g], 0, lses[g], segs[g], ctx_rows)
+        if g == 1:
+            dqkv, backs[0] = lax.optimization_barrier((dqkv, backs[0]))
         grad_bias_parts.append(jnp.sum(dqkv.astype(F32), axis=1))
+        back = dot(dqkv, w_qkv, 0, 1).astype(BF).reshape(nc, ctx_rows, width)
+        if g + 1 < groups:
+            qkvs[g + 1] = after(qkvs[g + 1], back)
+        backs.append(exchange_ctx(back))
         now = dot(inputs_all[g], dqkv, 0, 1)
         grad_qkv = now if grad_qkv is None else grad_qkv + now
-        back = dot(dqkv, w_qkv, 0, 1).astype(BF).reshape(nc, ctx_rows, width)
-        input_grads.append(scatter_ctx(back, order_a if g % 2 == 0 else order_b))
-    grad_tokens = grad_h1.reshape(groups, ctx_rows, width) + jnp.stack(input_grads)
-    grad_tokens = grad_tokens.reshape(micro, per_device, ctx_rows, width)
-
-    grad_qkv = grad_qkv.astype(BF).reshape(nc, nz, 2, rows_w, 3 * cols)
-    grad_qkv_got = core_swap(lax.dynamic_index_in_dim(grad_qkv, 1 - core, 2, False))
-    grad_qkv = lax.dynamic_index_in_dim(grad_qkv, core, 2, False).astype(F32) + grad_qkv_got.astype(F32)
-    grad_qkv = scatter_z(jnp.moveaxis(grad_qkv.astype(BF), 1, 0))
-    grad_qkv = exchange_ctx(grad_qkv).reshape(nc, rows_w, 3, cols)
-    grad_qkv = jnp.moveaxis(grad_qkv, 0, 2).reshape(rows_w, 3, width)
-
     grad_bias = sum(grad_bias_parts).reshape(3, cols)
     spread = lambda v: lax.dynamic_update_slice_in_dim(jnp.zeros((width,), F32), v, me * cols, 0)
     small = [
@@ -396,7 +420,29 @@
     pair = [jnp.where(core == j, grad_up_bias, 0.0) for j in range(2)]
     small.append(jnp.stack(pair, axis=1).reshape(nc * nf, ff_w))
     small = jnp.concatenate(small, axis=1)
-    small = jnp.sum(lax.all_to_all(small, BOTH, 0, 0), axis=0)
+    grad_qkv = grad_qkv.astype(BF).reshape(nc, nz, 2, rows_w, 3 * cols)
+    grad_qkv_got = core_swap(lax.dynamic_index_in_dim(grad_qkv, 1 - core, 2, False))
+    grad_out = total_of(after(out_raw, dqkv)).astype(BF)
+    out_got = z_send(grad_out)
+    grad_qkv = lax.dynamic_index_in_dim(grad_qkv, core, 2, False).astype(F32) + grad_qkv_got.astype(F32)
+    grad_qkv = jnp.moveaxis(grad_qkv.astype(BF), 1, 0)
+    grad_qkv = z_sum(grad_qkv, z_send(grad_qkv))
+    small = jnp.sum(lax.all_to_all(after(small, backs[-1]), BOTH, 0, 0), axis=0)
+    grad_qkv = exchange_ctx(after(grad_qkv, backs[-1])).reshape(nc, rows_w, 3, cols)
+    grad_qkv = jnp.moveaxis(grad_qkv, 0, 2).reshape(rows_w, 3, width)
+    input_grads = [jnp.sum(t.astype(F32), axis=0) for t in backs]
+    grad_out = z_sum(grad_out, out_got)
+    grad_up = [grad_ffn[j * 2 * rows_w : (j + 1) * 2 * rows_w] for j in range(parts)]
+    grad_up = jnp.concatenate(grad_up, axis=1).reshape(2, rows_w, half)
+    grad_up_got = core_swap(lax.dynamic_index_in_dim(grad_up, 1 - core, 0, False))
+    pair = [
+        t.reshape(rows_w, half // ff_w, ff_w)
+        for t in (lax.dynamic_index_in_dim(grad_up, core, 0, False), grad_up_got)
+    ]
+    grad_up = in_order(pair[0], pair[1], core, 2).reshape(rows_w, ff)
+    grad_tokens = grad_h1.reshape(groups, ctx_rows, width) + jnp.stack(input_grads)
+    grad_tokens = grad_tokens.reshape(micro, per_device, ctx_rows, width)
+
     small_out = [small[j * rows_w : (j + 1) * rows_w] for j in range(8)]
     g_bq, g_bv, g_bo, g_g1, g_b1, g_bd, g_g2, g_b2 = small_out
     g_bu = small[8 * rows_w :]

time: 592 us -> 482 us (0.81)
  the two profiles are of different devices: /device:TPU:0 before, /device:TPU:1 now
where the time goes in v2:
time: 482 us; the launch traced here: 472 us
  waiting for transfers between devices  151 us (31%)
  matrix products  74.3 us (15%)
  Pallas kernels  67.3 us (14%)
  starting transfers between devices  62.2 us (13%)
  local copies, waits for them, and re-layouts  48.9 us (10%)
  other arithmetic  41.1 us (9%)
  between operations  15.8 us (3%)
  blocking collectives  11.4 us (2%)
    ppermute x25, waiting for transfers between devices, swap(): return lax.ppermute(x, axis, [(i, i ^ r) for i in range(n)])  94.4 us
    dot_general x16, matrix products, dot(): lax.dot_general(a, b, (((ca,), (cb,)), ((), ())), preferred_element_type=...  74.3 us
    pallas_call x2, Pallas kernels, attend_back(): pl.pallas_call(functools.partial(attend_back_kernel, heads, nq, block), g...  42.4 us
    all_to_all x8, waiting for transfers between devices, exchange_ctx(): return lax.all_to_all(x, 'ctx', 0, 0)  39.4 us
    all_to_all x8, starting transfers between devices, exchange_ctx(): return lax.all_to_all(x, 'ctx', 0, 0)  34.2 us
    pallas_call x2, Pallas kernels, attend(): pl.pallas_call(attend_kernel, grid=(heads, nq), in_specs=[pl.BlockSpec((H...  24.9 us
    ppermute x25, starting transfers between devices, swap(): return lax.ppermute(x, axis, [(i, i ^ r) for i in range(n)])  23.5 us
    unnamed x109, local copies, waits for them, and re-layouts  13.1 us
  transfers between devices with their start and end apart: 36, of which 22 were waited for; matrix products, arithmetic and copies ran while one was open for 20% of the time, Pallas kernels for 14%

profile of v2, /device:TPU:1, one launch (start us, length us, event | category | flops | bytes accessed | tf_op | source)
XLA Modules:
  0.0 471.9 jit_solution(11526525836726414904)
XLA Ops:
  22.4 4.5 all-to-all-start
  30.9 14.0 %collective-permute-done.3 = bf16[4,40,768]{2,1,0:T(8,128)(2,1)S(1)} collective-permute-done((bf16[4,40,768]{2,1,0:T(8,128)(2,1)S(1)}, bf16[4,40,768]{2,1,0:T(8,128)(2,1)S(1)}, u32[]{:S(2)}, u32[]{:S(2)}) %collective-permute-start.3) | collective-permute-done | bytes 245792 | tf_op jit(solution)/shard_map/ppermute | solution.py:27
  45.0 27.5 %collective-permute-done.4 = bf16[4,40,768]{2,1,0:T(8,128)(2,1)S(1)} collective-permute-done((bf16[4,40,768]{2,1,0:T(8,128)(2,1)S(1)}, bf16[4,40,768]{2,1,0:T(8,128)(2,1)S(1)}, u32[]{:S(2)}, u32[]{:S(2)}) %collective-permute-start.4) | collective-permute-done | bytes 245792 | tf_op jit(solution)/shard_map/ppermute | solution.py:27
  77.4 4.5 all-to-all-start.2
  90.2 12.8 %attend.2 = (bf16[4,256,256]{2,1,0:T(8,128)(2,1)}, f32[4,1,1024]{2,1,0:T(1,128)S(1)}) custom-call(bf16[768,1024]{1,0:T(8,128)(2,1)S(1)} %add_convert_fusion.2.q_ref.k_ref.v_ref, bf16[768,1024]{1,0:T(8,128)(2,1)S(1)} %add_convert_fusion.2.q_ref.k_ref.v_ref, bf16[768,1024]{1,0:T(8,128)(2,1)S(1)} %add_convert_fusion.2.q_ref.k_ref.v_ref, ...), custom_call_target="tpu_custom_call" | custom-call | flops 1048576 | bytes 1048576 | tf_op jit(solution)/shard_map/attend/pallas_call | solution.py:129
  102.9 17.1 %all-to-all-done.2 = bf16[4,256,1024]{2,1,0:T(8,128)(2,1)} async-done(((bf16[4,256,1024]{2,1,0:T(8,128)(2,1)}), bf16[4,256,1024]{2,1,0:T(8,128)(2,1)}, u32[]{:S(2)}, u32[]{:S(2)}) %all-to-all-start.2) | async-done | bytes 2097184 | tf_op jit(solution)/shard_map/all_to_all | solution.py:109
  128.3 12.2 %attend.3 = (bf16[4,256,256]{2,1,0:T(8,128)(2,1)S(1)}, f32[4,1,1024]{2,1,0:T(1,128)S(1)}) custom-call(bf16[768,1024]{1,0:T(8,128)(2,1)S(1)} %add_convert_fusion.1.q_ref.k_ref.v_ref, bf16[768,1024]{1,0:T(8,128)(2,1)S(1)} %add_convert_fusion.1.q_ref.k_ref.v_ref, bf16[768,1024]{1,0:T(8,128)(2,1)S(1)} %add_convert_fusion.1.q_ref.k_ref.v_ref, ...), custom_call_target="tpu_custom_call" | custom-call | flops 1048576 | bytes 1048576 | tf_op jit(solution)/shard_map/attend/pallas_call | solution.py:129
  141.3 11.4 %all_to_all.54 = bf16[4,256,256]{2,1,0:T(8,128)(2,1)} all-to-all(bf16[4,256,256]{2,1,0:T(8,128)(2,1)} %copy-done.6), channel_id=1, replica_groups=mesh['ctx'=4,'fsdp'=8] {'ctx'}, dimensions={0} | all-to-all | bytes 1048576 | tf_op jit(solution)/shard_map/all_to_all | solution.py:109
  152.6 12.9 %all-gather.3.cloned.1.call-done = bf16[4608,1024]{1,0:T(8,128)(2,1)} async-done(((bf16[288,1024]{1,0:T(8,128)(2,1)}), bf16[4608,1024]{1,0:T(8,128)(2,1)}) %all-gather.3.cloned.1.call-update) | async-done | bytes 9437200 | tf_op jit(solution)/shard_map/all_gather | solution.py:313
  181.4 7.6 %multiply_convert_fusion.1 = (bf16[1024,2048]{1,0:T(8,128)(2,1)S(1)}, f32[1024,2048]{1,0:T(8,128)}) fusion(f32[2048]{0:T(1024)S(1)} %bitcast.258, bf16[1024,1024]{1,0:T(8,128)(2,1)S(1)} %bitcast.233, bf16[1024,1024]{1,0:T(8,128)(2,1)S(1)} %bitcast.231, bf16[512,1024]{1,0:T(8,128)(2,1)S(1)} %collective-permute-done.9, bf16[512,1024]{1,0:T(8,128)(2,1)S(1)} %fusion.29), kind=kOutput, calls=%fused_computation.9 | convolution fusion | flops 4320133120 | bytes 18882560 | tf_op jit(solution)/shard_map/dot_general | solution.py:22
  189.0 4.5 fusion.64
  210.7 4.9 %convolution_convert_fusion = bf16[2048,1024]{1,0:T(8,128)(2,1)S(1)} fusion(bf16[1024,2048]{1,0:T(8,128)(2,1)S(1)} %copy-done.51, bf16[512,1024]{1,0:T(8,128)(2,1)S(1)} %collective-permute-done.11, bf16[512,1024]{1,0:T(8,128)(2,1)S(1)} %get-tuple-element.153), kind=kOutput, calls=%fused_computation.14 | convolution fusion | flops 4301258752 | bytes 10485760 | tf_op jit(solution)/shard_map/dot_general | solution.py:22
  215.7 11.0 %convert_reduce_fusion = (f32[2048]{0:T(1024)S(1)}, bf16[1024,2048]{1,0:T(8,128)(2,1)S(1)}) fusion(f32[1024,2048]{1,0:T(8,128)} %get-tuple-element.218, f32[2048]{0:T(1024)S(1)} %bitcast.259, bf16[2048,1024]{1,0:T(8,128)(2,1)S(1)} %bitcast.215, bf16[512,1024]{1,0:T(8,128)(2,1)S(1)} %collective-permute-done.11, bf16[512,1024]{1,0:T(8,128)(2,1)S(1)} %get-tuple-element.153), kind=kOutput, calls=%fused_computation.7 | convolution fusion | flops 4330616832 | bytes 18890752 | tf_op jit(solution)/shard_map/dot_general | solution.py:22
  235.3 7.6 %fusion.5 = f32[1024,1024]{1,0:T(8,128)S(1)} fusion(bf16[1024,2048]{1,0:T(8,128)(2,1)} %copy-done.49, bf16[1024,1024]{1,0:T(8,128)(2,1)} %bitcast.234, bf16[1024,1024]{1,0:T(8,128)(2,1)} %bitcast.232), kind=kOutput, calls=%fused_computation.20 | convolution fusion | flops 4303355904 | bytes 12582912 | tf_op jit(solution)/shard_map/dot_general | solution.py:22
  250.2 5.6 %multiply_reduce_fusion = (f32[1024]{0:T(1024)S(1)}, f32[512]{0:T(512)S(1)}, f32[512]{0:T(512)S(1)}, f32[1024]{0:T(1024)S(1)}, f32[512,1024]{1,0:T(8,128)S(1)}, /*index=5*/bf16[512,1024]{1,0:T(8,128)(2,1)}) fusion(f32[512,1024]{1,0:T(8,128)} %copy-done.7, f32[512]{0:T(512)S(1)} %add_rsqrt_fusion.1, f32[512]{0:T(512)S(1)} %broadcast_multiply_fusion.4, ...), kind=kLoop, calls=%fused_computation.50 | loop fusion | flops 11531264 | bytes 12619776 | tf_op jit(solution)/shard_map/reduce_sum | solution.py:236
  267.1 4.4 all-to-all-start.4
  273.6 4.5 convolution_convert_fusion.1
  278.1 7.2 %all-to-all-done.4.do_ref = bf16[4,256,256]{2,1,0:T(8,128)(2,1)} async-done(((bf16[4,256,256]{2,1,0:T(8,128)(2,1)}), bf16[4,256,256]{2,1,0:T(8,128)(2,1)}, u32[]{:S(2)}, u32[]{:S(2)}) %all-to-all-start.4) | async-done | bytes 524320 | tf_op jit(solution)/shard_map/all_to_all | solution.py:109
  285.4 4.1 all-to-all-start.5
  290.6 21.2 %attend_back.2 = bf16[768,1024]{1,0:T(8,128)(2,1)S(1)} custom-call(bf16[768,1024]{1,0:T(8,128)(2,1)S(1)} %add_convert_fusion.2.q_ref.k_ref.v_ref, bf16[768,1024]{1,0:T(8,128)(2,1)S(1)} %add_convert_fusion.2.q_ref.k_ref.v_ref, bf16[768,1024]{1,0:T(8,128)(2,1)S(1)} %add_convert_fusion.2.q_ref.k_ref.v_ref, bf16[4,256,256]{2,1,0:T(8,128)(2,1)} %all-to-all-done.4.do_ref, ...), custom_call_target="tpu_custom_call" | custom-call | flops 1048576 | bytes 1048576 | tf_op jit(solution)/shard_map/attend_back/pallas_call | solution.py:197
  316.1 4.5 all-to-all-start.6
  324.4 5.2 %fusion.65 = f32[1024,768]{1,0:T(8,128)} fusion(bf16[1024,1024]{1,0:T(8,128)(2,1)} %bitcast.20, bf16[768,1024]{1,0:T(8,128)(2,1)S(1)} %copy-done.1), kind=kOutput, calls=%fused_computation.189 | convolution fusion | flops 1610612736 | bytes 6815744 | tf_op jit(solution)/shard_map/dot_general | solution.py:22
  329.6 21.2 %attend_back.3 = bf16[768,1024]{1,0:T(8,128)(2,1)S(1)} custom-call(bf16[768,1024]{1,0:T(8,128)(2,1)S(1)} %add_convert_fusion.1.q_ref.k_ref.v_ref, bf16[768,1024]{1,0:T(8,128)(2,1)S(1)} %add_convert_fusion.1.q_ref.k_ref.v_ref, bf16[768,1024]{1,0:T(8,128)(2,1)S(1)} %add_convert_fusion.1.q_ref.k_ref.v_ref, bf16[4,256,256]{2,1,0:T(8,128)(2,1)} %all-to-all-done.5.do_ref, ...), custom_call_target="tpu_custom_call" | custom-call | flops 1048576 | bytes 1048576 | tf_op jit(solution)/shard_map/attend_back/pallas_call | solution.py:197
  356.4 13.8 %all-to-all-done.6 = bf16[4,256,1024]{2,1,0:T(8,128)(2,1)} async-done(((bf16[4,256,1024]{2,1,0:T(8,128)(2,1)}), bf16[4,256,1024]{2,1,0:T(8,128)(2,1)}, u32[]{:S(2)}, u32[]{:S(2)}) %all-to-all-start.6) | async-done | bytes 2097184 | tf_op jit(solution)/shard_map/all_to_all | solution.py:109
  373.4 4.7 all-to-all-start.7
  378.1 4.5 add_convert_fusion
  384.8 6.8 %collective-permute-done.19 = bf16[4,32,1024]{2,1,0:T(8,128)(2,1)} collective-permute-done((bf16[4,32,1024]{2,1,0:T(8,128)(2,1)}, bf16[4,32,1024]{2,1,0:T(8,128)(2,1)}, u32[]{:S(2)}, u32[]{:S(2)}) %collective-permute-start.19) | collective-permute-done | bytes 262176 | tf_op jit(solution)/shard_map/ppermute | solution.py:27
  402.5 5.8 %collective-permute-done.22 = bf16[32,1024]{1,0:T(8,128)(2,1)} collective-permute-done((bf16[32,1024]{1,0:T(8,128)(2,1)S(1)}, bf16[32,1024]{1,0:T(8,128)(2,1)}, u32[]{:S(2)}, u32[]{:S(2)}) %collective-permute-start.22) | collective-permute-done | bytes 65568 | tf_op jit(solution)/shard_map/ppermute | solution.py:27
  409.9 5.9 %collective-permute-done.14 = bf16[4,32,768]{2,1,0:T(8,128)(2,1)S(1)} collective-permute-done((bf16[4,32,768]{2,1,0:T(8,128)(2,1)S(1)}, bf16[4,32,768]{2,1,0:T(8,128)(2,1)S(1)}, u32[]{:S(2)}, u32[]{:S(2)}) %collective-permute-start.14) | collective-permute-done | bytes 196640 | tf_op jit(solution)/shard_map/ppermute | solution.py:27
  415.8 4.2 collective-permute-done.16
  420.0 13.7 %collective-permute-done.15 = bf16[4,32,768]{2,1,0:T(8,128)(2,1)S(1)} collective-permute-done((bf16[4,32,768]{2,1,0:T(8,128)(2,1)S(1)}, bf16[4,32,768]{2,1,0:T(8,128)(2,1)S(1)}, u32[]{:S(2)}, u32[]{:S(2)}) %collective-permute-start.15) | collective-permute-done | bytes 196640 | tf_op jit(solution)/shard_map/ppermute | solution.py:27
  435.2 4.4 all-to-all-start.9
  (305 shorter events, 162.0 us)
Async XLA Ops:
  7.2 158.3 %all-gather.3.cloned.1.call-start = ((), (), s32[]{:S(2)}) async-start(), calls=%async_computation.12 | async-start | bytes 10027008 | tf_op jit(solution)/shard_map/all_gather | solution.py:313
  14.1 5.5 %collective-permute-start.2 = (bf16[40,768]{1,0:T(8,128)(2,1)S(1)}, bf16[40,768]{1,0:T(8,128)(2,1)S(1)}, u32[]{:S(2)}, u32[]{:S(2)}) collective-permute-start(bf16[40,768]{1,0:T(8,128)(2,1)S(1)} %get-tuple-element.197), channel_id=1, source_target_pairs={{0,24},{8,16},{16,8},{24,0},{1,25},{9,17},{17,9},{25,1},{2,26},{10... | collective-permute-start | bytes 184328 | tf_op jit(solution)/shard_map/ppermute | solution.py:27
  17.5 3.3 collective-permute-start
  22.4 53.4 %all-to-all-start = ((bf16[4,256,1024]{2,1,0:T(8,128)(2,1)}), bf16[4,256,1024]{2,1,0:T(8,128)(2,1)}, u32[]{:S(2)}, u32[]{:S(2)}) async-start(bf16[4,256,1024]{2,1,0:T(8,128)(2,1)} %broadcast_in_dim.98), calls=%async_computation | async-start | bytes 4194304 | tf_op jit(solution)/shard_map/all_to_all | solution.py:109
  27.0 18.0 %collective-permute-start.3 = (bf16[4,40,768]{2,1,0:T(8,128)(2,1)S(1)}, bf16[4,40,768]{2,1,0:T(8,128)(2,1)S(1)}, u32[]{:S(2)}, u32[]{:S(2)}) collective-permute-start(bf16[4,40,768]{2,1,0:T(8,128)(2,1)S(1)} %bitcast_dynamic-update-slice_fusion.4), channel_id=1, source_target_pairs={{0,2},{1,3},{2,0},{3,1},{4,6},{5,7},{6,4},{7,5},{8,10},{9,11},{10,... | collective-permute-start | bytes 737288 | tf_op jit(solution)/shard_map/ppermute | solution.py:27
  28.5 44.1 %collective-permute-start.5 = (bf16[4,40,768]{2,1,0:T(8,128)(2,1)S(1)}, bf16[4,40,768]{2,1,0:T(8,128)(2,1)S(1)}, u32[]{:S(2)}, u32[]{:S(2)}) collective-permute-start(bf16[4,40,768]{2,1,0:T(8,128)(2,1)S(1)} %bitcast_dynamic-update-slice_fusion.4), channel_id=1, source_target_pairs={{0,6},{1,7},{2,4},{3,5},{4,2},{5,3},{6,0},{7,1},{8,14},{9,15},{10,... | collective-permute-start | bytes 737288 | tf_op jit(solution)/shard_map/ppermute | solution.py:27
  30.7 41.8 %collective-permute-start.4 = (bf16[4,40,768]{2,1,0:T(8,128)(2,1)S(1)}, bf16[4,40,768]{2,1,0:T(8,128)(2,1)S(1)}, u32[]{:S(2)}, u32[]{:S(2)}) collective-permute-start(bf16[4,40,768]{2,1,0:T(8,128)(2,1)S(1)} %bitcast_dynamic-update-slice_fusion.4), channel_id=1, source_target_pairs={{0,4},{1,5},{2,6},{3,7},{4,0},{5,1},{6,2},{7,3},{8,12},{9,13},{10,... | collective-permute-start | bytes 737288 | tf_op jit(solution)/shard_map/ppermute | solution.py:27
  72.6 10.7 %collective-permute-start.6 = (bf16[4,4,40,768]{3,2,0,1:T(8,128)(2,1)S(1)}, bf16[4,4,40,768]{3,2,0,1:T(8,128)(2,1)S(1)}, u32[]{:S(2)}, u32[]{:S(2)}) collective-permute-start(bf16[4,4,40,768]{3,2,0,1:T(8,128)(2,1)S(1)} %bitcast_dynamic-update-slice_fusion.3), channel_id=1, source_target_pairs={{0,1},{1,0},{2,3},{3,2},{4,5},{5,4},{6,7},{7,6},{8,9},{9,8},{10,11... | collective-permute-start | bytes 2949128 | tf_op jit(solution)/shard_map/ppermute | solution.py:27
  77.4 42.6 %all-to-all-start.2 = ((bf16[4,256,1024]{2,1,0:T(8,128)(2,1)}), bf16[4,256,1024]{2,1,0:T(8,128)(2,1)}, u32[]{:S(2)}, u32[]{:S(2)}) async-start(bf16[4,256,1024]{2,1,0:T(8,128)(2,1)} %broadcast_in_dim.100), calls=%async_computation.2 | async-start | bytes 4194304 | tf_op jit(solution)/shard_map/all_to_all | solution.py:109
  120.0 21.3 %all-to-all-start.1 = ((bf16[4,256,256]{2,1,0:T(8,128)(2,1)}), bf16[4,256,256]{2,1,0:T(8,128)(2,1)}, u32[]{:S(2)}, u32[]{:S(2)}) async-start(bf16[4,256,256]{2,1,0:T(8,128)(2,1)} %get-tuple-element.38), calls=%async_computation.1 | async-start | bytes 1048576 | tf_op jit(solution)/shard_map/all_to_all | solution.py:109
  124.1 333.7 %reduce-scatter.2.cloned.1.call-start = ((), (), s32[]{:S(2)}) async-start(), calls=%async_computation.11 | async-start | bytes 8912896 | tf_op jit(solution)/shard_map/reduce_scatter | solution.py:373
  168.3 3.5 collective-permute-start.8
  196.3 4.5 collective-permute-start.10
  245.6 4.5 collective-permute-start.12
  267.1 18.2 %all-to-all-start.4 = ((bf16[4,256,256]{2,1,0:T(8,128)(2,1)}), bf16[4,256,256]{2,1,0:T(8,128)(2,1)}, u32[]{:S(2)}, u32[]{:S(2)}) async-start(bf16[4,256,256]{2,1,0:T(8,128)(2,1)} %bitcast.224), calls=%async_computation.4 | async-start | bytes 1048576 | tf_op jit(solution)/shard_map/all_to_all | solution.py:109
  285.4 30.7 %all-to-all-start.5 = ((bf16[4,256,256]{2,1,0:T(8,128)(2,1)}), bf16[4,256,256]{2,1,0:T(8,128)(2,1)}, u32[]{:S(2)}, u32[]{:S(2)}) async-start(bf16[4,256,256]{2,1,0:T(8,128)(2,1)} %bitcast.223), calls=%async_computation.5 | async-start | bytes 1048576 | tf_op jit(solution)/shard_map/all_to_all | solution.py:109
  316.1 54.1 %all-to-all-start.6 = ((bf16[4,256,1024]{2,1,0:T(8,128)(2,1)}), bf16[4,256,1024]{2,1,0:T(8,128)(2,1)}, u32[]{:S(2)}, u32[]{:S(2)}) async-start(bf16[4,256,1024]{2,1,0:T(8,128)(2,1)} %bitcast.230), calls=%async_computation.6 | async-start | bytes 4194304 | tf_op jit(solution)/shard_map/all_to_all | solution.py:109
  323.0 27.9 %collective-permute-start.17 = (bf16[4,4,32,1024]{3,2,1,0:T(8,128)(2,1)}, bf16[4,4,32,1024]{3,2,1,0:T(8,128)(2,1)}, u32[]{:S(2)}, u32[]{:S(2)}) collective-permute-start(bf16[4,4,32,1024]{3,2,1,0:T(8,128)(2,1)} %dynamic-slice_bitcast_fusion), channel_id=1, source_target_pairs={{0,1},{1,0},{2,3},{3,2},{4,5},{5,4},{6,7},{7,6},{8,9},{9,8},{10,11... | collective-permute-start | bytes 3145736 | tf_op jit(solution)/shard_map/ppermute | solution.py:27
  353.6 31.2 %collective-permute-start.20 = (bf16[4,32,1024]{2,1,0:T(8,128)(2,1)}, bf16[4,32,1024]{2,1,0:T(8,128)(2,1)}, u32[]{:S(2)}, u32[]{:S(2)}) collective-permute-start(bf16[4,32,1024]{2,1,0:T(8,128)(2,1)} %get-tuple-element.168), channel_id=1, source_target_pairs={{0,24},{8,16},{16,8},{24,0},{1,25},{9,17},{17,9},{25,1},{2,26},{10... | collective-permute-start | bytes 786440 | tf_op jit(solution)/shard_map/ppermute | solution.py:27
  356.2 35.4 %collective-permute-start.19 = (bf16[4,32,1024]{2,1,0:T(8,128)(2,1)}, bf16[4,32,1024]{2,1,0:T(8,128)(2,1)}, u32[]{:S(2)}, u32[]{:S(2)}) collective-permute-start(bf16[4,32,1024]{2,1,0:T(8,128)(2,1)} %get-tuple-element.169), channel_id=1, source_target_pairs={{0,16},{8,24},{16,0},{24,8},{1,17},{9,25},{17,1},{25,9},{2,18},{10... | collective-permute-start | bytes 786440 | tf_op jit(solution)/shard_map/ppermute | solution.py:27
  356.4 35.1 %collective-permute-start.18 = (bf16[4,32,1024]{2,1,0:T(8,128)(2,1)}, bf16[4,32,1024]{2,1,0:T(8,128)(2,1)}, u32[]{:S(2)}, u32[]{:S(2)}) collective-permute-start(bf16[4,32,1024]{2,1,0:T(8,128)(2,1)} %get-tuple-element.170), channel_id=1, source_target_pairs={{0,8},{8,0},{16,24},{24,16},{1,9},{9,1},{17,25},{25,17},{2,10},{10... | collective-permute-start | bytes 786440 | tf_op jit(solution)/shard_map/ppermute | solution.py:27
  373.4 61.1 %all-to-all-start.7 = ((bf16[4,256,1024]{2,1,0:T(8,128)(2,1)}), bf16[4,256,1024]{2,1,0:T(8,128)(2,1)}, u32[]{:S(2)}, u32[]{:S(2)}) async-start(bf16[4,256,1024]{2,1,0:T(8,128)(2,1)} %bitcast.229), calls=%async_computation.7 | async-start | bytes 4194304 | tf_op jit(solution)/shard_map/all_to_all | solution.py:109
  382.8 15.6 %collective-permute-start.13 = (bf16[4,4,32,768]{3,2,0,1:T(8,128)(2,1)S(1)}, bf16[4,4,32,768]{3,2,0,1:T(8,128)(2,1)}, u32[]{:S(2)}, u32[]{:S(2)}) collective-permute-start(bf16[4,4,32,768]{3,2,0,1:T(8,128)(2,1)S(1)} %bitcast.246), channel_id=1, source_target_pairs={{0,1},{1,0},{2,3},{3,2},{4,5},{5,4},{6,7},{7,6},{8,9},{9,8},{10,11... | collective-permute-start | bytes 2359304 | tf_op jit(solution)/shard_map/ppermute | solution.py:27
  393.5 8.6 %collective-permute-start.21 = (bf16[32,1024]{1,0:T(8,128)(2,1)}, bf16[32,1024]{1,0:T(8,128)(2,1)S(1)}, u32[]{:S(2)}, u32[]{:S(2)}) collective-permute-start(bf16[32,1024]{1,0:T(8,128)(2,1)} %get-tuple-element.192), channel_id=1, source_target_pairs={{0,2},{1,3},{2,0},{3,1},{4,6},{5,7},{6,4},{7,5},{8,10},{9,11},{10,... | collective-permute-start | bytes 196616 | tf_op jit(solution)/shard_map/ppermute | solution.py:27
  393.5 9.0 %collective-permute-start.23 = (bf16[32,1024]{1,0:T(8,128)(2,1)S(1)}, bf16[32,1024]{1,0:T(8,128)(2,1)S(1)}, u32[]{:S(2)}, u32[]{:S(2)}) collective-permute-start(bf16[32,1024]{1,0:T(8,128)(2,1)S(1)} %get-tuple-element.193), channel_id=1, source_target_pairs={{0,6},{1,7},{2,4},{3,5},{4,2},{5,3},{6,0},{7,1},{8,14},{9,15},{10,... | collective-permute-start | bytes 196616 | tf_op jit(solution)/shard_map/ppermute | solution.py:27
  393.5 14.8 %collective-permute-start.22 = (bf16[32,1024]{1,0:T(8,128)(2,1)S(1)}, bf16[32,1024]{1,0:T(8,128)(2,1)}, u32[]{:S(2)}, u32[]{:S(2)}) collective-permute-start(bf16[32,1024]{1,0:T(8,128)(2,1)S(1)} %get-tuple-element.194), channel_id=1, source_target_pairs={{0,4},{1,5},{2,6},{3,7},{4,0},{5,1},{6,2},{7,3},{8,12},{9,13},{10,... | collective-permute-start | bytes 196616 | tf_op jit(solution)/shard_map/ppermute | solution.py:27
  399.8 16.0 %collective-permute-start.14 = (bf16[4,32,768]{2,1,0:T(8,128)(2,1)S(1)}, bf16[4,32,768]{2,1,0:T(8,128)(2,1)S(1)}, u32[]{:S(2)}, u32[]{:S(2)}) collective-permute-start(bf16[4,32,768]{2,1,0:T(8,128)(2,1)S(1)} %get-tuple-element.176), channel_id=1, source_target_pairs={{0,2},{1,3},{2,0},{3,1},{4,6},{5,7},{6,4},{7,5},{8,10},{9,11},{10,... | collective-permute-start | bytes 589832 | tf_op jit(solution)/shard_map/ppermute | solution.py:27
  400.7 19.2 %collective-permute-start.16 = (bf16[4,32,768]{2,1,0:T(8,128)(2,1)S(1)}, bf16[4,32,768]{2,1,0:T(8,128)(2,1)S(1)}, u32[]{:S(2)}, u32[]{:S(2)}) collective-permute-start(bf16[4,32,768]{2,1,0:T(8,128)(2,1)S(1)} %get-tuple-element.177), channel_id=1, source_target_pairs={{0,6},{1,7},{2,4},{3,5},{4,2},{5,3},{6,0},{7,1},{8,14},{9,15},{10,... | collective-permute-start | bytes 589832 | tf_op jit(solution)/shard_map/ppermute | solution.py:27
  402.1 31.6 %collective-permute-start.15 = (bf16[4,32,768]{2,1,0:T(8,128)(2,1)S(1)}, bf16[4,32,768]{2,1,0:T(8,128)(2,1)S(1)}, u32[]{:S(2)}, u32[]{:S(2)}) collective-permute-start(bf16[4,32,768]{2,1,0:T(8,128)(2,1)S(1)} %get-tuple-element.178), channel_id=1, source_target_pairs={{0,4},{1,5},{2,6},{3,7},{4,0},{5,1},{6,2},{7,3},{8,12},{9,13},{10,... | collective-permute-start | bytes 589832 | tf_op jit(solution)/shard_map/ppermute | solution.py:27
  435.2 11.6 %all-to-all-start.9 = ((f32[32,1,384]{2,1,0:T(1,128)}), f32[32,1,384]{2,1,0:T(1,128)S(1)}, u32[]{:S(2)}, u32[]{:S(2)}) async-start(f32[32,1,384]{2,1,0:T(1,128)} %all_to_all.42), calls=%async_computation.9 | async-start | bytes 98304 | tf_op jit(solution)/shard_map/all_to_all | solution.py:430
  447.4 9.8 %all-to-all-start.8 = ((f32[4,32,768]{2,1,0:T(8,128)}), f32[4,32,768]{2,1,0:T(8,128)S(1)}, u32[]{:S(2)}, u32[]{:S(2)}) async-start(f32[4,32,768]{2,1,0:T(8,128)} %fusion.32), calls=%async_computation.8 | async-start | bytes 786432 | tf_op jit(solution)/shard_map/all_to_all | solution.py:109
  459.2 3.2 collective-permute-start.24
  (56 other events, 339.7 us)
Sparse Core Ops, SparseCore 0:
  12.7 152.7 all-gather.2
  235.4 197.4 reduce-scatter.1

commit v3 on v2

--- a/solution.py
+++ b/solution.py
@@ -45,6 +45,11 @@
 
 def core_groups():
     n = lax.axis_size("fsdp") * lax.axis_size("ctx")
+    return [list(range(k, n, 2)) for k in range(2)]
+
+
+def z_groups():
+    n = lax.axis_size("fsdp")
     return [list(range(k, n, 2)) for k in range(2)]
 
 
@@ -309,7 +314,7 @@
     give = lax.dynamic_index_in_dim(split, 1 - core, 2, False).reshape(rows_w, half)
     up_mine = in_order(keep, core_swap(give), core, 0).reshape(2 * rows_w, half)
     parts = half // width
-    own = jnp.concatenate([up_mine[:, j * width : (j + 1) * width] for j in range(parts)] + [w_down, w_out])
+    own = jnp.concatenate([up_mine[:, j * width : (j + 1) * width] for j in range(parts)] + [w_down])
     own = lax.all_gather(own, BOTH, axis=0, axis_index_groups=core_groups())
 
     key_pos = jnp.arange(length, dtype=jnp.int32)
@@ -332,6 +337,9 @@
         outs.append(o)
         lses.append(lse)
         mixed.append(exchange_ctx(o if g == 0 else after(o, mixed[-1])))
+    out_c = send_ctx([place(gather_z(after(w_out, outs[0])), me_z)] * nc)
+    out_mat = place(after(out_c, outs[-1]), me_c)
+    out_mat = in_order(out_mat, core_swap(out_mat), core, 2).reshape(width, width)
     own = after(own, mixed[-1])
     mixed = jnp.concatenate([t.reshape(width, ctx_rows) for t in mixed], axis=1)
     n_up = 2 * rows_w * parts
@@ -339,9 +347,6 @@
         [own[:, j * 2 * rows_w : (j + 1) * 2 * rows_w].reshape(width, width) for j in range(parts)], axis=1
     )
     down_mat = own[:, n_up : n_up + ff_w].reshape(half, width)
-    out_mine = own[:, n_up + ff_w :]
-    out_mat = in_order(out_mine, core_swap(out_mine), core, 1).reshape(width, width)
-
     inputs = mine.reshape(flat_rows, width).astype(F32)
     attended = dot(mixed, out_mat, 0, 0) + out_bias
     first, normed_one, inverse_one = norm_forward(inputs + attended, gain_one, bias_one)
@@ -351,8 +356,8 @@
     cdf = 0.5 * (1.0 + lax.erf(hidden * 0.7071067811865476))
     slope = (cdf + hidden * jnp.exp(-0.5 * hidden * hidden) * 0.3989422804014327).astype(BF)
     activated = (hidden * cdf).astype(BF)
-    part = dot(activated, down_mat, 1, 0)
-    branch = part[:flat_rows] + core_swap(part[flat_rows:]) + down_bias
+    away = core_swap(dot(activated[flat_rows:], down_mat, 1, 0).astype(BF))
+    branch = dot(activated[:flat_rows], down_mat, 1, 0) + away.astype(F32) + down_bias
     result, normed_two, inverse_two = norm_forward(first + branch, gain_two, bias_two)
     output = result.astype(BF).reshape(micro, per_device, ctx_rows, width)
 
@@ -362,32 +367,29 @@
     grad_down_bias = jnp.sum(grad_branch.astype(F32), axis=0)
     both_branch = jnp.concatenate([grad_branch, core_swap(grad_branch)])
     grad_down = dot(activated, both_branch, 0, 0).astype(BF)
+    both_branch = lax.optimization_barrier((both_branch, grad_down))[0]
+    grad_down = lax.psum_scatter(grad_down, "ctx", scatter_dimension=0, tiled=True)
     grad_hidden = (dot(both_branch, down_mat, 1, 1) * slope.astype(F32)).astype(BF)
-    grad_up_bias = jnp.sum(grad_hidden.astype(F32), axis=0)
+    grad_up_bias = dot(jnp.ones((8, grad_hidden.shape[0]), BF), grad_hidden, 1, 0)[0]
     grad_ups = [
         dot(both_first, grad_hidden[:, j * width : (j + 1) * width], 0, 0).astype(BF) for j in range(parts)
     ]
-    grad_ffn = jnp.concatenate(
-        [t.reshape(nc * nz, 2 * rows_w, width) for t in grad_ups] + [grad_down.reshape(nc * nz, ff_w, width)], axis=1
-    )
-    grad_ffn = lax.psum_scatter(grad_ffn, BOTH, scatter_dimension=0, axis_index_groups=core_groups()).astype(F32)
-    grad_down = grad_ffn[n_up:]
-    part = dot(grad_hidden, up_mat, 1, 1)
-    grad_first = part[:flat_rows] + core_swap(part[flat_rows:]) + grad_h2
+    away = core_swap(dot(grad_hidden[flat_rows:], up_mat, 1, 1).astype(BF))
+    grad_first = dot(grad_hidden[:flat_rows], up_mat, 1, 1) + away.astype(F32) + grad_h2
     grad_h1, grad_gain_one, grad_bias_one = norm_backward(grad_first, normed_one, inverse_one, gain_one)
     grad_attended = grad_h1.astype(BF)
     grad_out_bias = jnp.sum(grad_attended.astype(F32), axis=0)
-    grad_mixed = dot(out_mat, grad_attended, 1, 1).astype(BF)
-    grad_mixed = grad_mixed.reshape(nc, cols, groups, ctx_rows)
     dos = []
     for g in range(groups):
-        do = grad_mixed[:, :, g]
+        do = dot(out_mat, grad_attended[g * ctx_rows : (g + 1) * ctx_rows], 1, 1).astype(BF)
+        do = do.reshape(nc, cols, ctx_rows)
         dos.append(exchange_ctx(do if g == 0 else after(do, dos[0])))
     grad_out = dot(mixed, grad_attended, 1, 0).astype(BF).reshape(nc, nz, 2, rows_w, width)
     grad_out_got = core_swap(lax.dynamic_index_in_dim(grad_out, 1 - core, 2, False))
     grad_out = lax.dynamic_index_in_dim(grad_out, core, 2, False).astype(F32) + grad_out_got.astype(F32)
-    grad_out = after(grad_out.astype(BF), dos[0])
-    out_raw = send_ctx([pick(grad_out, me ^ r) for r in range(nc)])
+    mats = [t.reshape(nc, nz, 2 * rows_w, width) for t in grad_ups] + [grad_out.astype(BF)]
+    grad_up = jnp.concatenate(mats, axis=2).reshape(nc, nz * (n_up + rows_w), width)
+    grad_up = lax.psum_scatter(grad_up, "ctx", scatter_dimension=0).reshape(nz, n_up + rows_w, width)
 
     backs = []
     grad_qkv = None
@@ -395,12 +397,17 @@
     for g in range(groups):
         dqkv = attend_back(qkvs[g], dos[g], 0, lses[g], segs[g], ctx_rows)
         if g == 1:
-            dqkv, backs[0] = lax.optimization_barrier((dqkv, backs[0]))
+            dqkv, backs[0], down_got = lax.optimization_barrier((dqkv, backs[0], down_got))
         grad_bias_parts.append(jnp.sum(dqkv.astype(F32), axis=1))
         back = dot(dqkv, w_qkv, 0, 1).astype(BF).reshape(nc, ctx_rows, width)
         if g + 1 < groups:
+            grad_down = after(grad_down, dqkv).reshape(nz, ff_w, width)
+            down_got = z_send(grad_down)
             qkvs[g + 1] = after(qkvs[g + 1], back)
-        backs.append(exchange_ctx(back))
+        if g + 1 < groups:
+            backs.append(exchange_ctx(back))
+        else:
+            backs.append(send_ctx([pick(back, me ^ r) for r in range(nc)]))
         now = dot(inputs_all[g], dqkv, 0, 1)
         grad_qkv = now if grad_qkv is None else grad_qkv + now
     grad_bias = sum(grad_bias_parts).reshape(3, cols)
@@ -422,17 +429,19 @@
     small = jnp.concatenate(small, axis=1)
     grad_qkv = grad_qkv.astype(BF).reshape(nc, nz, 2, rows_w, 3 * cols)
     grad_qkv_got = core_swap(lax.dynamic_index_in_dim(grad_qkv, 1 - core, 2, False))
-    grad_out = total_of(after(out_raw, dqkv)).astype(BF)
-    out_got = z_send(grad_out)
     grad_qkv = lax.dynamic_index_in_dim(grad_qkv, core, 2, False).astype(F32) + grad_qkv_got.astype(F32)
     grad_qkv = jnp.moveaxis(grad_qkv.astype(BF), 1, 0)
+    small = jnp.sum(lax.all_to_all(after(small, grad_qkv), BOTH, 0, 0), axis=0)
+    up_got = z_send(after(grad_up, grad_qkv))
     grad_qkv = z_sum(grad_qkv, z_send(grad_qkv))
-    small = jnp.sum(lax.all_to_all(after(small, backs[-1]), BOTH, 0, 0), axis=0)
-    grad_qkv = exchange_ctx(after(grad_qkv, backs[-1])).reshape(nc, rows_w, 3, cols)
+    backs_last = after(backs[-1], grad_qkv)
+    grad_qkv = exchange_ctx(grad_qkv).reshape(nc, rows_w, 3, cols)
     grad_qkv = jnp.moveaxis(grad_qkv, 0, 2).reshape(rows_w, 3, width)
-    input_grads = [jnp.sum(t.astype(F32), axis=0) for t in backs]
-    grad_out = z_sum(grad_out, out_got)
-    grad_up = [grad_ffn[j * 2 * rows_w : (j + 1) * 2 * rows_w] for j in range(parts)]
+    input_grads = [total_of([t[r] for r in range(nc)]) for t in backs[:-1] + [backs_last]]
+    grad_down = z_sum(grad_down, down_got)
+    grad_up = z_sum(grad_up, up_got)
+    grad_out = grad_up[n_up:]
+    grad_up = [grad_up[j * 2 * rows_w : (j + 1) * 2 * rows_w] for j in range(parts)]
     grad_up = jnp.concatenate(grad_up, axis=1).reshape(2, rows_w, half)
     grad_up_got = core_swap(lax.dynamic_index_in_dim(grad_up, 1 - core, 0, False))
     pair = [

time: 482 us -> 437 us (0.907)
  the two profiles are of different devices: /device:TPU:1 before, /device:TPU:13 now
where the time goes in v3:
time: 437 us; the launch traced here: 431 us
  matrix products  88.6 us (20%)
  waiting for transfers between devices  87.4 us (20%)
  starting transfers between devices  73.8 us (17%)
  Pallas kernels  66.6 us (15%)
  local copies, waits for them, and re-layouts  47.1 us (11%)
  other arithmetic  36.4 us (8%)
  blocking collectives  15.8 us (4%)
  between operations  15.5 us (4%)
    dot_general x20, matrix products, dot(): lax.dot_general(a, b, (((ca,), (cb,)), ((), ())), preferred_element_type=...  88.6 us
    ppermute x34, waiting for transfers between devices, swap(): return lax.ppermute(x, axis, [(i, i ^ r) for i in range(n)])  69.9 us
    pallas_call x2, Pallas kernels, attend_back(): pl.pallas_call(functools.partial(attend_back_kernel, heads, nq, block), g...  42.3 us
    all_to_all x7, starting transfers between devices, exchange_ctx(): return lax.all_to_all(x, 'ctx', 0, 0)  33.3 us
    ppermute x34, starting transfers between devices, swap(): return lax.ppermute(x, axis, [(i, i ^ r) for i in range(n)])  32.9 us
    pallas_call x2, Pallas kernels, attend(): pl.pallas_call(attend_kernel, grid=(heads, nq), in_specs=[pl.BlockSpec((H...  24.3 us
    all_to_all x1, blocking collectives, exchange_ctx(): return lax.all_to_all(x, 'ctx', 0, 0)  15.8 us
    all_to_all x7, waiting for transfers between devices, exchange_ctx(): return lax.all_to_all(x, 'ctx', 0, 0)  9.73 us
  transfers between devices with their start and end apart: 45, of which 21 were waited for; matrix products, arithmetic and copies ran while one was open for 29% of the time, Pallas kernels for 15%

profile of v3, /device:TPU:13, one launch (start us, length us, event | category | flops | bytes accessed | tf_op | source)
XLA Modules:
  0.0 431.1 jit_solution(10330118278374600152)
XLA Ops:
  25.1 5.5 %all-to-all-start = ((bf16[4,256,1024]{2,1,0:T(8,128)(2,1)}), bf16[4,256,1024]{2,1,0:T(8,128)(2,1)}, u32[]{:S(2)}, u32[]{:S(2)}) async-start(bf16[4,256,1024]{2,1,0:T(8,128)(2,1)} %broadcast_in_dim.133), calls=%async_computation | async-start | bytes 4194304 | tf_op jit(solution)/shard_map/all_to_all | solution.py:114
  30.8 19.1 %collective-permute-done.4 = bf16[4,40,768]{2,1,0:T(8,128)(2,1)S(1)} collective-permute-done((bf16[4,40,768]{2,1,0:T(8,128)(2,1)S(1)}, bf16[4,40,768]{2,1,0:T(8,128)(2,1)S(1)}, u32[]{:S(2)}, u32[]{:S(2)}) %collective-permute-start.4) | collective-permute-done | bytes 245792 | tf_op jit(solution)/shard_map/ppermute | solution.py:27
  49.9 5.9 %collective-permute-done.5 = bf16[4,40,768]{2,1,0:T(8,128)(2,1)S(1)} collective-permute-done((bf16[4,40,768]{2,1,0:T(8,128)(2,1)S(1)}, bf16[4,40,768]{2,1,0:T(8,128)(2,1)S(1)}, u32[]{:S(2)}, u32[]{:S(2)}) %collective-permute-start.5) | collective-permute-done | bytes 245792 | tf_op jit(solution)/shard_map/ppermute | solution.py:27
  65.4 5.7 %all-to-all-start.2 = ((bf16[4,256,1024]{2,1,0:T(8,128)(2,1)}), bf16[4,256,1024]{2,1,0:T(8,128)(2,1)}, u32[]{:S(2)}, u32[]{:S(2)}) async-start(bf16[4,256,1024]{2,1,0:T(8,128)(2,1)} %broadcast_in_dim.135), calls=%async_computation.2 | async-start | bytes 4194304 | tf_op jit(solution)/shard_map/all_to_all | solution.py:114
  73.0 4.0 add_convert_fusion.2.q_ref.k_ref.v_ref
  77.0 12.1 %attend.2 = (bf16[4,256,256]{2,1,0:T(8,128)(2,1)S(1)}, f32[4,1,1024]{2,1,0:T(1,128)S(1)}) custom-call(bf16[768,1024]{1,0:T(8,128)(2,1)S(1)} %add_convert_fusion.2.q_ref.k_ref.v_ref, bf16[768,1024]{1,0:T(8,128)(2,1)S(1)} %add_convert_fusion.2.q_ref.k_ref.v_ref, bf16[768,1024]{1,0:T(8,128)(2,1)S(1)} %add_convert_fusion.2.q_ref.k_ref.v_ref, ...), custom_call_target="tpu_custom_call" | custom-call | flops 1048576 | bytes 1048576 | tf_op jit(solution)/shard_map/attend/pallas_call | solution.py:134
  101.1 4.2 add_convert_fusion.1.q_ref.k_ref.v_ref
  105.3 12.2 %attend.3 = (bf16[4,256,256]{2,1,0:T(8,128)(2,1)S(1)}, f32[4,1,1024]{2,1,0:T(1,128)S(1)}) custom-call(bf16[768,1024]{1,0:T(8,128)(2,1)S(1)} %add_convert_fusion.1.q_ref.k_ref.v_ref, bf16[768,1024]{1,0:T(8,128)(2,1)S(1)} %add_convert_fusion.1.q_ref.k_ref.v_ref, bf16[768,1024]{1,0:T(8,128)(2,1)S(1)} %add_convert_fusion.1.q_ref.k_ref.v_ref, ...), custom_call_target="tpu_custom_call" | custom-call | flops 1048576 | bytes 1048576 | tf_op jit(solution)/shard_map/attend/pallas_call | solution.py:134
  117.5 6.0 %collective-permute-done.12 = bf16[4,32,1024]{2,1,0:T(8,128)(2,1)} collective-permute-done((bf16[4,32,1024]{2,1,0:T(8,128)(2,1)S(1)}, bf16[4,32,1024]{2,1,0:T(8,128)(2,1)}, u32[]{:S(2)}, u32[]{:S(2)}) %collective-permute-start.12) | collective-permute-done | bytes 262176 | tf_op jit(solution)/shard_map/ppermute | solution.py:27
  132.2 15.8 %all_to_all.49 = bf16[4,256,256]{2,1,0:T(8,128)(2,1)} all-to-all(bf16[4,256,256]{2,1,0:T(8,128)(2,1)S(1)} %copy-done.7), channel_id=1, replica_groups=mesh['ctx'=4,'fsdp'=8] {'ctx'}, dimensions={0} | all-to-all | bytes 1048576 | tf_op jit(solution)/shard_map/all_to_all | solution.py:114
  148.0 5.0 %all-to-all-start.3 = ((bf16[4,256,256]{2,1,0:T(8,128)(2,1)}), bf16[4,256,256]{2,1,0:T(8,128)(2,1)}, u32[]{:S(2)}, u32[]{:S(2)}) async-start(bf16[4,256,256]{2,1,0:T(8,128)(2,1)} %copy-done.8), calls=%async_computation.3 | async-start | bytes 1048576 | tf_op jit(solution)/shard_map/all_to_all | solution.py:114
  153.2 3.9 maximum_select_fusion
  160.4 3.5 fusion.78
  173.3 11.2 %multiply_convert_fusion.1 = (bf16[1024,2048]{1,0:T(8,128)(2,1)S(1)}, f32[1024,2048]{1,0:T(8,128)}) fusion(f32[2048]{0:T(1024)S(1)} %bitcast.287, bf16[1024,1024]{1,0:T(8,128)(2,1)S(1)} %bitcast.260, bf16[1024,1024]{1,0:T(8,128)(2,1)S(1)} %bitcast.257, bf16[512,1024]{1,0:T(8,128)(2,1)} %collective-permute-done.14, bf16[512,1024]{1,0:T(8,128)(2,1)} %fusion.32), kind=kOutput, calls=%fused_computation.7 | convolution fusion | flops 4320133120 | bytes 18882560 | tf_op jit(solution)/shard_map/dot_general | solution.py:22
  190.8 6.5 %fusion.73 = (f32[512]{0:T(512)S(1)}, f32[512,1024]{1,0:T(8,128)S(1)}) fusion(f32[1024]{0:T(1024)S(1)} %reshape.567, bf16[512,1024]{1,0:T(8,128)(2,1)} %collective-permute-done.16, f32[1024]{0:T(1024)S(1)} %reshape.565, f32[1024]{0:T(1024)S(1)} %reshape.564, f32[512]{0:T(512)S(1)} %add_rsqrt_fusion.1, f32[512,1024]{1,0:T(8,128)} %copy-done.9, ...), kind=kOutput, calls=%fused_computation.198 | convolution fusion | flops 2152201728 | bytes 11552768 | tf_op jit(solution)/shard_map/dot_general | solution.py:22
  205.6 6.3 %convolution_convert_fusion = bf16[2048,1024]{1,0:T(8,128)(2,1)} fusion(bf16[1024,2048]{1,0:T(8,128)(2,1)S(1)} %copy-done.48, bf16[512,1024]{1,0:T(8,128)(2,1)S(1)} %collective-permute-done.17, bf16[512,1024]{1,0:T(8,128)(2,1)S(1)} %get-tuple-element.171), kind=kOutput, calls=%fused_computation.11 | convolution fusion | flops 4301258752 | bytes 10485760 | tf_op jit(solution)/shard_map/dot_general | solution.py:22
  214.8 9.5 %multiply_convert_fusion = bf16[1024,2048]{1,0:T(8,128)(2,1)S(1)} fusion(f32[1024,2048]{1,0:T(8,128)} %get-tuple-element.236, f32[2048]{0:T(1024)S(1)} %bitcast.288, bf16[1024,1024]{1,0:T(8,128)(2,1)S(1)} %pad_maximum_fusion.3, bf16[2048,1024]{1,0:T(8,128)(2,1)S(1)} %bitcast.244), kind=kOutput, calls=%fused_computation.6 | convolution fusion | flops 4322230272 | bytes 18882560 | tf_op jit(solution)/shard_map/dot_general | solution.py:22
  237.7 3.9 fusion.26
  241.6 4.0 fusion.29
  252.8 4.4 %all-to-all-start.4 = ((bf16[4,256,256]{2,1,0:T(8,128)(2,1)}), bf16[4,256,256]{2,1,0:T(8,128)(2,1)}, u32[]{:S(2)}, u32[]{:S(2)}) async-start(bf16[4,256,256]{2,1,0:T(8,128)(2,1)} %bitcast.279), calls=%async_computation.4 | async-start | bytes 1048576 | tf_op jit(solution)/shard_map/all_to_all | solution.py:114
  260.4 6.4 %all-to-all-done.4.do_ref = bf16[4,256,256]{2,1,0:T(8,128)(2,1)} async-done(((bf16[4,256,256]{2,1,0:T(8,128)(2,1)}), bf16[4,256,256]{2,1,0:T(8,128)(2,1)}, u32[]{:S(2)}, u32[]{:S(2)}) %all-to-all-start.4) | async-done | bytes 524320 | tf_op jit(solution)/shard_map/all_to_all | solution.py:114
  266.8 4.4 %all-to-all-start.5 = ((bf16[4,256,256]{2,1,0:T(8,128)(2,1)}), bf16[4,256,256]{2,1,0:T(8,128)(2,1)}, u32[]{:S(2)}, u32[]{:S(2)}) async-start(bf16[4,256,256]{2,1,0:T(8,128)(2,1)} %bitcast.278), calls=%async_computation.5 | async-start | bytes 1048576 | tf_op jit(solution)/shard_map/all_to_all | solution.py:114
  272.2 21.2 %attend_back.2 = bf16[768,1024]{1,0:T(8,128)(2,1)S(1)} custom-call(bf16[768,1024]{1,0:T(8,128)(2,1)S(1)} %add_convert_fusion.2.q_ref.k_ref.v_ref, bf16[768,1024]{1,0:T(8,128)(2,1)S(1)} %add_convert_fusion.2.q_ref.k_ref.v_ref, bf16[768,1024]{1,0:T(8,128)(2,1)S(1)} %add_convert_fusion.2.q_ref.k_ref.v_ref, bf16[4,256,256]{2,1,0:T(8,128)(2,1)} %all-to-all-done.4.do_ref, ...), custom_call_target="tpu_custom_call" | custom-call | flops 1048576 | bytes 1048576 | tf_op jit(solution)/shard_map/attend_back/pallas_call | solution.py:202
  297.7 4.5 %all-to-all-start.6 = ((bf16[4,256,1024]{2,1,0:T(8,128)(2,1)}), bf16[4,256,1024]{2,1,0:T(8,128)(2,1)}, u32[]{:S(2)}, u32[]{:S(2)}) async-start(bf16[4,256,1024]{2,1,0:T(8,128)(2,1)} %bitcast.255), calls=%async_computation.6 | async-start | bytes 4194304 | tf_op jit(solution)/shard_map/all_to_all | solution.py:114
  310.3 5.2 %fusion.81 = f32[1024,768]{1,0:T(8,128)} fusion(bf16[1024,1024]{1,0:T(8,128)(2,1)} %bitcast.20, bf16[768,1024]{1,0:T(8,128)(2,1)S(1)} %copy-done.1), kind=kOutput, calls=%fused_computation.204 | convolution fusion | flops 1610612736 | bytes 6815744 | tf_op jit(solution)/shard_map/dot_general | solution.py:22
  315.7 21.1 %attend_back.3 = bf16[768,1024]{1,0:T(8,128)(2,1)S(1)} custom-call(bf16[768,1024]{1,0:T(8,128)(2,1)S(1)} %add_convert_fusion.1.q_ref.k_ref.v_ref, bf16[768,1024]{1,0:T(8,128)(2,1)S(1)} %add_convert_fusion.1.q_ref.k_ref.v_ref, bf16[768,1024]{1,0:T(8,128)(2,1)S(1)} %add_convert_fusion.1.q_ref.k_ref.v_ref, bf16[4,256,256]{2,1,0:T(8,128)(2,1)} %all-to-all-done.5.do_ref, ...), custom_call_target="tpu_custom_call" | custom-call | flops 1048576 | bytes 1048576 | tf_op jit(solution)/shard_map/attend_back/pallas_call | solution.py:202
  336.9 4.5 %add_convert_fusion = bf16[1024,768]{1,0:T(8,128)(2,1)S(1)} fusion(f32[1024,768]{1,0:T(8,128)} %fusion.81, bf16[1024,1024]{1,0:T(8,128)(2,1)} %bitcast.28, bf16[768,1024]{1,0:T(8,128)(2,1)S(1)} %attend_back.3), kind=kOutput, calls=%fused_computation.14 | convolution fusion | flops 1612185600 | bytes 8388608 | tf_op jit(solution)/shard_map/dot_general | solution.py:22
  357.7 7.4 %all-to-all-start.8 = ((f32[32,1,384]{2,1,0:T(1,128)}), f32[32,1,384]{2,1,0:T(1,128)S(1)}, u32[]{:S(2)}, u32[]{:S(2)}) async-start(f32[32,1,384]{2,1,0:T(1,128)} %copy.117), calls=%async_computation.9 | async-start | bytes 98304 | tf_op jit(solution)/shard_map/all_to_all | solution.py:434
  368.3 7.7 %all-to-all-done.8 = f32[32,1,384]{2,1,0:T(1,128)S(1)} async-done(((f32[32,1,384]{2,1,0:T(1,128)}), f32[32,1,384]{2,1,0:T(1,128)S(1)}, u32[]{:S(2)}, u32[]{:S(2)}) %all-to-all-start.8) | async-done | bytes 49184 | tf_op jit(solution)/shard_map/all_to_all | solution.py:434
  389.6 3.7 all-to-all-start.7
  395.6 10.8 %collective-permute-done.31 = bf16[160,1024]{1,0:T(8,128)(2,1)} collective-permute-done((bf16[160,1024]{1,0:T(8,128)(2,1)S(1)}, bf16[160,1024]{1,0:T(8,128)(2,1)}, u32[]{:S(2)}, u32[]{:S(2)}) %collective-permute-start.31) | collective-permute-done | bytes 327712 | tf_op jit(solution)/shard_map/ppermute | solution.py:27
  406.5 8.3 %collective-permute-done.32 = bf16[160,1024]{1,0:T(8,128)(2,1)} collective-permute-done((bf16[160,1024]{1,0:T(8,128)(2,1)S(1)}, bf16[160,1024]{1,0:T(8,128)(2,1)}, u32[]{:S(2)}, u32[]{:S(2)}) %collective-permute-start.32) | collective-permute-done | bytes 327712 | tf_op jit(solution)/shard_map/ppermute | solution.py:27
  (323 shorter events, 161.6 us)
Async XLA Ops:
  7.2 160.7 %all-gather.3.cloned.1.call-start = ((), (), s32[]{:S(2)}) async-start(), calls=%async_computation.12 | async-start | bytes 8912896 | tf_op jit(solution)/shard_map/all_gather | solution.py:318
  19.9 10.8 %collective-permute-start.3 = (bf16[4,40,768]{2,1,0:T(8,128)(2,1)S(1)}, bf16[4,40,768]{2,1,0:T(8,128)(2,1)S(1)}, u32[]{:S(2)}, u32[]{:S(2)}) collective-permute-start(bf16[4,40,768]{2,1,0:T(8,128)(2,1)S(1)} %bitcast_dynamic-update-slice_fusion.12), channel_id=1, source_target_pairs={{0,2},{1,3},{2,0},{3,1},{4,6},{5,7},{6,4},{7,5},{8,10},{9,11},{10,... | collective-permute-start | bytes 737288 | tf_op jit(solution)/shard_map/ppermute | solution.py:27
  21.0 28.9 %collective-permute-start.4 = (bf16[4,40,768]{2,1,0:T(8,128)(2,1)S(1)}, bf16[4,40,768]{2,1,0:T(8,128)(2,1)S(1)}, u32[]{:S(2)}, u32[]{:S(2)}) collective-permute-start(bf16[4,40,768]{2,1,0:T(8,128)(2,1)S(1)} %bitcast_dynamic-update-slice_fusion.12), channel_id=1, source_target_pairs={{0,4},{1,5},{2,6},{3,7},{4,0},{5,1},{6,2},{7,3},{8,12},{9,13},{10,... | collective-permute-start | bytes 737288 | tf_op jit(solution)/shard_map/ppermute | solution.py:27
  23.3 32.5 %collective-permute-start.5 = (bf16[4,40,768]{2,1,0:T(8,128)(2,1)S(1)}, bf16[4,40,768]{2,1,0:T(8,128)(2,1)S(1)}, u32[]{:S(2)}, u32[]{:S(2)}) collective-permute-start(bf16[4,40,768]{2,1,0:T(8,128)(2,1)S(1)} %bitcast_dynamic-update-slice_fusion.12), channel_id=1, source_target_pairs={{0,6},{1,7},{2,4},{3,5},{4,2},{5,3},{6,0},{7,1},{8,14},{9,15},{10,... | collective-permute-start | bytes 737288 | tf_op jit(solution)/shard_map/ppermute | solution.py:27
  25.1 37.5 %all-to-all-start = ((bf16[4,256,1024]{2,1,0:T(8,128)(2,1)}), bf16[4,256,1024]{2,1,0:T(8,128)(2,1)}, u32[]{:S(2)}, u32[]{:S(2)}) async-start(bf16[4,256,1024]{2,1,0:T(8,128)(2,1)} %broadcast_in_dim.133), calls=%async_computation | async-start | bytes 4194304 | tf_op jit(solution)/shard_map/all_to_all | solution.py:114
  65.4 35.7 %all-to-all-start.2 = ((bf16[4,256,1024]{2,1,0:T(8,128)(2,1)}), bf16[4,256,1024]{2,1,0:T(8,128)(2,1)}, u32[]{:S(2)}, u32[]{:S(2)}) async-start(bf16[4,256,1024]{2,1,0:T(8,128)(2,1)} %broadcast_in_dim.135), calls=%async_computation.2 | async-start | bytes 4194304 | tf_op jit(solution)/shard_map/all_to_all | solution.py:114
  98.4 19.1 %collective-permute-start.10 = (bf16[4,32,1024]{2,1,0:T(8,128)(2,1)S(1)}, bf16[4,32,1024]{2,1,0:T(8,128)(2,1)}, u32[]{:S(2)}, u32[]{:S(2)}) collective-permute-start(bf16[4,32,1024]{2,1,0:T(8,128)(2,1)S(1)} %bitcast_dynamic-update-slice_fusion.8), channel_id=1, source_target_pairs={{0,8},{8,0},{16,24},{24,16},{1,9},{9,1},{17,25},{25,17},{2,10},{10... | collective-permute-start | bytes 786440 | tf_op jit(solution)/shard_map/ppermute | solution.py:27
  99.5 18.0 %collective-permute-start.11 = (bf16[4,32,1024]{2,1,0:T(8,128)(2,1)S(1)}, bf16[4,32,1024]{2,1,0:T(8,128)(2,1)}, u32[]{:S(2)}, u32[]{:S(2)}) collective-permute-start(bf16[4,32,1024]{2,1,0:T(8,128)(2,1)S(1)} %bitcast_dynamic-update-slice_fusion.8), channel_id=1, source_target_pairs={{0,16},{8,24},{16,0},{24,8},{1,17},{9,25},{17,1},{25,9},{2,18},{10... | collective-permute-start | bytes 786440 | tf_op jit(solution)/shard_map/ppermute | solution.py:27
  99.9 23.6 %collective-permute-start.12 = (bf16[4,32,1024]{2,1,0:T(8,128)(2,1)S(1)}, bf16[4,32,1024]{2,1,0:T(8,128)(2,1)}, u32[]{:S(2)}, u32[]{:S(2)}) collective-permute-start(bf16[4,32,1024]{2,1,0:T(8,128)(2,1)S(1)} %bitcast_dynamic-update-slice_fusion.8), channel_id=1, source_target_pairs={{0,24},{8,16},{16,8},{24,0},{1,25},{9,17},{17,9},{25,1},{2,26},{10... | collective-permute-start | bytes 786440 | tf_op jit(solution)/shard_map/ppermute | solution.py:27
  130.3 22.9 %collective-permute-start.13 = (bf16[4,4,32,1024]{3,2,1,0:T(8,128)(2,1)}, bf16[4,4,32,1024]{3,2,1,0:T(8,128)(2,1)}, u32[]{:S(2)}, u32[]{:S(2)}) collective-permute-start(bf16[4,4,32,1024]{3,2,1,0:T(8,128)(2,1)} %bitcast_dynamic-update-slice_fusion), channel_id=1, source_target_pairs={{0,1},{1,0},{2,3},{3,2},{4,5},{5,4},{6,7},{7,6},{8,9},{9,8},{10,11... | collective-permute-start | bytes 3145736 | tf_op jit(solution)/shard_map/ppermute | solution.py:27
  148.0 12.5 %all-to-all-start.3 = ((bf16[4,256,256]{2,1,0:T(8,128)(2,1)}), bf16[4,256,256]{2,1,0:T(8,128)(2,1)}, u32[]{:S(2)}, u32[]{:S(2)}) async-start(bf16[4,256,256]{2,1,0:T(8,128)(2,1)} %copy-done.8), calls=%async_computation.3 | async-start | bytes 1048576 | tf_op jit(solution)/shard_map/all_to_all | solution.py:114
  153.0 152.7 %reduce-scatter.5.cloned.1.call-start = ((), (), s32[]{:S(2)}) async-start(), calls=%async_computation.11 | async-start | bytes 5242880 | tf_op jit(solution)/shard_map/reduce_scatter | solution.py:371
  211.9 166.6 %reduce-scatter.7.cloned.1.call-start = ((), (), s32[]{:S(2)}) async-start(), calls=%async_computation.13 | async-start | bytes 6553600
  237.4 8.2 %collective-permute-start.29 = (bf16[4,4,32,1024]{3,2,1,0:T(8,128)(2,1)S(1)}, bf16[4,4,32,1024]{3,2,1,0:T(8,128)(2,1)S(1)}, u32[]{:S(2)}, u32[]{:S(2)}) collective-permute-start(bf16[4,4,32,1024]{3,2,1,0:T(8,128)(2,1)S(1)} %dynamic-slice_bitcast_fusion), channel_id=1, source_target_pairs={{0,1},{1,0},{2,3},{3,2},{4,5},{5,4},{6,7},{7,6},{8,9},{9,8},{10,11... | collective-permute-start | bytes 3145736 | tf_op jit(solution)/shard_map/ppermute | solution.py:27
  252.8 14.0 %all-to-all-start.4 = ((bf16[4,256,256]{2,1,0:T(8,128)(2,1)}), bf16[4,256,256]{2,1,0:T(8,128)(2,1)}, u32[]{:S(2)}, u32[]{:S(2)}) async-start(bf16[4,256,256]{2,1,0:T(8,128)(2,1)} %bitcast.279), calls=%async_computation.4 | async-start | bytes 1048576 | tf_op jit(solution)/shard_map/all_to_all | solution.py:114
  266.8 30.9 %all-to-all-start.5 = ((bf16[4,256,256]{2,1,0:T(8,128)(2,1)}), bf16[4,256,256]{2,1,0:T(8,128)(2,1)}, u32[]{:S(2)}, u32[]{:S(2)}) async-start(bf16[4,256,256]{2,1,0:T(8,128)(2,1)} %bitcast.278), calls=%async_computation.5 | async-start | bytes 1048576 | tf_op jit(solution)/shard_map/all_to_all | solution.py:114
  297.7 39.1 %all-to-all-start.6 = ((bf16[4,256,1024]{2,1,0:T(8,128)(2,1)}), bf16[4,256,1024]{2,1,0:T(8,128)(2,1)}, u32[]{:S(2)}, u32[]{:S(2)}) async-start(bf16[4,256,1024]{2,1,0:T(8,128)(2,1)} %bitcast.255), calls=%async_computation.6 | async-start | bytes 4194304 | tf_op jit(solution)/shard_map/all_to_all | solution.py:114
  307.6 29.2 %collective-permute-start.19 = (bf16[128,1024]{1,0:T(8,128)(2,1)}, bf16[128,1024]{1,0:T(8,128)(2,1)}, u32[]{:S(2)}, u32[]{:S(2)}) collective-permute-start(bf16[128,1024]{1,0:T(8,128)(2,1)} %get-tuple-element.192), channel_id=1, source_target_pairs={{0,2},{1,3},{2,0},{3,1},{4,6},{5,7},{6,4},{7,5},{8,10},{9,11},{10,... | collective-permute-start | bytes 786440 | tf_op jit(solution)/shard_map/ppermute | solution.py:27
  307.9 29.0 %collective-permute-start.20 = (bf16[128,1024]{1,0:T(8,128)(2,1)}, bf16[128,1024]{1,0:T(8,128)(2,1)}, u32[]{:S(2)}, u32[]{:S(2)}) collective-permute-start(bf16[128,1024]{1,0:T(8,128)(2,1)} %get-tuple-element.191), channel_id=1, source_target_pairs={{0,4},{1,5},{2,6},{3,7},{4,0},{5,1},{6,2},{7,3},{8,12},{9,13},{10,... | collective-permute-start | bytes 786440 | tf_op jit(solution)/shard_map/ppermute | solution.py:27
  310.0 26.9 %collective-permute-start.21 = (bf16[128,1024]{1,0:T(8,128)(2,1)S(1)}, bf16[128,1024]{1,0:T(8,128)(2,1)}, u32[]{:S(2)}, u32[]{:S(2)}) collective-permute-start(bf16[128,1024]{1,0:T(8,128)(2,1)S(1)} %get-tuple-element.190), channel_id=1, source_target_pairs={{0,6},{1,7},{2,4},{3,5},{4,2},{5,3},{6,0},{7,1},{8,14},{9,15},{10,... | collective-permute-start | bytes 786440 | tf_op jit(solution)/shard_map/ppermute | solution.py:27
  343.3 12.4 %collective-permute-start.25 = (bf16[4,4,32,768]{3,2,0,1:T(8,128)(2,1)}, bf16[4,4,32,768]{3,2,0,1:T(8,128)(2,1)}, u32[]{:S(2)}, u32[]{:S(2)}) collective-permute-start(bf16[4,4,32,768]{3,2,0,1:T(8,128)(2,1)} %bitcast.227), channel_id=1, source_target_pairs={{0,1},{1,0},{2,3},{3,2},{4,5},{5,4},{6,7},{7,6},{8,9},{9,8},{10,11... | collective-permute-start | bytes 2359304 | tf_op jit(solution)/shard_map/ppermute | solution.py:27
  348.8 27.3 %collective-permute-start.22 = (bf16[256,1024]{1,0:T(8,128)(2,1)}, bf16[256,1024]{1,0:T(8,128)(2,1)}, u32[]{:S(2)}, u32[]{:S(2)}) collective-permute-start(bf16[256,1024]{1,0:T(8,128)(2,1)} %get-tuple-element.183), channel_id=1, source_target_pairs={{0,8},{8,0},{16,24},{24,16},{1,9},{9,1},{17,25},{25,17},{2,10},{10... | collective-permute-start | bytes 1572872 | tf_op jit(solution)/shard_map/ppermute | solution.py:27
  350.1 43.2 %collective-permute-start.23 = (bf16[256,1024]{1,0:T(8,128)(2,1)}, bf16[256,1024]{1,0:T(8,128)(2,1)}, u32[]{:S(2)}, u32[]{:S(2)}) collective-permute-start(bf16[256,1024]{1,0:T(8,128)(2,1)} %get-tuple-element.182), channel_id=1, source_target_pairs={{0,16},{8,24},{16,0},{24,8},{1,17},{9,25},{17,1},{25,9},{2,18},{10... | collective-permute-start | bytes 1572872 | tf_op jit(solution)/shard_map/ppermute | solution.py:27
  350.2 43.1 %collective-permute-start.24 = (bf16[256,1024]{1,0:T(8,128)(2,1)}, bf16[256,1024]{1,0:T(8,128)(2,1)}, u32[]{:S(2)}, u32[]{:S(2)}) collective-permute-start(bf16[256,1024]{1,0:T(8,128)(2,1)} %get-tuple-element.181), channel_id=1, source_target_pairs={{0,24},{8,16},{16,8},{24,0},{1,25},{9,17},{17,9},{25,1},{2,26},{10... | collective-permute-start | bytes 1572872 | tf_op jit(solution)/shard_map/ppermute | solution.py:27
  357.7 18.3 %all-to-all-start.8 = ((f32[32,1,384]{2,1,0:T(1,128)}), f32[32,1,384]{2,1,0:T(1,128)S(1)}, u32[]{:S(2)}, u32[]{:S(2)}) async-start(f32[32,1,384]{2,1,0:T(1,128)} %copy.117), calls=%async_computation.9 | async-start | bytes 98304 | tf_op jit(solution)/shard_map/all_to_all | solution.py:434
  366.0 14.6 %collective-permute-start.26 = (bf16[4,32,768]{2,1,0:T(8,128)(2,1)}, bf16[4,32,768]{2,1,0:T(8,128)(2,1)}, u32[]{:S(2)}, u32[]{:S(2)}) collective-permute-start(bf16[4,32,768]{2,1,0:T(8,128)(2,1)} %get-tuple-element.195), channel_id=1, source_target_pairs={{0,2},{1,3},{2,0},{3,1},{4,6},{5,7},{6,4},{7,5},{8,10},{9,11},{10,... | collective-permute-start | bytes 589832 | tf_op jit(solution)/shard_map/ppermute | solution.py:27
  366.2 17.4 %collective-permute-start.27 = (bf16[4,32,768]{2,1,0:T(8,128)(2,1)S(1)}, bf16[4,32,768]{2,1,0:T(8,128)(2,1)}, u32[]{:S(2)}, u32[]{:S(2)}) collective-permute-start(bf16[4,32,768]{2,1,0:T(8,128)(2,1)S(1)} %get-tuple-element.197), channel_id=1, source_target_pairs={{0,4},{1,5},{2,6},{3,7},{4,0},{5,1},{6,2},{7,3},{8,12},{9,13},{10,... | collective-permute-start | bytes 589832 | tf_op jit(solution)/shard_map/ppermute | solution.py:27
  376.1 10.5 %collective-permute-start.28 = (bf16[4,32,768]{2,1,0:T(8,128)(2,1)S(1)}, bf16[4,32,768]{2,1,0:T(8,128)(2,1)}, u32[]{:S(2)}, u32[]{:S(2)}) collective-permute-start(bf16[4,32,768]{2,1,0:T(8,128)(2,1)S(1)} %get-tuple-element.196), channel_id=1, source_target_pairs={{0,6},{1,7},{2,4},{3,5},{4,2},{5,3},{6,0},{7,1},{8,14},{9,15},{10,... | collective-permute-start | bytes 589832 | tf_op jit(solution)/shard_map/ppermute | solution.py:27
  380.5 15.1 %collective-permute-start.30 = (bf16[160,1024]{1,0:T(8,128)(2,1)}, bf16[160,1024]{1,0:T(8,128)(2,1)}, u32[]{:S(2)}, u32[]{:S(2)}) collective-permute-start(bf16[160,1024]{1,0:T(8,128)(2,1)} %get-tuple-element.187), channel_id=1, source_target_pairs={{0,2},{1,3},{2,0},{3,1},{4,6},{5,7},{6,4},{7,5},{8,10},{9,11},{10,... | collective-permute-start | bytes 983048 | tf_op jit(solution)/shard_map/ppermute | solution.py:27
  383.6 22.9 %collective-permute-start.31 = (bf16[160,1024]{1,0:T(8,128)(2,1)S(1)}, bf16[160,1024]{1,0:T(8,128)(2,1)}, u32[]{:S(2)}, u32[]{:S(2)}) collective-permute-start(bf16[160,1024]{1,0:T(8,128)(2,1)S(1)} %get-tuple-element.189), channel_id=1, source_target_pairs={{0,4},{1,5},{2,6},{3,7},{4,0},{5,1},{6,2},{7,3},{8,12},{9,13},{10,... | collective-permute-start | bytes 983048 | tf_op jit(solution)/shard_map/ppermute | solution.py:27
  386.6 28.1 %collective-permute-start.32 = (bf16[160,1024]{1,0:T(8,128)(2,1)S(1)}, bf16[160,1024]{1,0:T(8,128)(2,1)}, u32[]{:S(2)}, u32[]{:S(2)}) collective-permute-start(bf16[160,1024]{1,0:T(8,128)(2,1)S(1)} %get-tuple-element.188), channel_id=1, source_target_pairs={{0,6},{1,7},{2,4},{3,5},{4,2},{5,3},{6,0},{7,1},{8,14},{9,15},{10,... | collective-permute-start | bytes 983048 | tf_op jit(solution)/shard_map/ppermute | solution.py:27
  389.6 29.8 %all-to-all-start.7 = ((f32[4,32,768]{2,1,0:T(8,128)}), f32[4,32,768]{2,1,0:T(8,128)S(1)}, u32[]{:S(2)}, u32[]{:S(2)}) async-start(f32[4,32,768]{2,1,0:T(8,128)} %fusion.50), calls=%async_computation.8 | async-start | bytes 786432 | tf_op jit(solution)/shard_map/all_to_all | solution.py:114
  (62 other events, 379.4 us)
Sparse Core Ops, SparseCore 0:
  12.9 150.8 all-gather.2
  212.0 53.6 reduce-scatter.4
  269.0 76.5 reduce-scatter.6

commit v4 on v3

--- a/solution.py
+++ b/solution.py
@@ -160,38 +160,34 @@
 
 
 def attend_back_kernel(
-    heads, nq, block, q_ref, k_ref, v_ref, do_ref, lse_ref, srow_ref, scol_ref, out_ref, dk_ref, dv_ref
+    heads, nq, block, q_ref, k_ref, v_ref, do_ref, lse_ref, srow_ref, scol_ref, out_ref, dk_ref, dv_ref, kt_ref, vt_ref
 ):
     h = pl.program_id(0)
     i = pl.program_id(1)
+
+    @pl.when(i == 0)
+    def _():
+        kt_ref[...] = k_ref[...].T
+        vt_ref[...] = v_ref[...].T
+        dk_ref[...] = jnp.zeros_like(dk_ref)
+        dv_ref[...] = jnp.zeros_like(dv_ref)
+
     q = q_ref[...] * jnp.asarray(SCORE_SCALE, BF)
-    k = k_ref[...]
     do = do_ref[0]
-    s = dot(k, q, 0, 0)
-    p = jnp.exp(s - lse_ref[0])
+    p = jnp.exp(dot(kt_ref[...], q, 1, 0) - lse_ref[0])
     p = jnp.where(scol_ref[...] == srow_ref[...], p, 0.0)
-    dp = dot(v_ref[...], do, 0, 0)
+    dp = dot(vt_ref[...], do, 1, 0)
     central = jnp.sum(p * dp, axis=0, keepdims=True)
     ds = (p * (dp - central)).astype(BF)
-    dq = dot(k, ds, 1, 0) * SCORE_SCALE
-    dk = dot(q, ds, 1, 1)
-    dv = dot(do, p.astype(BF), 1, 1)
+    dq = dot(k_ref[...], ds, 1, 0) * SCORE_SCALE
     out_ref[pl.ds(pl.multiple_of(h * HD, HD), HD), pl.ds(pl.multiple_of(i * block, block), block)] = dq.astype(BF)
-
-    @pl.when(i == 0)
-    def _():
-        dk_ref[...] = dk
-        dv_ref[...] = dv
-
-    @pl.when(i > 0)
-    def _():
-        dk_ref[...] += dk
-        dv_ref[...] += dv
+    dk_ref[...] += dot(ds, q.T, 1, 0)
+    dv_ref[...] += dot(p.astype(BF), do.T, 1, 0)
 
     @pl.when(i == nq - 1)
     def _():
-        out_ref[pl.ds(pl.multiple_of((heads + h) * HD, HD), HD), :] = dk_ref[...].astype(BF)
-        out_ref[pl.ds(pl.multiple_of((2 * heads + h) * HD, HD), HD), :] = dv_ref[...].astype(BF)
+        out_ref[pl.ds(pl.multiple_of((heads + h) * HD, HD), HD), :] = dk_ref[...].T.astype(BF)
+        out_ref[pl.ds(pl.multiple_of((2 * heads + h) * HD, HD), HD), :] = dv_ref[...].T.astype(BF)
 
 
 def attend_back(qkv, do, group, lse, seg, block):
@@ -213,7 +209,7 @@
         ],
         out_specs=pl.BlockSpec((rows, length), lambda h, i: (0, 0)),
         out_shape=jax.ShapeDtypeStruct((rows, length), BF),
-        scratch_shapes=[pltpu.VMEM((HD, length), F32), pltpu.VMEM((HD, length), F32)],
+        scratch_shapes=[pltpu.VMEM((length, HD), F32)] * 2 + [pltpu.VMEM((length, HD), BF)] * 2,
         compiler_params=pltpu.CompilerParams(vmem_limit_bytes=VMEM_LIMIT),
         cost_estimate=pl.CostEstimate(
             flops=1 << 20,
@@ -371,9 +367,6 @@
     grad_down = lax.psum_scatter(grad_down, "ctx", scatter_dimension=0, tiled=True)
     grad_hidden = (dot(both_branch, down_mat, 1, 1) * slope.astype(F32)).astype(BF)
     grad_up_bias = dot(jnp.ones((8, grad_hidden.shape[0]), BF), grad_hidden, 1, 0)[0]
-    grad_ups = [
-        dot(both_first, grad_hidden[:, j * width : (j + 1) * width], 0, 0).astype(BF) for j in range(parts)
-    ]
     away = core_swap(dot(grad_hidden[flat_rows:], up_mat, 1, 1).astype(BF))
     grad_first = dot(grad_hidden[:flat_rows], up_mat, 1, 1) + away.astype(F32) + grad_h2
     grad_h1, grad_gain_one, grad_bias_one = norm_backward(grad_first, normed_one, inverse_one, gain_one)
@@ -382,9 +375,14 @@
     dos = []
     for g in range(groups):
         do = dot(out_mat, grad_attended[g * ctx_rows : (g + 1) * ctx_rows], 1, 1).astype(BF)
-        do = do.reshape(nc, cols, ctx_rows)
-        dos.append(exchange_ctx(do if g == 0 else after(do, dos[0])))
-    grad_out = dot(mixed, grad_attended, 1, 0).astype(BF).reshape(nc, nz, 2, rows_w, width)
+        dos.append(do.reshape(nc, cols, ctx_rows))
+    for g in range(groups):
+        dos[g] = exchange_ctx(dos[g] if g == 0 else after(dos[g], dos[0]))
+    later = after((both_first, grad_hidden, mixed, grad_attended), dos[0])
+    grad_out = dot(later[2], later[3], 1, 0).astype(BF).reshape(nc, nz, 2, rows_w, width)
+    grad_ups = [
+        dot(later[0], later[1][:, j * width : (j + 1) * width], 0, 0).astype(BF) for j in range(parts)
+    ]
     grad_out_got = core_swap(lax.dynamic_index_in_dim(grad_out, 1 - core, 2, False))
     grad_out = lax.dynamic_index_in_dim(grad_out, core, 2, False).astype(F32) + grad_out_got.astype(F32)
     mats = [t.reshape(nc, nz, 2 * rows_w, width) for t in grad_ups] + [grad_out.astype(BF)]
@@ -427,19 +425,22 @@
     pair = [jnp.where(core == j, grad_up_bias, 0.0) for j in range(2)]
     small.append(jnp.stack(pair, axis=1).reshape(nc * nf, ff_w))
     small = jnp.concatenate(small, axis=1)
+    small = jnp.pad(small, ((0, 0), (0, 8 * 3 * cols - small.shape[1]))).astype(BF)
+    small = small.reshape(nc, nz, 2, 8, 3 * cols)
     grad_qkv = grad_qkv.astype(BF).reshape(nc, nz, 2, rows_w, 3 * cols)
+    grad_qkv = jnp.concatenate([grad_qkv, small], axis=3)
     grad_qkv_got = core_swap(lax.dynamic_index_in_dim(grad_qkv, 1 - core, 2, False))
     grad_qkv = lax.dynamic_index_in_dim(grad_qkv, core, 2, False).astype(F32) + grad_qkv_got.astype(F32)
     grad_qkv = jnp.moveaxis(grad_qkv.astype(BF), 1, 0)
-    small = jnp.sum(lax.all_to_all(after(small, grad_qkv), BOTH, 0, 0), axis=0)
-    up_got = z_send(after(grad_up, grad_qkv))
-    grad_qkv = z_sum(grad_qkv, z_send(grad_qkv))
-    backs_last = after(backs[-1], grad_qkv)
-    grad_qkv = exchange_ctx(grad_qkv).reshape(nc, rows_w, 3, cols)
-    grad_qkv = jnp.moveaxis(grad_qkv, 0, 2).reshape(rows_w, 3, width)
-    input_grads = [total_of([t[r] for r in range(nc)]) for t in backs[:-1] + [backs_last]]
+    grad_qkv = z_sum(grad_qkv, z_send(grad_qkv)).astype(BF)
+    backs[-1] = after(backs[-1], grad_qkv)
+    got = send_ctx([pick(grad_qkv, me ^ r) for r in range(nc)])
+    small = total_of([t[rows_w:] for t in got]).reshape(8 * 3 * cols)
+    grad_qkv = place([t[:rows_w] for t in got], me_c).reshape(nc, rows_w, 3, cols)
+    grad_qkv = jnp.moveaxis(grad_qkv, 0, 2).reshape(rows_w, 3, width).astype(F32)
+    grad_up = lax.psum_scatter(grad_up, "fsdp", scatter_dimension=0, axis_index_groups=z_groups()).astype(F32)
+    input_grads = [total_of([t[r] for r in range(nc)]) for t in backs]
     grad_down = z_sum(grad_down, down_got)
-    grad_up = z_sum(grad_up, up_got)
     grad_out = grad_up[n_up:]
     grad_up = [grad_up[j * 2 * rows_w : (j + 1) * 2 * rows_w] for j in range(parts)]
     grad_up = jnp.concatenate(grad_up, axis=1).reshape(2, rows_w, half)
@@ -454,7 +455,7 @@
 
     small_out = [small[j * rows_w : (j + 1) * rows_w] for j in range(8)]
     g_bq, g_bv, g_bo, g_g1, g_b1, g_bd, g_g2, g_b2 = small_out
-    g_bu = small[8 * rows_w :]
+    g_bu = small[8 * rows_w : 8 * rows_w + ff_w]
 
     return (
         output,

time: 437 us -> 431 us (0.986)
  the two profiles are of different devices: /device:TPU:13 before, /device:TPU:9 now
where the time goes in v4:
time: 431 us; the launch traced here: 425 us
  waiting for transfers between devices  91.2 us (21%)
  matrix products  84 us (19%)
  Pallas kernels  67 us (16%)
  starting transfers between devices  66.2 us (15%)
  local copies, waits for them, and re-layouts  44.1 us (10%)
  other arithmetic  40.6 us (9%)
  blocking collectives  16 us (4%)
  between operations  15.4 us (4%)
    ppermute x34, waiting for transfers between devices, swap(): return lax.ppermute(x, axis, [(i, i ^ r) for i in range(n)])  85.2 us
    dot_general x20, matrix products, dot(): lax.dot_general(a, b, (((ca,), (cb,)), ((), ())), preferred_element_type=...  84 us
    pallas_call x2, Pallas kernels, attend_back(): pl.pallas_call(functools.partial(attend_back_kernel, heads, nq, block), g...  42.7 us
    ppermute x34, starting transfers between devices, swap(): return lax.ppermute(x, axis, [(i, i ^ r) for i in range(n)])  39.6 us
    all_to_all x6, starting transfers between devices, exchange_ctx(): return lax.all_to_all(x, 'ctx', 0, 0)  26.1 us
    pallas_call x2, Pallas kernels, attend(): pl.pallas_call(attend_kernel, grid=(heads, nq), in_specs=[pl.BlockSpec((H...  24.3 us
    all_to_all x1, blocking collectives, exchange_ctx(): return lax.all_to_all(x, 'ctx', 0, 0)  16 us
    unnamed x111, local copies, waits for them, and re-layouts  10.4 us
  transfers between devices with their start and end apart: 44, of which 21 were waited for; matrix products, arithmetic and copies ran while one was open for 29% of the time, Pallas kernels for 16%

profile of v4, /device:TPU:9, one launch (start us, length us, event | category | flops | bytes accessed | tf_op | source)
XLA Modules:
  0.0 424.5 jit_solution(1523307043289767511)
XLA Ops:
  26.0 4.5 %all-to-all-start = ((bf16[4,256,1024]{2,1,0:T(8,128)(2,1)}), bf16[4,256,1024]{2,1,0:T(8,128)(2,1)}, u32[]{:S(2)}, u32[]{:S(2)}) async-start(bf16[4,256,1024]{2,1,0:T(8,128)(2,1)} %broadcast_in_dim.147), calls=%async_computation | async-start | bytes 4194304 | tf_op jit(solution)/shard_map/all_to_all | solution.py:114
  30.8 8.8 %collective-permute-done.4 = bf16[4,40,768]{2,1,0:T(8,128)(2,1)S(1)} collective-permute-done((bf16[4,40,768]{2,1,0:T(8,128)(2,1)S(1)}, bf16[4,40,768]{2,1,0:T(8,128)(2,1)S(1)}, u32[]{:S(2)}, u32[]{:S(2)}) %collective-permute-start.4) | collective-permute-done | bytes 245792 | tf_op jit(solution)/shard_map/ppermute | solution.py:27
  39.6 17.5 %collective-permute-done.5 = bf16[4,40,768]{2,1,0:T(8,128)(2,1)S(1)} collective-permute-done((bf16[4,40,768]{2,1,0:T(8,128)(2,1)S(1)}, bf16[4,40,768]{2,1,0:T(8,128)(2,1)S(1)}, u32[]{:S(2)}, u32[]{:S(2)}) %collective-permute-start.5) | collective-permute-done | bytes 245792 | tf_op jit(solution)/shard_map/ppermute | solution.py:27
  66.3 4.6 %all-to-all-start.2 = ((bf16[4,256,1024]{2,1,0:T(8,128)(2,1)}), bf16[4,256,1024]{2,1,0:T(8,128)(2,1)}, u32[]{:S(2)}, u32[]{:S(2)}) async-start(bf16[4,256,1024]{2,1,0:T(8,128)(2,1)} %broadcast_in_dim.149), calls=%async_computation.2 | async-start | bytes 4194304 | tf_op jit(solution)/shard_map/all_to_all | solution.py:114
  72.7 4.0 add_convert_fusion.2.q_ref.k_ref.v_ref
  76.7 12.1 %attend.2 = (bf16[4,256,256]{2,1,0:T(8,128)(2,1)S(1)}, f32[4,1,1024]{2,1,0:T(1,128)S(1)}) custom-call(bf16[768,1024]{1,0:T(8,128)(2,1)S(1)} %add_convert_fusion.2.q_ref.k_ref.v_ref, bf16[768,1024]{1,0:T(8,128)(2,1)S(1)} %add_convert_fusion.2.q_ref.k_ref.v_ref, bf16[768,1024]{1,0:T(8,128)(2,1)S(1)} %add_convert_fusion.2.q_ref.k_ref.v_ref, ...), custom_call_target="tpu_custom_call" | custom-call | flops 1048576 | bytes 1048576 | tf_op jit(solution)/shard_map/attend/pallas_call | solution.py:134
  101.7 4.0 add_convert_fusion.1.q_ref.k_ref.v_ref
  105.7 12.2 %attend.3 = (bf16[4,256,256]{2,1,0:T(8,128)(2,1)S(1)}, f32[4,1,1024]{2,1,0:T(1,128)S(1)}) custom-call(bf16[768,1024]{1,0:T(8,128)(2,1)S(1)} %add_convert_fusion.1.q_ref.k_ref.v_ref, bf16[768,1024]{1,0:T(8,128)(2,1)S(1)} %add_convert_fusion.1.q_ref.k_ref.v_ref, bf16[768,1024]{1,0:T(8,128)(2,1)S(1)} %add_convert_fusion.1.q_ref.k_ref.v_ref, ...), custom_call_target="tpu_custom_call" | custom-call | flops 1048576 | bytes 1048576 | tf_op jit(solution)/shard_map/attend/pallas_call | solution.py:134
  118.0 4.2 collective-permute-done.12
  128.9 3.6 collective-permute-start.13
  132.6 16.0 %all_to_all.35 = bf16[4,256,256]{2,1,0:T(8,128)(2,1)} all-to-all(bf16[4,256,256]{2,1,0:T(8,128)(2,1)S(1)} %copy-done.7), channel_id=1, replica_groups=mesh['ctx'=4,'fsdp'=8] {'ctx'}, dimensions={0} | all-to-all | bytes 1048576 | tf_op jit(solution)/shard_map/all_to_all | solution.py:114
  148.6 4.1 all-to-all-start.3
  153.0 4.0 maximum_select_fusion
  157.0 3.4 all-to-all-done.3
  160.4 3.5 fusion.84
  173.3 10.9 %multiply_convert_fusion.1 = (bf16[1024,2048]{1,0:T(8,128)(2,1)S(1)}, f32[1024,2048]{1,0:T(8,128)}) fusion(f32[2048]{0:T(1024)S(1)} %bitcast.307, bf16[1024,1024]{1,0:T(8,128)(2,1)S(1)} %bitcast.280, bf16[1024,1024]{1,0:T(8,128)(2,1)S(1)} %bitcast.277, bf16[512,1024]{1,0:T(8,128)(2,1)} %collective-permute-done.14, bf16[512,1024]{1,0:T(8,128)(2,1)} %fusion.33), kind=kOutput, calls=%fused_computation.7 | convolution fusion | flops 4320133120 | bytes 18882560 | tf_op jit(solution)/shard_map/dot_general | solution.py:22
  184.2 3.3 fusion.34
  190.6 6.5 %fusion.80 = (f32[512]{0:T(512)S(1)}, f32[512,1024]{1,0:T(8,128)S(1)}) fusion(f32[1024]{0:T(1024)S(1)} %reshape.589, bf16[512,1024]{1,0:T(8,128)(2,1)} %collective-permute-done.16, f32[1024]{0:T(1024)S(1)} %reshape.587, f32[1024]{0:T(1024)S(1)} %reshape.586, f32[512]{0:T(512)S(1)} %add_rsqrt_fusion.1, f32[512,1024]{1,0:T(8,128)} %copy-done.9, ...), kind=kOutput, calls=%fused_computation.212 | convolution fusion | flops 2152201728 | bytes 11552768 | tf_op jit(solution)/shard_map/dot_general | solution.py:22
  205.9 6.3 %convolution_convert_fusion = bf16[2048,1024]{1,0:T(8,128)(2,1)} fusion(bf16[1024,2048]{1,0:T(8,128)(2,1)S(1)} %copy-done.52, bf16[512,1024]{1,0:T(8,128)(2,1)S(1)} %collective-permute-done.17, bf16[512,1024]{1,0:T(8,128)(2,1)S(1)} %get-tuple-element.173), kind=kOutput, calls=%fused_computation.11 | convolution fusion | flops 4301258752 | bytes 10485760 | tf_op jit(solution)/shard_map/dot_general | solution.py:22
  215.1 9.7 %multiply_convert_fusion = bf16[1024,2048]{1,0:T(8,128)(2,1)S(1)} fusion(f32[1024,2048]{1,0:T(8,128)} %get-tuple-element.238, f32[2048]{0:T(1024)S(1)} %bitcast.308, bf16[1024,1024]{1,0:T(8,128)(2,1)S(1)} %pad_maximum_fusion.3, bf16[2048,1024]{1,0:T(8,128)(2,1)S(1)} %bitcast.266), kind=kOutput, calls=%fused_computation.6 | convolution fusion | flops 4322230272 | bytes 18882560 | tf_op jit(solution)/shard_map/dot_general | solution.py:22
  236.8 4.1 all-to-all-start.4
  262.0 3.3 convolution_convert_fusion.4
  265.3 4.1 all-to-all-start.5
  270.5 21.4 %attend_back.2 = bf16[768,1024]{1,0:T(8,128)(2,1)S(1)} custom-call(bf16[768,1024]{1,0:T(8,128)(2,1)S(1)} %add_convert_fusion.2.q_ref.k_ref.v_ref, bf16[768,1024]{1,0:T(8,128)(2,1)S(1)} %add_convert_fusion.2.q_ref.k_ref.v_ref, bf16[768,1024]{1,0:T(8,128)(2,1)S(1)} %add_convert_fusion.2.q_ref.k_ref.v_ref, bf16[4,256,256]{2,1,0:T(8,128)(2,1)} %all-to-all-done.4.do_ref, ...), custom_call_target="tpu_custom_call" | custom-call | flops 1048576 | bytes 1048576 | tf_op jit(solution)/shard_map/attend_back/pallas_call | solution.py:198
  296.2 4.6 %all-to-all-start.6 = ((bf16[4,256,1024]{2,1,0:T(8,128)(2,1)}), bf16[4,256,1024]{2,1,0:T(8,128)(2,1)}, u32[]{:S(2)}, u32[]{:S(2)}) async-start(bf16[4,256,1024]{2,1,0:T(8,128)(2,1)} %bitcast.275), calls=%async_computation.6 | async-start | bytes 4194304 | tf_op jit(solution)/shard_map/all_to_all | solution.py:114
  309.4 5.2 %fusion.87 = f32[1024,768]{1,0:T(8,128)} fusion(bf16[1024,1024]{1,0:T(8,128)(2,1)} %bitcast.20, bf16[768,1024]{1,0:T(8,128)(2,1)S(1)} %copy-done.1), kind=kOutput, calls=%fused_computation.217 | convolution fusion | flops 1610612736 | bytes 6815744 | tf_op jit(solution)/shard_map/dot_general | solution.py:22
  314.8 21.3 %attend_back.3 = bf16[768,1024]{1,0:T(8,128)(2,1)S(1)} custom-call(bf16[768,1024]{1,0:T(8,128)(2,1)S(1)} %add_convert_fusion.1.q_ref.k_ref.v_ref, bf16[768,1024]{1,0:T(8,128)(2,1)S(1)} %add_convert_fusion.1.q_ref.k_ref.v_ref, bf16[768,1024]{1,0:T(8,128)(2,1)S(1)} %add_convert_fusion.1.q_ref.k_ref.v_ref, bf16[4,256,256]{2,1,0:T(8,128)(2,1)} %all-to-all-done.5.do_ref, ...), custom_call_target="tpu_custom_call" | custom-call | flops 1048576 | bytes 1048576 | tf_op jit(solution)/shard_map/attend_back/pallas_call | solution.py:198
  337.1 4.4 %add_convert_fusion = bf16[1024,768]{1,0:T(8,128)(2,1)S(1)} fusion(f32[1024,768]{1,0:T(8,128)} %fusion.87, bf16[1024,1024]{1,0:T(8,128)(2,1)} %bitcast.28, bf16[768,1024]{1,0:T(8,128)(2,1)S(1)} %attend_back.3), kind=kOutput, calls=%fused_computation.14 | convolution fusion | flops 1612185600 | bytes 8388608 | tf_op jit(solution)/shard_map/dot_general | solution.py:22
  357.7 4.4 %collective-permute-done.26 = bf16[4,40,768]{2,1,0:T(8,128)(2,1)} collective-permute-done((bf16[4,40,768]{2,1,0:T(8,128)(2,1)}, bf16[4,40,768]{2,1,0:T(8,128)(2,1)}, u32[]{:S(2)}, u32[]{:S(2)}) %collective-permute-start.26) | collective-permute-done | bytes 245792 | tf_op jit(solution)/shard_map/ppermute | solution.py:27
  365.9 3.5 collective-permute-done.27
  369.4 27.3 %collective-permute-done.28 = bf16[4,40,768]{2,1,0:T(8,128)(2,1)S(1)} collective-permute-done((bf16[4,40,768]{2,1,0:T(8,128)(2,1)S(1)}, bf16[4,40,768]{2,1,0:T(8,128)(2,1)S(1)}, u32[]{:S(2)}, u32[]{:S(2)}) %collective-permute-start.28) | collective-permute-done | bytes 245792 | tf_op jit(solution)/shard_map/ppermute | solution.py:27
  406.8 6.6 %collective-permute-start.33 = (f32[32,2048]{1,0:T(8,128)S(1)}, f32[32,2048]{1,0:T(8,128)S(1)}, u32[]{:S(2)}, u32[]{:S(2)}) collective-permute-start(f32[32,2048]{1,0:T(8,128)S(1)} %get-tuple-element.200), channel_id=1, source_target_pairs={{0,1},{1,0},{2,3},{3,2},{4,5},{5,4},{6,7},{7,6},{8,9},{9,8},{10,11... | collective-permute-start | bytes 786440 | tf_op jit(solution)/shard_map/ppermute | solution.py:27
  (342 shorter events, 155.8 us)
Async XLA Ops:
  7.2 160.7 %all-gather.3.cloned.1.call-start = ((), (), s32[]{:S(2)}) async-start(), calls=%async_computation.12 | async-start | bytes 8912896 | tf_op jit(solution)/shard_map/all_gather | solution.py:314
  20.8 10.0 %collective-permute-start.3 = (bf16[4,40,768]{2,1,0:T(8,128)(2,1)S(1)}, bf16[4,40,768]{2,1,0:T(8,128)(2,1)S(1)}, u32[]{:S(2)}, u32[]{:S(2)}) collective-permute-start(bf16[4,40,768]{2,1,0:T(8,128)(2,1)S(1)} %bitcast_dynamic-update-slice_fusion.12), channel_id=1, source_target_pairs={{0,2},{1,3},{2,0},{3,1},{4,6},{5,7},{6,4},{7,5},{8,10},{9,11},{10,... | collective-permute-start | bytes 737288 | tf_op jit(solution)/shard_map/ppermute | solution.py:27
  22.0 17.6 %collective-permute-start.4 = (bf16[4,40,768]{2,1,0:T(8,128)(2,1)S(1)}, bf16[4,40,768]{2,1,0:T(8,128)(2,1)S(1)}, u32[]{:S(2)}, u32[]{:S(2)}) collective-permute-start(bf16[4,40,768]{2,1,0:T(8,128)(2,1)S(1)} %bitcast_dynamic-update-slice_fusion.12), channel_id=1, source_target_pairs={{0,4},{1,5},{2,6},{3,7},{4,0},{5,1},{6,2},{7,3},{8,12},{9,13},{10,... | collective-permute-start | bytes 737288 | tf_op jit(solution)/shard_map/ppermute | solution.py:27
  24.2 32.8 %collective-permute-start.5 = (bf16[4,40,768]{2,1,0:T(8,128)(2,1)S(1)}, bf16[4,40,768]{2,1,0:T(8,128)(2,1)S(1)}, u32[]{:S(2)}, u32[]{:S(2)}) collective-permute-start(bf16[4,40,768]{2,1,0:T(8,128)(2,1)S(1)} %bitcast_dynamic-update-slice_fusion.12), channel_id=1, source_target_pairs={{0,6},{1,7},{2,4},{3,5},{4,2},{5,3},{6,0},{7,1},{8,14},{9,15},{10,... | collective-permute-start | bytes 737288 | tf_op jit(solution)/shard_map/ppermute | solution.py:27
  26.0 37.5 %all-to-all-start = ((bf16[4,256,1024]{2,1,0:T(8,128)(2,1)}), bf16[4,256,1024]{2,1,0:T(8,128)(2,1)}, u32[]{:S(2)}, u32[]{:S(2)}) async-start(bf16[4,256,1024]{2,1,0:T(8,128)(2,1)} %broadcast_in_dim.147), calls=%async_computation | async-start | bytes 4194304 | tf_op jit(solution)/shard_map/all_to_all | solution.py:114
  66.3 35.4 %all-to-all-start.2 = ((bf16[4,256,1024]{2,1,0:T(8,128)(2,1)}), bf16[4,256,1024]{2,1,0:T(8,128)(2,1)}, u32[]{:S(2)}, u32[]{:S(2)}) async-start(bf16[4,256,1024]{2,1,0:T(8,128)(2,1)} %broadcast_in_dim.149), calls=%async_computation.2 | async-start | bytes 4194304 | tf_op jit(solution)/shard_map/all_to_all | solution.py:114
  89.7 6.8 %collective-permute-start.8 = (bf16[32,1024]{1,0:T(8,128)(2,1)S(1)}, bf16[32,1024]{1,0:T(8,128)(2,1)S(1)}, u32[]{:S(2)}, u32[]{:S(2)}) collective-permute-start(bf16[32,1024]{1,0:T(8,128)(2,1)S(1)} %copy-done.40), channel_id=1, source_target_pairs={{0,4},{1,5},{2,6},{3,7},{4,0},{5,1},{6,2},{7,3},{8,12},{9,13},{10,... | collective-permute-start | bytes 196616 | tf_op jit(solution)/shard_map/ppermute | solution.py:27
  91.1 7.9 %collective-permute-start.9 = (bf16[32,1024]{1,0:T(8,128)(2,1)S(1)}, bf16[32,1024]{1,0:T(8,128)(2,1)S(1)}, u32[]{:S(2)}, u32[]{:S(2)}) collective-permute-start(bf16[32,1024]{1,0:T(8,128)(2,1)S(1)} %copy-done.40), channel_id=1, source_target_pairs={{0,6},{1,7},{2,4},{3,5},{4,2},{5,3},{6,0},{7,1},{8,14},{9,15},{10,... | collective-permute-start | bytes 196616 | tf_op jit(solution)/shard_map/ppermute | solution.py:27
  99.0 19.0 %collective-permute-start.10 = (bf16[4,32,1024]{2,1,0:T(8,128)(2,1)S(1)}, bf16[4,32,1024]{2,1,0:T(8,128)(2,1)}, u32[]{:S(2)}, u32[]{:S(2)}) collective-permute-start(bf16[4,32,1024]{2,1,0:T(8,128)(2,1)S(1)} %bitcast_dynamic-update-slice_fusion.8), channel_id=1, source_target_pairs={{0,8},{8,0},{16,24},{24,16},{1,9},{9,1},{17,25},{25,17},{2,10},{10... | collective-permute-start | bytes 786440 | tf_op jit(solution)/shard_map/ppermute | solution.py:27
  99.7 18.3 %collective-permute-start.11 = (bf16[4,32,1024]{2,1,0:T(8,128)(2,1)S(1)}, bf16[4,32,1024]{2,1,0:T(8,128)(2,1)}, u32[]{:S(2)}, u32[]{:S(2)}) collective-permute-start(bf16[4,32,1024]{2,1,0:T(8,128)(2,1)S(1)} %bitcast_dynamic-update-slice_fusion.8), channel_id=1, source_target_pairs={{0,16},{8,24},{16,0},{24,8},{1,17},{9,25},{17,1},{25,9},{2,18},{10... | collective-permute-start | bytes 786440 | tf_op jit(solution)/shard_map/ppermute | solution.py:27
  100.8 21.3 %collective-permute-start.12 = (bf16[4,32,1024]{2,1,0:T(8,128)(2,1)S(1)}, bf16[4,32,1024]{2,1,0:T(8,128)(2,1)}, u32[]{:S(2)}, u32[]{:S(2)}) collective-permute-start(bf16[4,32,1024]{2,1,0:T(8,128)(2,1)S(1)} %bitcast_dynamic-update-slice_fusion.8), channel_id=1, source_target_pairs={{0,24},{8,16},{16,8},{24,0},{1,25},{9,17},{17,9},{25,1},{2,26},{10... | collective-permute-start | bytes 786440 | tf_op jit(solution)/shard_map/ppermute | solution.py:27
  128.9 24.1 %collective-permute-start.13 = (bf16[4,4,32,1024]{3,2,1,0:T(8,128)(2,1)}, bf16[4,4,32,1024]{3,2,1,0:T(8,128)(2,1)}, u32[]{:S(2)}, u32[]{:S(2)}) collective-permute-start(bf16[4,4,32,1024]{3,2,1,0:T(8,128)(2,1)} %bitcast_dynamic-update-slice_fusion), channel_id=1, source_target_pairs={{0,1},{1,0},{2,3},{3,2},{4,5},{5,4},{6,7},{7,6},{8,9},{9,8},{10,11... | collective-permute-start | bytes 3145736 | tf_op jit(solution)/shard_map/ppermute | solution.py:27
  148.6 11.8 %all-to-all-start.3 = ((bf16[4,256,256]{2,1,0:T(8,128)(2,1)}), bf16[4,256,256]{2,1,0:T(8,128)(2,1)}, u32[]{:S(2)}, u32[]{:S(2)}) async-start(bf16[4,256,256]{2,1,0:T(8,128)(2,1)} %copy-done.8), calls=%async_computation.3 | async-start | bytes 1048576 | tf_op jit(solution)/shard_map/all_to_all | solution.py:114
  152.7 152.0 %reduce-scatter.6.cloned.1.call-start = ((), (), s32[]{:S(2)}) async-start(), calls=%async_computation.10 | async-start | bytes 5242880 | tf_op jit(solution)/shard_map/reduce_scatter | solution.py:367
  165.8 7.5 %collective-permute-start.14 = (bf16[512,1024]{1,0:T(8,128)(2,1)}, bf16[512,1024]{1,0:T(8,128)(2,1)}, u32[]{:S(2)}, u32[]{:S(2)}) collective-permute-start(bf16[512,1024]{1,0:T(8,128)(2,1)} %fusion.33), channel_id=1, source_target_pairs={{0,1},{1,0},{2,3},{3,2},{4,5},{5,4},{6,7},{7,6},{8,9},{9,8},{10,11... | collective-permute-start | bytes 3145736 | tf_op jit(solution)/shard_map/ppermute | solution.py:27
  236.8 12.2 %all-to-all-start.4 = ((bf16[4,256,256]{2,1,0:T(8,128)(2,1)}), bf16[4,256,256]{2,1,0:T(8,128)(2,1)}, u32[]{:S(2)}, u32[]{:S(2)}) async-start(bf16[4,256,256]{2,1,0:T(8,128)(2,1)} %bitcast.300), calls=%async_computation.4 | async-start | bytes 1048576 | tf_op jit(solution)/shard_map/all_to_all | solution.py:114
  240.9 113.8 %reduce-scatter.10.cloned.1.call-start = ((), (), s32[]{:S(2)}) async-start(), calls=%async_computation.13 | async-start | bytes 6553600
  252.1 6.3 %collective-permute-start.32 = (bf16[4,4,32,1024]{3,2,1,0:T(8,128)(2,1)S(1)}, bf16[4,4,32,1024]{3,2,1,0:T(8,128)(2,1)S(1)}, u32[]{:S(2)}, u32[]{:S(2)}) collective-permute-start(bf16[4,4,32,1024]{3,2,1,0:T(8,128)(2,1)S(1)} %dynamic-slice_bitcast_fusion), channel_id=1, source_target_pairs={{0,1},{1,0},{2,3},{3,2},{4,5},{5,4},{6,7},{7,6},{8,9},{9,8},{10,11... | collective-permute-start | bytes 3145736 | tf_op jit(solution)/shard_map/ppermute | solution.py:27
  265.3 30.9 %all-to-all-start.5 = ((bf16[4,256,256]{2,1,0:T(8,128)(2,1)}), bf16[4,256,256]{2,1,0:T(8,128)(2,1)}, u32[]{:S(2)}, u32[]{:S(2)}) async-start(bf16[4,256,256]{2,1,0:T(8,128)(2,1)} %bitcast.299), calls=%async_computation.5 | async-start | bytes 1048576 | tf_op jit(solution)/shard_map/all_to_all | solution.py:114
  296.2 39.9 %all-to-all-start.6 = ((bf16[4,256,1024]{2,1,0:T(8,128)(2,1)}), bf16[4,256,1024]{2,1,0:T(8,128)(2,1)}, u32[]{:S(2)}, u32[]{:S(2)}) async-start(bf16[4,256,1024]{2,1,0:T(8,128)(2,1)} %bitcast.275), calls=%async_computation.6 | async-start | bytes 4194304 | tf_op jit(solution)/shard_map/all_to_all | solution.py:114
  300.8 104.9 %reduce-scatter.8.cloned.1.call-start = ((), (), s32[]{:S(2)}) async-start(), calls=%async_computation.11 | async-start | bytes 1638400 | tf_op jit(solution)/shard_map/reduce_scatter | solution.py:441
  306.7 29.4 %collective-permute-start.19 = (bf16[128,1024]{1,0:T(8,128)(2,1)}, bf16[128,1024]{1,0:T(8,128)(2,1)}, u32[]{:S(2)}, u32[]{:S(2)}) collective-permute-start(bf16[128,1024]{1,0:T(8,128)(2,1)} %get-tuple-element.191), channel_id=1, source_target_pairs={{0,2},{1,3},{2,0},{3,1},{4,6},{5,7},{6,4},{7,5},{8,10},{9,11},{10,... | collective-permute-start | bytes 786440 | tf_op jit(solution)/shard_map/ppermute | solution.py:27
  306.8 29.4 %collective-permute-start.20 = (bf16[128,1024]{1,0:T(8,128)(2,1)}, bf16[128,1024]{1,0:T(8,128)(2,1)}, u32[]{:S(2)}, u32[]{:S(2)}) collective-permute-start(bf16[128,1024]{1,0:T(8,128)(2,1)} %get-tuple-element.190), channel_id=1, source_target_pairs={{0,4},{1,5},{2,6},{3,7},{4,0},{5,1},{6,2},{7,3},{8,12},{9,13},{10,... | collective-permute-start | bytes 786440 | tf_op jit(solution)/shard_map/ppermute | solution.py:27
  308.6 27.6 %collective-permute-start.21 = (bf16[128,1024]{1,0:T(8,128)(2,1)S(1)}, bf16[128,1024]{1,0:T(8,128)(2,1)}, u32[]{:S(2)}, u32[]{:S(2)}) collective-permute-start(bf16[128,1024]{1,0:T(8,128)(2,1)S(1)} %get-tuple-element.189), channel_id=1, source_target_pairs={{0,6},{1,7},{2,4},{3,5},{4,2},{5,3},{6,0},{7,1},{8,14},{9,15},{10,... | collective-permute-start | bytes 786440 | tf_op jit(solution)/shard_map/ppermute | solution.py:27
  343.6 8.0 %collective-permute-start.25 = (bf16[4,4,40,768]{3,2,0,1:T(8,128)(2,1)}, bf16[4,4,40,768]{3,2,0,1:T(8,128)(2,1)}, u32[]{:S(2)}, u32[]{:S(2)}) collective-permute-start(bf16[4,4,40,768]{3,2,0,1:T(8,128)(2,1)} %bitcast.247), channel_id=1, source_target_pairs={{0,1},{1,0},{2,3},{3,2},{4,5},{5,4},{6,7},{7,6},{8,9},{9,8},{10,11... | collective-permute-start | bytes 2949128 | tf_op jit(solution)/shard_map/ppermute | solution.py:27
  348.5 51.7 %collective-permute-start.22 = (bf16[256,1024]{1,0:T(8,128)(2,1)}, bf16[256,1024]{1,0:T(8,128)(2,1)S(1)}, u32[]{:S(2)}, u32[]{:S(2)}) collective-permute-start(bf16[256,1024]{1,0:T(8,128)(2,1)} %get-tuple-element.185), channel_id=1, source_target_pairs={{0,8},{8,0},{16,24},{24,16},{1,9},{9,1},{17,25},{25,17},{2,10},{10... | collective-permute-start | bytes 1572872 | tf_op jit(solution)/shard_map/ppermute | solution.py:27
  350.3 50.2 %collective-permute-start.23 = (bf16[256,1024]{1,0:T(8,128)(2,1)}, bf16[256,1024]{1,0:T(8,128)(2,1)S(1)}, u32[]{:S(2)}, u32[]{:S(2)}) collective-permute-start(bf16[256,1024]{1,0:T(8,128)(2,1)} %get-tuple-element.184), channel_id=1, source_target_pairs={{0,16},{8,24},{16,0},{24,8},{1,17},{9,25},{17,1},{25,9},{2,18},{10... | collective-permute-start | bytes 1572872 | tf_op jit(solution)/shard_map/ppermute | solution.py:27
  351.5 49.0 %collective-permute-start.24 = (bf16[256,1024]{1,0:T(8,128)(2,1)}, bf16[256,1024]{1,0:T(8,128)(2,1)S(1)}, u32[]{:S(2)}, u32[]{:S(2)}) collective-permute-start(bf16[256,1024]{1,0:T(8,128)(2,1)} %get-tuple-element.183), channel_id=1, source_target_pairs={{0,24},{8,16},{16,8},{24,0},{1,25},{9,17},{17,9},{25,1},{2,26},{10... | collective-permute-start | bytes 1572872 | tf_op jit(solution)/shard_map/ppermute | solution.py:27
  353.9 8.2 %collective-permute-start.26 = (bf16[4,40,768]{2,1,0:T(8,128)(2,1)}, bf16[4,40,768]{2,1,0:T(8,128)(2,1)}, u32[]{:S(2)}, u32[]{:S(2)}) collective-permute-start(bf16[4,40,768]{2,1,0:T(8,128)(2,1)} %get-tuple-element.194), channel_id=1, source_target_pairs={{0,2},{1,3},{2,0},{3,1},{4,6},{5,7},{6,4},{7,5},{8,10},{9,11},{10,... | collective-permute-start | bytes 737288 | tf_op jit(solution)/shard_map/ppermute | solution.py:27
  356.7 12.7 %collective-permute-start.27 = (bf16[4,40,768]{2,1,0:T(8,128)(2,1)S(1)}, bf16[4,40,768]{2,1,0:T(8,128)(2,1)S(1)}, u32[]{:S(2)}, u32[]{:S(2)}) collective-permute-start(bf16[4,40,768]{2,1,0:T(8,128)(2,1)S(1)} %copy-done.36), channel_id=1, source_target_pairs={{0,4},{1,5},{2,6},{3,7},{4,0},{5,1},{6,2},{7,3},{8,12},{9,13},{10,... | collective-permute-start | bytes 737288 | tf_op jit(solution)/shard_map/ppermute | solution.py:27
  362.1 34.6 %collective-permute-start.28 = (bf16[4,40,768]{2,1,0:T(8,128)(2,1)S(1)}, bf16[4,40,768]{2,1,0:T(8,128)(2,1)S(1)}, u32[]{:S(2)}, u32[]{:S(2)}) collective-permute-start(bf16[4,40,768]{2,1,0:T(8,128)(2,1)S(1)} %get-tuple-element.195), channel_id=1, source_target_pairs={{0,6},{1,7},{2,4},{3,5},{4,2},{5,3},{6,0},{7,1},{8,14},{9,15},{10,... | collective-permute-start | bytes 737288 | tf_op jit(solution)/shard_map/ppermute | solution.py:27
  406.8 8.7 %collective-permute-start.33 = (f32[32,2048]{1,0:T(8,128)S(1)}, f32[32,2048]{1,0:T(8,128)S(1)}, u32[]{:S(2)}, u32[]{:S(2)}) collective-permute-start(f32[32,2048]{1,0:T(8,128)S(1)} %get-tuple-element.200), channel_id=1, source_target_pairs={{0,1},{1,0},{2,3},{3,2},{4,5},{5,4},{6,7},{7,6},{8,9},{9,8},{10,11... | collective-permute-start | bytes 786440 | tf_op jit(solution)/shard_map/ppermute | solution.py:27
  (65 other events, 375.9 us)
Sparse Core Ops, SparseCore 0:
  12.9 152.9 all-gather.2
  212.4 50.4 reduce-scatter.5
  266.1 78.0 reduce-scatter.9
  354.9 47.9 reduce-scatter.7

commit v5 on v4

--- a/solution.py
+++ b/solution.py
@@ -15,7 +15,7 @@
 BF = jnp.bfloat16
 F32 = jnp.float32
 BOTH = ("ctx", "fsdp")
-VMEM_LIMIT = 48 << 20
+VMEM_LIMIT = 16 << 20
 
 
 def dot(a, b, ca, cb):
@@ -361,24 +361,21 @@
     grad_h2, grad_gain_two, grad_bias_two = norm_backward(upstream, normed_two, inverse_two, gain_two)
     grad_branch = grad_h2.astype(BF)
     grad_down_bias = jnp.sum(grad_branch.astype(F32), axis=0)
-    both_branch = jnp.concatenate([grad_branch, core_swap(grad_branch)])
-    grad_down = dot(activated, both_branch, 0, 0).astype(BF)
-    both_branch = lax.optimization_barrier((both_branch, grad_down))[0]
+    other_branch = core_swap(grad_branch)
+    hidden_own = (dot(grad_branch, down_mat, 1, 1) * slope[:flat_rows].astype(F32)).astype(BF)
+    grad_down = dot(activated, jnp.concatenate([grad_branch, other_branch]), 0, 0).astype(BF)
+    other_branch = lax.optimization_barrier((other_branch, grad_down))[0]
     grad_down = lax.psum_scatter(grad_down, "ctx", scatter_dimension=0, tiled=True)
-    grad_hidden = (dot(both_branch, down_mat, 1, 1) * slope.astype(F32)).astype(BF)
+    hidden_other = (dot(other_branch, down_mat, 1, 1) * slope[flat_rows:].astype(F32)).astype(BF)
+    grad_hidden = jnp.concatenate([hidden_own, hidden_other])
     grad_up_bias = dot(jnp.ones((8, grad_hidden.shape[0]), BF), grad_hidden, 1, 0)[0]
-    away = core_swap(dot(grad_hidden[flat_rows:], up_mat, 1, 1).astype(BF))
-    grad_first = dot(grad_hidden[:flat_rows], up_mat, 1, 1) + away.astype(F32) + grad_h2
+    away = core_swap(dot(hidden_other, up_mat, 1, 1).astype(BF))
+    grad_first = dot(hidden_own, up_mat, 1, 1) + away.astype(F32) + grad_h2
     grad_h1, grad_gain_one, grad_bias_one = norm_backward(grad_first, normed_one, inverse_one, gain_one)
     grad_attended = grad_h1.astype(BF)
     grad_out_bias = jnp.sum(grad_attended.astype(F32), axis=0)
-    dos = []
-    for g in range(groups):
-        do = dot(out_mat, grad_attended[g * ctx_rows : (g + 1) * ctx_rows], 1, 1).astype(BF)
-        dos.append(do.reshape(nc, cols, ctx_rows))
-    for g in range(groups):
-        dos[g] = exchange_ctx(dos[g] if g == 0 else after(dos[g], dos[0]))
-    later = after((both_first, grad_hidden, mixed, grad_attended), dos[0])
+    do_all = exchange_ctx(dot(out_mat, grad_attended, 1, 1).astype(BF).reshape(nc, cols, flat_rows))
+    later = after((both_first, grad_hidden, mixed, grad_attended), do_all)
     grad_out = dot(later[2], later[3], 1, 0).astype(BF).reshape(nc, nz, 2, rows_w, width)
     grad_ups = [
         dot(later[0], later[1][:, j * width : (j + 1) * width], 0, 0).astype(BF) for j in range(parts)
@@ -393,7 +390,7 @@
     grad_qkv = None
     grad_bias_parts = []
     for g in range(groups):
-        dqkv = attend_back(qkvs[g], dos[g], 0, lses[g], segs[g], ctx_rows)
+        dqkv = attend_back(qkvs[g], do_all, g, lses[g], segs[g], ctx_rows)
         if g == 1:
             dqkv, backs[0], down_got = lax.optimization_barrier((dqkv, backs[0], down_got))
         grad_bias_parts.append(jnp.sum(dqkv.astype(F32), axis=1))
@@ -438,10 +435,10 @@
     small = total_of([t[rows_w:] for t in got]).reshape(8 * 3 * cols)
     grad_qkv = place([t[:rows_w] for t in got], me_c).reshape(nc, rows_w, 3, cols)
     grad_qkv = jnp.moveaxis(grad_qkv, 0, 2).reshape(rows_w, 3, width).astype(F32)
-    grad_up = lax.psum_scatter(grad_up, "fsdp", scatter_dimension=0, axis_index_groups=z_groups()).astype(F32)
+    grad_up = lax.psum_scatter(grad_up, "fsdp", scatter_dimension=0, axis_index_groups=z_groups())
     input_grads = [total_of([t[r] for r in range(nc)]) for t in backs]
     grad_down = z_sum(grad_down, down_got)
-    grad_out = grad_up[n_up:]
+    grad_out = grad_up[n_up:].astype(F32)
     grad_up = [grad_up[j * 2 * rows_w : (j + 1) * 2 * rows_w] for j in range(parts)]
     grad_up = jnp.concatenate(grad_up, axis=1).reshape(2, rows_w, half)
     grad_up_got = core_swap(lax.dynamic_index_in_dim(grad_up, 1 - core, 0, False))
@@ -449,7 +446,7 @@
         t.reshape(rows_w, half // ff_w, ff_w)
         for t in (lax.dynamic_index_in_dim(grad_up, core, 0, False), grad_up_got)
     ]
-    grad_up = in_order(pair[0], pair[1], core, 2).reshape(rows_w, ff)
+    grad_up = in_order(pair[0], pair[1], core, 2).reshape(rows_w, ff).astype(F32)
     grad_tokens = grad_h1.reshape(groups, ctx_rows, width) + jnp.stack(input_grads)
     grad_tokens = grad_tokens.reshape(micro, per_device, ctx_rows, width)
 

time: 431 us -> 423 us (0.981)
  the two profiles are of different devices: /device:TPU:9 before, /device:TPU:1 now
where the time goes in v5:
time: 423 us; the launch traced here: 417 us
  matrix products  83.4 us (20%)
  waiting for transfers between devices  80 us (19%)
  starting transfers between devices  69.3 us (16%)
  Pallas kernels  67.2 us (16%)
  local copies, waits for them, and re-layouts  44.9 us (11%)
  other arithmetic  41.7 us (10%)
  between operations  15.7 us (4%)
  blocking collectives  15.3 us (4%)
    dot_general x20, matrix products, dot(): lax.dot_general(a, b, (((ca,), (cb,)), ((), ())), preferred_element_type=...  83.4 us
    ppermute x34, waiting for transfers between devices, swap(): return lax.ppermute(x, axis, [(i, i ^ r) for i in range(n)])  54.9 us
    ppermute x34, starting transfers between devices, swap(): return lax.ppermute(x, axis, [(i, i ^ r) for i in range(n)])  46.5 us
    pallas_call x2, Pallas kernels, attend_back(): pl.pallas_call(functools.partial(attend_back_kernel, heads, nq, block), g...  42.9 us
    pallas_call x2, Pallas kernels, attend(): pl.pallas_call(attend_kernel, grid=(heads, nq), in_specs=[pl.BlockSpec((H...  24.3 us
    all_to_all x5, starting transfers between devices, exchange_ctx(): return lax.all_to_all(x, 'ctx', 0, 0)  22.2 us
    all_to_all x1, blocking collectives, exchange_ctx(): return lax.all_to_all(x, 'ctx', 0, 0)  15.3 us
    all_to_all x5, waiting for transfers between devices, exchange_ctx(): return lax.all_to_all(x, 'ctx', 0, 0)  11.7 us
  transfers between devices with their start and end apart: 43, of which 20 were waited for; matrix products, arithmetic and copies ran while one was open for 29% of the time, Pallas kernels for 16%

profile of v5, /device:TPU:1, one launch (start us, length us, event | category | flops | bytes accessed | tf_op | source)
XLA Modules:
  0.0 417.5 jit_solution(11358443062574765817)
XLA Ops:
  27.8 4.5 %all-to-all-start = ((bf16[4,256,1024]{2,1,0:T(8,128)(2,1)}), bf16[4,256,1024]{2,1,0:T(8,128)(2,1)}, u32[]{:S(2)}, u32[]{:S(2)}) async-start(bf16[4,256,1024]{2,1,0:T(8,128)(2,1)} %broadcast_in_dim.147), calls=%async_computation | async-start | bytes 4194304 | tf_op jit(solution)/shard_map/all_to_all | solution.py:114
  32.4 16.3 %collective-permute-done.4 = bf16[4,40,768]{2,1,0:T(8,128)(2,1)S(1)} collective-permute-done((bf16[4,40,768]{2,1,0:T(8,128)(2,1)S(1)}, bf16[4,40,768]{2,1,0:T(8,128)(2,1)S(1)}, u32[]{:S(2)}, u32[]{:S(2)}) %collective-permute-start.4) | collective-permute-done | bytes 245792 | tf_op jit(solution)/shard_map/ppermute | solution.py:27
  51.3 4.7 %collective-permute-start.6 = (bf16[4,4,40,768]{3,2,0,1:T(8,128)(2,1)S(1)}, bf16[4,4,40,768]{3,2,0,1:T(8,128)(2,1)S(1)}, u32[]{:S(2)}, u32[]{:S(2)}) collective-permute-start(bf16[4,4,40,768]{3,2,0,1:T(8,128)(2,1)S(1)} %bitcast_dynamic-update-slice_fusion.7), channel_id=1, source_target_pairs={{0,1},{1,0},{2,3},{3,2},{4,5},{5,4},{6,7},{7,6},{8,9},{9,8},{10,11... | collective-permute-start | bytes 2949128 | tf_op jit(solution)/shard_map/ppermute | solution.py:27
  64.2 4.7 %all-to-all-start.2 = ((bf16[4,256,1024]{2,1,0:T(8,128)(2,1)}), bf16[4,256,1024]{2,1,0:T(8,128)(2,1)}, u32[]{:S(2)}, u32[]{:S(2)}) async-start(bf16[4,256,1024]{2,1,0:T(8,128)(2,1)} %broadcast_in_dim.149), calls=%async_computation.2 | async-start | bytes 4194304 | tf_op jit(solution)/shard_map/all_to_all | solution.py:114
  70.7 4.0 add_convert_fusion.2.q_ref.k_ref.v_ref
  74.7 12.1 %attend.2 = (bf16[4,256,256]{2,1,0:T(8,128)(2,1)S(1)}, f32[4,1,1024]{2,1,0:T(1,128)S(1)}) custom-call(bf16[768,1024]{1,0:T(8,128)(2,1)S(1)} %add_convert_fusion.2.q_ref.k_ref.v_ref, bf16[768,1024]{1,0:T(8,128)(2,1)S(1)} %add_convert_fusion.2.q_ref.k_ref.v_ref, bf16[768,1024]{1,0:T(8,128)(2,1)S(1)} %add_convert_fusion.2.q_ref.k_ref.v_ref, ...), custom_call_target="tpu_custom_call" | custom-call | flops 1048576 | bytes 1048576 | tf_op jit(solution)/shard_map/attend/pallas_call | solution.py:134
  87.7 4.2 %collective-permute-start.7 = (bf16[32,1024]{1,0:T(8,128)(2,1)S(1)}, bf16[32,1024]{1,0:T(8,128)(2,1)S(1)}, u32[]{:S(2)}, u32[]{:S(2)}) collective-permute-start(bf16[32,1024]{1,0:T(8,128)(2,1)S(1)} %copy-done.41), channel_id=1, source_target_pairs={{0,2},{1,3},{2,0},{3,1},{4,6},{5,7},{6,4},{7,5},{8,10},{9,11},{10,... | collective-permute-start | bytes 196616 | tf_op jit(solution)/shard_map/ppermute | solution.py:27
  102.4 4.0 add_convert_fusion.1.q_ref.k_ref.v_ref
  106.4 12.2 %attend.3 = (bf16[4,256,256]{2,1,0:T(8,128)(2,1)S(1)}, f32[4,1,1024]{2,1,0:T(1,128)S(1)}) custom-call(bf16[768,1024]{1,0:T(8,128)(2,1)S(1)} %add_convert_fusion.1.q_ref.k_ref.v_ref, bf16[768,1024]{1,0:T(8,128)(2,1)S(1)} %add_convert_fusion.1.q_ref.k_ref.v_ref, bf16[768,1024]{1,0:T(8,128)(2,1)S(1)} %add_convert_fusion.1.q_ref.k_ref.v_ref, ...), custom_call_target="tpu_custom_call" | custom-call | flops 1048576 | bytes 1048576 | tf_op jit(solution)/shard_map/attend/pallas_call | solution.py:134
  118.6 4.8 %collective-permute-done.12 = bf16[4,32,1024]{2,1,0:T(8,128)(2,1)} collective-permute-done((bf16[4,32,1024]{2,1,0:T(8,128)(2,1)S(1)}, bf16[4,32,1024]{2,1,0:T(8,128)(2,1)}, u32[]{:S(2)}, u32[]{:S(2)}) %collective-permute-start.12) | collective-permute-done | bytes 262176 | tf_op jit(solution)/shard_map/ppermute | solution.py:27
  130.2 3.7 collective-permute-start.13
  133.9 15.3 %all_to_all.30 = bf16[4,256,256]{2,1,0:T(8,128)(2,1)} all-to-all(bf16[4,256,256]{2,1,0:T(8,128)(2,1)S(1)} %copy-done.8), channel_id=1, replica_groups=mesh['ctx'=4,'fsdp'=8] {'ctx'}, dimensions={0} | all-to-all | bytes 1048576 | tf_op jit(solution)/shard_map/all_to_all | solution.py:114
  149.2 4.2 all-to-all-start.3
  153.7 4.0 maximum_select_fusion
  160.9 3.5 fusion.85
  173.9 12.6 %fusion.4 = (bf16[1024,2048]{1,0:T(8,128)(2,1)}, bf16[1024,2048]{1,0:T(8,128)(2,1)S(1)}) fusion(f32[2048]{0:T(1024)S(1)} %bitcast.322, bf16[1024,1024]{1,0:T(8,128)(2,1)S(1)} %bitcast.291, bf16[1024,1024]{1,0:T(8,128)(2,1)S(1)} %bitcast.288, bf16[512,1024]{1,0:T(8,128)(2,1)} %collective-permute-done.14, bf16[512,1024]{1,0:T(8,128)(2,1)} %fusion.32), kind=kOutput, calls=%fused_computation.5 | convolution fusion | flops 4332716032 | bytes 14688256 | tf_op jit(solution)/shard_map/dot_general | solution.py:22
  186.5 3.3 fusion.33
  192.9 6.5 %fusion.80 = (f32[512]{0:T(512)S(1)}, f32[512,1024]{1,0:T(8,128)S(1)}) fusion(f32[1024]{0:T(1024)S(1)} %reshape.589, bf16[512,1024]{1,0:T(8,128)(2,1)} %collective-permute-done.16, f32[1024]{0:T(1024)S(1)} %reshape.587, f32[1024]{0:T(1024)S(1)} %reshape.586, f32[512]{0:T(512)S(1)} %add_rsqrt_fusion.1, f32[512,1024]{1,0:T(8,128)} %copy-done.10, ...), kind=kOutput, calls=%fused_computation.216 | convolution fusion | flops 2152201728 | bytes 11552768 | tf_op jit(solution)/shard_map/dot_general | solution.py:22
  208.2 6.5 %convolution_convert_fusion = bf16[2048,1024]{1,0:T(8,128)(2,1)} fusion(bf16[1024,2048]{1,0:T(8,128)(2,1)S(1)} %copy-done.54, bf16[512,1024]{1,0:T(8,128)(2,1)S(1)} %collective-permute-done.17, bf16[512,1024]{1,0:T(8,128)(2,1)S(1)} %get-tuple-element.171), kind=kOutput, calls=%fused_computation.13 | convolution fusion | flops 4301258752 | bytes 10485760 | tf_op jit(solution)/shard_map/dot_general | solution.py:22
  214.7 5.7 %multiply_convert_fusion.1 = bf16[512,2048]{1,0:T(8,128)(2,1)S(1)} fusion(bf16[512,1024]{1,0:T(8,128)(2,1)} %copy-done.52, bf16[2048,1024]{1,0:T(8,128)(2,1)} %bitcast.277, bf16[1024,2048]{1,0:T(8,128)(2,1)} %get-tuple-element.178), kind=kOutput, calls=%fused_computation.11 | convolution fusion | flops 2150629376 | bytes 9437184 | tf_op jit(solution)/shard_map/dot_general | solution.py:22
  235.1 4.3 %all-to-all-start.4 = ((bf16[4,256,512]{2,1,0:T(8,128)(2,1)}), bf16[4,256,512]{2,1,0:T(8,128)(2,1)}, u32[]{:S(2)}, u32[]{:S(2)}) async-start(bf16[4,256,512]{2,1,0:T(8,128)(2,1)} %bitcast.306), calls=%async_computation.4 | async-start | bytes 2097152 | tf_op jit(solution)/shard_map/all_to_all | solution.py:114
  247.7 7.8 %all-to-all-done.4.do_ref = bf16[4,256,512]{2,1,0:T(8,128)(2,1)} async-done(((bf16[4,256,512]{2,1,0:T(8,128)(2,1)}), bf16[4,256,512]{2,1,0:T(8,128)(2,1)}, u32[]{:S(2)}, u32[]{:S(2)}) %all-to-all-start.4) | async-done | bytes 1048608 | tf_op jit(solution)/shard_map/all_to_all | solution.py:114
  269.9 21.4 %attend_back.2 = bf16[768,1024]{1,0:T(8,128)(2,1)S(1)} custom-call(bf16[768,1024]{1,0:T(8,128)(2,1)S(1)} %add_convert_fusion.2.q_ref.k_ref.v_ref, bf16[768,1024]{1,0:T(8,128)(2,1)S(1)} %add_convert_fusion.2.q_ref.k_ref.v_ref, bf16[768,1024]{1,0:T(8,128)(2,1)S(1)} %add_convert_fusion.2.q_ref.k_ref.v_ref, bf16[4,256,512]{2,1,0:T(8,128)(2,1)} %all-to-all-done.4.do_ref, ...), custom_call_target="tpu_custom_call" | custom-call | flops 1048576 | bytes 1048576 | tf_op jit(solution)/shard_map/attend_back/pallas_call | solution.py:198
  294.5 4.6 %all-to-all-start.5 = ((bf16[4,256,1024]{2,1,0:T(8,128)(2,1)}), bf16[4,256,1024]{2,1,0:T(8,128)(2,1)}, u32[]{:S(2)}, u32[]{:S(2)}) async-start(bf16[4,256,1024]{2,1,0:T(8,128)(2,1)} %bitcast.286), calls=%async_computation.5 | async-start | bytes 4194304 | tf_op jit(solution)/shard_map/all_to_all | solution.py:114
  299.8 3.3 fusion.67
  308.9 5.1 %fusion.88 = f32[1024,768]{1,0:T(8,128)} fusion(bf16[1024,1024]{1,0:T(8,128)(2,1)} %bitcast.20, bf16[768,1024]{1,0:T(8,128)(2,1)S(1)} %copy-done.1), kind=kOutput, calls=%fused_computation.222 | convolution fusion | flops 1610612736 | bytes 6815744 | tf_op jit(solution)/shard_map/dot_general | solution.py:22
  314.0 21.5 %attend_back.3 = bf16[768,1024]{1,0:T(8,128)(2,1)S(1)} custom-call(bf16[768,1024]{1,0:T(8,128)(2,1)S(1)} %add_convert_fusion.1.q_ref.k_ref.v_ref, bf16[768,1024]{1,0:T(8,128)(2,1)S(1)} %add_convert_fusion.1.q_ref.k_ref.v_ref, bf16[768,1024]{1,0:T(8,128)(2,1)S(1)} %add_convert_fusion.1.q_ref.k_ref.v_ref, bf16[4,256,512]{2,1,0:T(8,128)(2,1)} %all-to-all-done.4.do_ref, ...), custom_call_target="tpu_custom_call" | custom-call | flops 1048576 | bytes 1048576 | tf_op jit(solution)/shard_map/attend_back/pallas_call | solution.py:198
  337.3 4.5 %add_convert_fusion = bf16[1024,768]{1,0:T(8,128)(2,1)S(1)} fusion(f32[1024,768]{1,0:T(8,128)} %fusion.88, bf16[1024,1024]{1,0:T(8,128)(2,1)} %bitcast.28, bf16[768,1024]{1,0:T(8,128)(2,1)S(1)} %attend_back.3), kind=kOutput, calls=%fused_computation.16 | convolution fusion | flops 1612185600 | bytes 8388608 | tf_op jit(solution)/shard_map/dot_general | solution.py:22
  358.3 8.8 %reduce-scatter.10.cloned.1.call-done = bf16[1,640,1024]{2,1,0:T(8,128)(2,1)} async-done(((bf16[4,640,1024]{2,1,0:T(8,128)(2,1)}), bf16[1,640,1024]{2,1,0:T(8,128)(2,1)}) %reduce-scatter.10.cloned.1.call-update) | async-done | bytes 1310736
  367.1 4.7 %collective-permute-start.26 = (bf16[4,40,768]{2,1,0:T(8,128)(2,1)S(1)}, bf16[4,40,768]{2,1,0:T(8,128)(2,1)S(1)}, u32[]{:S(2)}, u32[]{:S(2)}) collective-permute-start(bf16[4,40,768]{2,1,0:T(8,128)(2,1)S(1)} %get-tuple-element.194), channel_id=1, source_target_pairs={{0,2},{1,3},{2,0},{3,1},{4,6},{5,7},{6,4},{7,5},{8,10},{9,11},{10,... | collective-permute-start | bytes 737288 | tf_op jit(solution)/shard_map/ppermute | solution.py:27
  376.8 13.4 %collective-permute-done.26 = bf16[4,40,768]{2,1,0:T(8,128)(2,1)S(1)} collective-permute-done((bf16[4,40,768]{2,1,0:T(8,128)(2,1)S(1)}, bf16[4,40,768]{2,1,0:T(8,128)(2,1)S(1)}, u32[]{:S(2)}, u32[]{:S(2)}) %collective-permute-start.26) | collective-permute-done | bytes 245792 | tf_op jit(solution)/shard_map/ppermute | solution.py:27
  400.2 4.6 %reduce-scatter.8.cloned.1.call-done = bf16[1,160,1024]{2,1,0:T(8,128)(2,1)} async-done(((bf16[4,160,1024]{2,1,0:T(8,128)(2,1)}), bf16[1,160,1024]{2,1,0:T(8,128)(2,1)}) %reduce-scatter.8.cloned.1.call-update) | async-done | bytes 327696 | tf_op jit(solution)/shard_map/reduce_scatter | solution.py:438
  (345 shorter events, 161.3 us)
Async XLA Ops:
  7.2 161.3 %all-gather.3.cloned.1.call-start = ((), (), s32[]{:S(2)}) async-start(), calls=%async_computation.11 | async-start | bytes 8912896 | tf_op jit(solution)/shard_map/all_gather | solution.py:314
  21.7 10.7 %collective-permute-start.3 = (bf16[4,40,768]{2,1,0:T(8,128)(2,1)S(1)}, bf16[4,40,768]{2,1,0:T(8,128)(2,1)S(1)}, u32[]{:S(2)}, u32[]{:S(2)}) collective-permute-start(bf16[4,40,768]{2,1,0:T(8,128)(2,1)S(1)} %bitcast_dynamic-update-slice_fusion.12), channel_id=1, source_target_pairs={{0,2},{1,3},{2,0},{3,1},{4,6},{5,7},{6,4},{7,5},{8,10},{9,11},{10,... | collective-permute-start | bytes 737288 | tf_op jit(solution)/shard_map/ppermute | solution.py:27
  23.9 24.9 %collective-permute-start.4 = (bf16[4,40,768]{2,1,0:T(8,128)(2,1)S(1)}, bf16[4,40,768]{2,1,0:T(8,128)(2,1)S(1)}, u32[]{:S(2)}, u32[]{:S(2)}) collective-permute-start(bf16[4,40,768]{2,1,0:T(8,128)(2,1)S(1)} %bitcast_dynamic-update-slice_fusion.12), channel_id=1, source_target_pairs={{0,4},{1,5},{2,6},{3,7},{4,0},{5,1},{6,2},{7,3},{8,12},{9,13},{10,... | collective-permute-start | bytes 737288 | tf_op jit(solution)/shard_map/ppermute | solution.py:27
  26.2 25.1 %collective-permute-start.5 = (bf16[4,40,768]{2,1,0:T(8,128)(2,1)S(1)}, bf16[4,40,768]{2,1,0:T(8,128)(2,1)S(1)}, u32[]{:S(2)}, u32[]{:S(2)}) collective-permute-start(bf16[4,40,768]{2,1,0:T(8,128)(2,1)S(1)} %bitcast_dynamic-update-slice_fusion.12), channel_id=1, source_target_pairs={{0,6},{1,7},{2,4},{3,5},{4,2},{5,3},{6,0},{7,1},{8,14},{9,15},{10,... | collective-permute-start | bytes 737288 | tf_op jit(solution)/shard_map/ppermute | solution.py:27
  27.8 33.6 %all-to-all-start = ((bf16[4,256,1024]{2,1,0:T(8,128)(2,1)}), bf16[4,256,1024]{2,1,0:T(8,128)(2,1)}, u32[]{:S(2)}, u32[]{:S(2)}) async-start(bf16[4,256,1024]{2,1,0:T(8,128)(2,1)} %broadcast_in_dim.147), calls=%async_computation | async-start | bytes 4194304 | tf_op jit(solution)/shard_map/all_to_all | solution.py:114
  51.3 6.9 %collective-permute-start.6 = (bf16[4,4,40,768]{3,2,0,1:T(8,128)(2,1)S(1)}, bf16[4,4,40,768]{3,2,0,1:T(8,128)(2,1)S(1)}, u32[]{:S(2)}, u32[]{:S(2)}) collective-permute-start(bf16[4,4,40,768]{3,2,0,1:T(8,128)(2,1)S(1)} %bitcast_dynamic-update-slice_fusion.7), channel_id=1, source_target_pairs={{0,1},{1,0},{2,3},{3,2},{4,5},{5,4},{6,7},{7,6},{8,9},{9,8},{10,11... | collective-permute-start | bytes 2949128 | tf_op jit(solution)/shard_map/ppermute | solution.py:27
  64.2 38.2 %all-to-all-start.2 = ((bf16[4,256,1024]{2,1,0:T(8,128)(2,1)}), bf16[4,256,1024]{2,1,0:T(8,128)(2,1)}, u32[]{:S(2)}, u32[]{:S(2)}) async-start(bf16[4,256,1024]{2,1,0:T(8,128)(2,1)} %broadcast_in_dim.149), calls=%async_computation.2 | async-start | bytes 4194304 | tf_op jit(solution)/shard_map/all_to_all | solution.py:114
  87.7 6.4 %collective-permute-start.7 = (bf16[32,1024]{1,0:T(8,128)(2,1)S(1)}, bf16[32,1024]{1,0:T(8,128)(2,1)S(1)}, u32[]{:S(2)}, u32[]{:S(2)}) collective-permute-start(bf16[32,1024]{1,0:T(8,128)(2,1)S(1)} %copy-done.41), channel_id=1, source_target_pairs={{0,2},{1,3},{2,0},{3,1},{4,6},{5,7},{6,4},{7,5},{8,10},{9,11},{10,... | collective-permute-start | bytes 196616 | tf_op jit(solution)/shard_map/ppermute | solution.py:27
  91.9 7.8 %collective-permute-start.9 = (bf16[32,1024]{1,0:T(8,128)(2,1)S(1)}, bf16[32,1024]{1,0:T(8,128)(2,1)S(1)}, u32[]{:S(2)}, u32[]{:S(2)}) collective-permute-start(bf16[32,1024]{1,0:T(8,128)(2,1)S(1)} %copy-done.41), channel_id=1, source_target_pairs={{0,6},{1,7},{2,4},{3,5},{4,2},{5,3},{6,0},{7,1},{8,14},{9,15},{10,... | collective-permute-start | bytes 196616 | tf_op jit(solution)/shard_map/ppermute | solution.py:27
  99.7 19.0 %collective-permute-start.10 = (bf16[4,32,1024]{2,1,0:T(8,128)(2,1)S(1)}, bf16[4,32,1024]{2,1,0:T(8,128)(2,1)}, u32[]{:S(2)}, u32[]{:S(2)}) collective-permute-start(bf16[4,32,1024]{2,1,0:T(8,128)(2,1)S(1)} %bitcast_dynamic-update-slice_fusion.8), channel_id=1, source_target_pairs={{0,8},{8,0},{16,24},{24,16},{1,9},{9,1},{17,25},{25,17},{2,10},{10... | collective-permute-start | bytes 786440 | tf_op jit(solution)/shard_map/ppermute | solution.py:27
  100.2 18.4 %collective-permute-start.11 = (bf16[4,32,1024]{2,1,0:T(8,128)(2,1)S(1)}, bf16[4,32,1024]{2,1,0:T(8,128)(2,1)}, u32[]{:S(2)}, u32[]{:S(2)}) collective-permute-start(bf16[4,32,1024]{2,1,0:T(8,128)(2,1)S(1)} %bitcast_dynamic-update-slice_fusion.8), channel_id=1, source_target_pairs={{0,16},{8,24},{16,0},{24,8},{1,17},{9,25},{17,1},{25,9},{2,18},{10... | collective-permute-start | bytes 786440 | tf_op jit(solution)/shard_map/ppermute | solution.py:27
  100.8 22.6 %collective-permute-start.12 = (bf16[4,32,1024]{2,1,0:T(8,128)(2,1)S(1)}, bf16[4,32,1024]{2,1,0:T(8,128)(2,1)}, u32[]{:S(2)}, u32[]{:S(2)}) collective-permute-start(bf16[4,32,1024]{2,1,0:T(8,128)(2,1)S(1)} %bitcast_dynamic-update-slice_fusion.8), channel_id=1, source_target_pairs={{0,24},{8,16},{16,8},{24,0},{1,25},{9,17},{17,9},{25,1},{2,26},{10... | collective-permute-start | bytes 786440 | tf_op jit(solution)/shard_map/ppermute | solution.py:27
  130.2 23.4 %collective-permute-start.13 = (bf16[4,4,32,1024]{3,2,1,0:T(8,128)(2,1)}, bf16[4,4,32,1024]{3,2,1,0:T(8,128)(2,1)}, u32[]{:S(2)}, u32[]{:S(2)}) collective-permute-start(bf16[4,4,32,1024]{3,2,1,0:T(8,128)(2,1)} %bitcast_dynamic-update-slice_fusion), channel_id=1, source_target_pairs={{0,1},{1,0},{2,3},{3,2},{4,5},{5,4},{6,7},{7,6},{8,9},{9,8},{10,11... | collective-permute-start | bytes 3145736 | tf_op jit(solution)/shard_map/ppermute | solution.py:27
  149.2 11.7 %all-to-all-start.3 = ((bf16[4,256,256]{2,1,0:T(8,128)(2,1)}), bf16[4,256,256]{2,1,0:T(8,128)(2,1)}, u32[]{:S(2)}, u32[]{:S(2)}) async-start(bf16[4,256,256]{2,1,0:T(8,128)(2,1)} %copy-done.9), calls=%async_computation.3 | async-start | bytes 1048576 | tf_op jit(solution)/shard_map/all_to_all | solution.py:114
  153.4 150.0 %reduce-scatter.6.cloned.1.call-start = ((), (), s32[]{:S(2)}) async-start(), calls=%async_computation.9 | async-start | bytes 5242880 | tf_op jit(solution)/shard_map/reduce_scatter | solution.py:368
  166.3 7.6 %collective-permute-start.14 = (bf16[512,1024]{1,0:T(8,128)(2,1)}, bf16[512,1024]{1,0:T(8,128)(2,1)}, u32[]{:S(2)}, u32[]{:S(2)}) collective-permute-start(bf16[512,1024]{1,0:T(8,128)(2,1)} %fusion.32), channel_id=1, source_target_pairs={{0,1},{1,0},{2,3},{3,2},{4,5},{5,4},{6,7},{7,6},{8,9},{9,8},{10,11... | collective-permute-start | bytes 3145736 | tf_op jit(solution)/shard_map/ppermute | solution.py:27
  235.1 20.4 %all-to-all-start.4 = ((bf16[4,256,512]{2,1,0:T(8,128)(2,1)}), bf16[4,256,512]{2,1,0:T(8,128)(2,1)}, u32[]{:S(2)}, u32[]{:S(2)}) async-start(bf16[4,256,512]{2,1,0:T(8,128)(2,1)} %bitcast.306), calls=%async_computation.4 | async-start | bytes 2097152 | tf_op jit(solution)/shard_map/all_to_all | solution.py:114
  239.4 127.7 %reduce-scatter.10.cloned.1.call-start = ((), (), s32[]{:S(2)}) async-start(), calls=%async_computation.12 | async-start | bytes 6553600
  258.6 6.7 %collective-permute-start.32 = (bf16[4,4,32,1024]{3,2,1,0:T(8,128)(2,1)S(1)}, bf16[4,4,32,1024]{3,2,1,0:T(8,128)(2,1)S(1)}, u32[]{:S(2)}, u32[]{:S(2)}) collective-permute-start(bf16[4,4,32,1024]{3,2,1,0:T(8,128)(2,1)S(1)} %dynamic-slice_bitcast_fusion), channel_id=1, source_target_pairs={{0,1},{1,0},{2,3},{3,2},{4,5},{5,4},{6,7},{7,6},{8,9},{9,8},{10,11... | collective-permute-start | bytes 3145736 | tf_op jit(solution)/shard_map/ppermute | solution.py:27
  294.5 41.9 %all-to-all-start.5 = ((bf16[4,256,1024]{2,1,0:T(8,128)(2,1)}), bf16[4,256,1024]{2,1,0:T(8,128)(2,1)}, u32[]{:S(2)}, u32[]{:S(2)}) async-start(bf16[4,256,1024]{2,1,0:T(8,128)(2,1)} %bitcast.286), calls=%async_computation.5 | async-start | bytes 4194304 | tf_op jit(solution)/shard_map/all_to_all | solution.py:114
  299.1 105.7 %reduce-scatter.8.cloned.1.call-start = ((), (), s32[]{:S(2)}) async-start(), calls=%async_computation.10 | async-start | bytes 1638400 | tf_op jit(solution)/shard_map/reduce_scatter | solution.py:438
  305.4 31.0 %collective-permute-start.19 = (bf16[128,1024]{1,0:T(8,128)(2,1)}, bf16[128,1024]{1,0:T(8,128)(2,1)}, u32[]{:S(2)}, u32[]{:S(2)}) collective-permute-start(bf16[128,1024]{1,0:T(8,128)(2,1)} %get-tuple-element.191), channel_id=1, source_target_pairs={{0,2},{1,3},{2,0},{3,1},{4,6},{5,7},{6,4},{7,5},{8,10},{9,11},{10,... | collective-permute-start | bytes 786440 | tf_op jit(solution)/shard_map/ppermute | solution.py:27
  306.1 30.3 %collective-permute-start.20 = (bf16[128,1024]{1,0:T(8,128)(2,1)}, bf16[128,1024]{1,0:T(8,128)(2,1)}, u32[]{:S(2)}, u32[]{:S(2)}) collective-permute-start(bf16[128,1024]{1,0:T(8,128)(2,1)} %get-tuple-element.190), channel_id=1, source_target_pairs={{0,4},{1,5},{2,6},{3,7},{4,0},{5,1},{6,2},{7,3},{8,12},{9,13},{10,... | collective-permute-start | bytes 786440 | tf_op jit(solution)/shard_map/ppermute | solution.py:27
  308.0 28.3 %collective-permute-start.21 = (bf16[128,1024]{1,0:T(8,128)(2,1)S(1)}, bf16[128,1024]{1,0:T(8,128)(2,1)}, u32[]{:S(2)}, u32[]{:S(2)}) collective-permute-start(bf16[128,1024]{1,0:T(8,128)(2,1)S(1)} %get-tuple-element.189), channel_id=1, source_target_pairs={{0,6},{1,7},{2,4},{3,5},{4,2},{5,3},{6,0},{7,1},{8,14},{9,15},{10,... | collective-permute-start | bytes 786440 | tf_op jit(solution)/shard_map/ppermute | solution.py:27
  342.9 8.3 %collective-permute-start.25 = (bf16[4,4,40,768]{3,2,0,1:T(8,128)(2,1)}, bf16[4,4,40,768]{3,2,0,1:T(8,128)(2,1)}, u32[]{:S(2)}, u32[]{:S(2)}) collective-permute-start(bf16[4,4,40,768]{3,2,0,1:T(8,128)(2,1)} %bitcast.259), channel_id=1, source_target_pairs={{0,1},{1,0},{2,3},{3,2},{4,5},{5,4},{6,7},{7,6},{8,9},{9,8},{10,11... | collective-permute-start | bytes 2949128 | tf_op jit(solution)/shard_map/ppermute | solution.py:27
  348.3 43.1 %collective-permute-start.22 = (bf16[256,1024]{1,0:T(8,128)(2,1)}, bf16[256,1024]{1,0:T(8,128)(2,1)S(1)}, u32[]{:S(2)}, u32[]{:S(2)}) collective-permute-start(bf16[256,1024]{1,0:T(8,128)(2,1)} %get-tuple-element.185), channel_id=1, source_target_pairs={{0,8},{8,0},{16,24},{24,16},{1,9},{9,1},{17,25},{25,17},{2,10},{10... | collective-permute-start | bytes 1572872 | tf_op jit(solution)/shard_map/ppermute | solution.py:27
  350.1 41.4 %collective-permute-start.23 = (bf16[256,1024]{1,0:T(8,128)(2,1)}, bf16[256,1024]{1,0:T(8,128)(2,1)}, u32[]{:S(2)}, u32[]{:S(2)}) collective-permute-start(bf16[256,1024]{1,0:T(8,128)(2,1)} %get-tuple-element.184), channel_id=1, source_target_pairs={{0,16},{8,24},{16,0},{24,8},{1,17},{9,25},{17,1},{25,9},{2,18},{10... | collective-permute-start | bytes 1572872 | tf_op jit(solution)/shard_map/ppermute | solution.py:27
  351.0 40.4 %collective-permute-start.24 = (bf16[256,1024]{1,0:T(8,128)(2,1)}, bf16[256,1024]{1,0:T(8,128)(2,1)}, u32[]{:S(2)}, u32[]{:S(2)}) collective-permute-start(bf16[256,1024]{1,0:T(8,128)(2,1)} %get-tuple-element.183), channel_id=1, source_target_pairs={{0,24},{8,16},{16,8},{24,0},{1,25},{9,17},{17,9},{25,1},{2,26},{10... | collective-permute-start | bytes 1572872 | tf_op jit(solution)/shard_map/ppermute | solution.py:27
  353.5 13.6 %collective-permute-start.28 = (bf16[4,40,768]{2,1,0:T(8,128)(2,1)}, bf16[4,40,768]{2,1,0:T(8,128)(2,1)}, u32[]{:S(2)}, u32[]{:S(2)}) collective-permute-start(bf16[4,40,768]{2,1,0:T(8,128)(2,1)} %get-tuple-element.195), channel_id=1, source_target_pairs={{0,6},{1,7},{2,4},{3,5},{4,2},{5,3},{6,0},{7,1},{8,14},{9,15},{10,... | collective-permute-start | bytes 737288 | tf_op jit(solution)/shard_map/ppermute | solution.py:27
  358.2 18.6 %collective-permute-start.27 = (bf16[4,40,768]{2,1,0:T(8,128)(2,1)}, bf16[4,40,768]{2,1,0:T(8,128)(2,1)}, u32[]{:S(2)}, u32[]{:S(2)}) collective-permute-start(bf16[4,40,768]{2,1,0:T(8,128)(2,1)} %get-tuple-element.196), channel_id=1, source_target_pairs={{0,4},{1,5},{2,6},{3,7},{4,0},{5,1},{6,2},{7,3},{8,12},{9,13},{10,... | collective-permute-start | bytes 737288 | tf_op jit(solution)/shard_map/ppermute | solution.py:27
  367.1 23.1 %collective-permute-start.26 = (bf16[4,40,768]{2,1,0:T(8,128)(2,1)S(1)}, bf16[4,40,768]{2,1,0:T(8,128)(2,1)S(1)}, u32[]{:S(2)}, u32[]{:S(2)}) collective-permute-start(bf16[4,40,768]{2,1,0:T(8,128)(2,1)S(1)} %get-tuple-element.194), channel_id=1, source_target_pairs={{0,2},{1,3},{2,0},{3,1},{4,6},{5,7},{6,4},{7,5},{8,10},{9,11},{10,... | collective-permute-start | bytes 737288 | tf_op jit(solution)/shard_map/ppermute | solution.py:27
  391.5 6.0 %collective-permute-start.29 = (bf16[40,768]{1,0:T(8,128)(2,1)S(1)}, bf16[40,768]{1,0:T(8,128)(2,1)S(1)}, u32[]{:S(2)}, u32[]{:S(2)}) collective-permute-start(bf16[40,768]{1,0:T(8,128)(2,1)S(1)} %get-tuple-element.216), channel_id=1, source_target_pairs={{0,8},{8,0},{16,24},{24,16},{1,9},{9,1},{17,25},{25,17},{2,10},{10... | collective-permute-start | bytes 184328 | tf_op jit(solution)/shard_map/ppermute | solution.py:27
  (67 other events, 404.4 us)
Sparse Core Ops, SparseCore 0:
  12.6 155.2 all-gather.2
  214.8 59.1 reduce-scatter.5
  277.3 89.7 reduce-scatter.9
  369.3 35.3 reduce-scatter.7

commit v6 on v5

--- a/solution.py
+++ b/solution.py
@@ -151,7 +151,7 @@
         ],
         compiler_params=pltpu.CompilerParams(vmem_limit_bytes=VMEM_LIMIT),
         cost_estimate=pl.CostEstimate(
-            flops=1 << 20,
+            flops=12000 << 20,
             transcendentals=1 << 10,
             bytes_accessed=1 << 20,
         ),

time: 423 us -> 422 us (level)
    unnamed x119 -> x117, local copies, waits for them, and re-layouts: 11.2 us -> 9.33 us
  transfers between devices with their start and end apart: 43 -> 43, of which waited for: 20 -> 21; matrix products, arithmetic and copies ran while one was open for 29% -> 28% of each run, Pallas kernels for 16% -> 16%
where the time goes in v6:
time: 422 us; the launch traced here: 416 us
  matrix products  83.1 us (20%)
  waiting for transfers between devices  81 us (19%)
  starting transfers between devices  70.3 us (17%)
  Pallas kernels  67.2 us (16%)
  local copies, waits for them, and re-layouts  41.2 us (10%)
  other arithmetic  39.8 us (9%)
  blocking collectives  18.3 us (4%)
  between operations  15.7 us (4%)
    dot_general x20, matrix products, dot(): lax.dot_general(a, b, (((ca,), (cb,)), ((), ())), preferred_element_type=...  83.1 us
    ppermute x34, waiting for transfers between devices, swap(): return lax.ppermute(x, axis, [(i, i ^ r) for i in range(n)])  55.9 us
    ppermute x34, starting transfers between devices, swap(): return lax.ppermute(x, axis, [(i, i ^ r) for i in range(n)])  47.5 us
    pallas_call x2, Pallas kernels, attend_back(): pl.pallas_call(functools.partial(attend_back_kernel, heads, nq, block), g...  42.9 us
    pallas_call x2, Pallas kernels, attend(): pl.pallas_call(attend_kernel, grid=(heads, nq), in_specs=[pl.BlockSpec((H...  24.3 us
    all_to_all x5, starting transfers between devices, exchange_ctx(): return lax.all_to_all(x, 'ctx', 0, 0)  22.2 us
    all_to_all x1, blocking collectives, exchange_ctx(): return lax.all_to_all(x, 'ctx', 0, 0)  18.3 us
    all_to_all x5, waiting for transfers between devices, exchange_ctx(): return lax.all_to_all(x, 'ctx', 0, 0)  13.1 us
  transfers between devices with their start and end apart: 43, of which 21 were waited for; matrix products, arithmetic and copies ran while one was open for 28% of the time, Pallas kernels for 16%

profile of v6, /device:TPU:1, one launch (start us, length us, event | category | flops | bytes accessed | tf_op | source)
XLA Modules:
  0.0 416.5 jit_solution(7152801720643315193)
XLA Ops:
  27.1 4.5 %all-to-all-start = ((bf16[4,256,1024]{2,1,0:T(8,128)(2,1)}), bf16[4,256,1024]{2,1,0:T(8,128)(2,1)}, u32[]{:S(2)}, u32[]{:S(2)}) async-start(bf16[4,256,1024]{2,1,0:T(8,128)(2,1)} %broadcast_in_dim.147), calls=%async_computation | async-start | bytes 4194304 | tf_op jit(solution)/shard_map/all_to_all | solution.py:114
  31.8 8.8 %collective-permute-done.4 = bf16[4,40,768]{2,1,0:T(8,128)(2,1)S(1)} collective-permute-done((bf16[4,40,768]{2,1,0:T(8,128)(2,1)S(1)}, bf16[4,40,768]{2,1,0:T(8,128)(2,1)S(1)}, u32[]{:S(2)}, u32[]{:S(2)}) %collective-permute-start.4) | collective-permute-done | bytes 245792 | tf_op jit(solution)/shard_map/ppermute | solution.py:27
  40.6 10.6 %collective-permute-done.5 = bf16[4,40,768]{2,1,0:T(8,128)(2,1)S(1)} collective-permute-done((bf16[4,40,768]{2,1,0:T(8,128)(2,1)S(1)}, bf16[4,40,768]{2,1,0:T(8,128)(2,1)S(1)}, u32[]{:S(2)}, u32[]{:S(2)}) %collective-permute-start.5) | collective-permute-done | bytes 245792 | tf_op jit(solution)/shard_map/ppermute | solution.py:27
  51.3 4.4 %collective-permute-start.6 = (bf16[4,4,40,768]{3,2,0,1:T(8,128)(2,1)S(1)}, bf16[4,4,40,768]{3,2,0,1:T(8,128)(2,1)S(1)}, u32[]{:S(2)}, u32[]{:S(2)}) collective-permute-start(bf16[4,4,40,768]{3,2,0,1:T(8,128)(2,1)S(1)} %bitcast_dynamic-update-slice_fusion.7), channel_id=1, source_target_pairs={{0,1},{1,0},{2,3},{3,2},{4,5},{5,4},{6,7},{7,6},{8,9},{9,8},{10,11... | collective-permute-start | bytes 2949128 | tf_op jit(solution)/shard_map/ppermute | solution.py:27
  61.7 4.7 %all-to-all-start.2 = ((bf16[4,256,1024]{2,1,0:T(8,128)(2,1)}), bf16[4,256,1024]{2,1,0:T(8,128)(2,1)}, u32[]{:S(2)}, u32[]{:S(2)}) async-start(bf16[4,256,1024]{2,1,0:T(8,128)(2,1)} %broadcast_in_dim.149), calls=%async_computation.2 | async-start | bytes 4194304 | tf_op jit(solution)/shard_map/all_to_all | solution.py:114
  66.3 4.0 add_convert_fusion.2.q_ref.k_ref.v_ref
  70.4 12.1 %attend.2 = (bf16[4,256,256]{2,1,0:T(8,128)(2,1)S(1)}, f32[4,1,1024]{2,1,0:T(1,128)S(1)}) custom-call(bf16[768,1024]{1,0:T(8,128)(2,1)S(1)} %add_convert_fusion.2.q_ref.k_ref.v_ref, bf16[768,1024]{1,0:T(8,128)(2,1)S(1)} %add_convert_fusion.2.q_ref.k_ref.v_ref, bf16[768,1024]{1,0:T(8,128)(2,1)S(1)} %add_convert_fusion.2.q_ref.k_ref.v_ref, ...), custom_call_target="tpu_custom_call" | custom-call | flops 12582912000 | bytes 1048576 | tf_op jit(solution)/shard_map/attend/pallas_call | solution.py:134
  83.3 4.2 %collective-permute-start.7 = (bf16[32,1024]{1,0:T(8,128)(2,1)S(1)}, bf16[32,1024]{1,0:T(8,128)(2,1)S(1)}, u32[]{:S(2)}, u32[]{:S(2)}) collective-permute-start(bf16[32,1024]{1,0:T(8,128)(2,1)S(1)} %copy-done.40), channel_id=1, source_target_pairs={{0,2},{1,3},{2,0},{3,1},{4,6},{5,7},{6,4},{7,5},{8,10},{9,11},{10,... | collective-permute-start | bytes 196616 | tf_op jit(solution)/shard_map/ppermute | solution.py:27
  93.3 4.7 %collective-permute-done.9 = bf16[32,1024]{1,0:T(8,128)(2,1)S(1)} collective-permute-done((bf16[32,1024]{1,0:T(8,128)(2,1)S(1)}, bf16[32,1024]{1,0:T(8,128)(2,1)S(1)}, u32[]{:S(2)}, u32[]{:S(2)}) %collective-permute-start.9) | collective-permute-done | bytes 65568 | tf_op jit(solution)/shard_map/ppermute | solution.py:27
  101.2 4.0 add_convert_fusion.1.q_ref.k_ref.v_ref
  105.2 12.2 %attend.3 = (bf16[4,256,256]{2,1,0:T(8,128)(2,1)S(1)}, f32[4,1,1024]{2,1,0:T(1,128)S(1)}) custom-call(bf16[768,1024]{1,0:T(8,128)(2,1)S(1)} %add_convert_fusion.1.q_ref.k_ref.v_ref, bf16[768,1024]{1,0:T(8,128)(2,1)S(1)} %add_convert_fusion.1.q_ref.k_ref.v_ref, bf16[768,1024]{1,0:T(8,128)(2,1)S(1)} %add_convert_fusion.1.q_ref.k_ref.v_ref, ...), custom_call_target="tpu_custom_call" | custom-call | flops 12582912000 | bytes 1048576 | tf_op jit(solution)/shard_map/attend/pallas_call | solution.py:134
  124.3 3.3 collective-permute-start.13
  127.6 18.3 %all_to_all.30 = bf16[4,256,256]{2,1,0:T(8,128)(2,1)} all-to-all(bf16[4,256,256]{2,1,0:T(8,128)(2,1)S(1)} %copy-done.8), channel_id=1, replica_groups=mesh['ctx'=4,'fsdp'=8] {'ctx'}, dimensions={0} | all-to-all | bytes 1048576 | tf_op jit(solution)/shard_map/all_to_all | solution.py:114
  145.9 4.2 all-to-all-start.3
  150.4 4.0 maximum_select_fusion
  157.6 3.5 fusion.85
  171.5 12.6 %fusion.4 = (bf16[1024,2048]{1,0:T(8,128)(2,1)}, bf16[1024,2048]{1,0:T(8,128)(2,1)S(1)}) fusion(f32[2048]{0:T(1024)S(1)} %bitcast.322, bf16[1024,1024]{1,0:T(8,128)(2,1)S(1)} %bitcast.291, bf16[1024,1024]{1,0:T(8,128)(2,1)S(1)} %bitcast.288, bf16[512,1024]{1,0:T(8,128)(2,1)} %collective-permute-done.14, bf16[512,1024]{1,0:T(8,128)(2,1)} %fusion.32), kind=kOutput, calls=%fused_computation.5 | convolution fusion | flops 4332716032 | bytes 14688256 | tf_op jit(solution)/shard_map/dot_general | solution.py:22
  184.1 3.3 fusion.33
  190.9 6.5 %fusion.80 = (f32[512]{0:T(512)S(1)}, f32[512,1024]{1,0:T(8,128)S(1)}) fusion(f32[1024]{0:T(1024)S(1)} %reshape.589, bf16[512,1024]{1,0:T(8,128)(2,1)} %collective-permute-done.16, f32[1024]{0:T(1024)S(1)} %reshape.587, f32[1024]{0:T(1024)S(1)} %reshape.586, f32[512]{0:T(512)S(1)} %add_rsqrt_fusion.1, f32[512,1024]{1,0:T(8,128)} %copy-done.10, ...), kind=kOutput, calls=%fused_computation.216 | convolution fusion | flops 2152201728 | bytes 11552768 | tf_op jit(solution)/shard_map/dot_general | solution.py:22
  206.2 6.4 %convolution_convert_fusion = bf16[2048,1024]{1,0:T(8,128)(2,1)} fusion(bf16[1024,2048]{1,0:T(8,128)(2,1)S(1)} %copy-done.53, bf16[512,1024]{1,0:T(8,128)(2,1)S(1)} %collective-permute-done.17, bf16[512,1024]{1,0:T(8,128)(2,1)S(1)} %get-tuple-element.171), kind=kOutput, calls=%fused_computation.13 | convolution fusion | flops 4301258752 | bytes 10485760 | tf_op jit(solution)/shard_map/dot_general | solution.py:22
  212.6 5.7 %multiply_convert_fusion.1 = bf16[512,2048]{1,0:T(8,128)(2,1)S(1)} fusion(bf16[512,1024]{1,0:T(8,128)(2,1)} %copy-done.51, bf16[2048,1024]{1,0:T(8,128)(2,1)} %bitcast.277, bf16[1024,2048]{1,0:T(8,128)(2,1)} %get-tuple-element.178), kind=kOutput, calls=%fused_computation.11 | convolution fusion | flops 2150629376 | bytes 9437184 | tf_op jit(solution)/shard_map/dot_general | solution.py:22
  232.9 4.3 %all-to-all-start.4 = ((bf16[4,256,512]{2,1,0:T(8,128)(2,1)}), bf16[4,256,512]{2,1,0:T(8,128)(2,1)}, u32[]{:S(2)}, u32[]{:S(2)}) async-start(bf16[4,256,512]{2,1,0:T(8,128)(2,1)} %bitcast.306), calls=%async_computation.4 | async-start | bytes 2097152 | tf_op jit(solution)/shard_map/all_to_all | solution.py:114
  245.7 7.9 %all-to-all-done.4.do_ref = bf16[4,256,512]{2,1,0:T(8,128)(2,1)} async-done(((bf16[4,256,512]{2,1,0:T(8,128)(2,1)}), bf16[4,256,512]{2,1,0:T(8,128)(2,1)}, u32[]{:S(2)}, u32[]{:S(2)}) %all-to-all-start.4) | async-done | bytes 1048608 | tf_op jit(solution)/shard_map/all_to_all | solution.py:114
  267.6 21.4 %attend_back.2 = bf16[768,1024]{1,0:T(8,128)(2,1)S(1)} custom-call(bf16[768,1024]{1,0:T(8,128)(2,1)S(1)} %add_convert_fusion.2.q_ref.k_ref.v_ref, bf16[768,1024]{1,0:T(8,128)(2,1)S(1)} %add_convert_fusion.2.q_ref.k_ref.v_ref, bf16[768,1024]{1,0:T(8,128)(2,1)S(1)} %add_convert_fusion.2.q_ref.k_ref.v_ref, bf16[4,256,512]{2,1,0:T(8,128)(2,1)} %all-to-all-done.4.do_ref, ...), custom_call_target="tpu_custom_call" | custom-call | flops 1048576 | bytes 1048576 | tf_op jit(solution)/shard_map/attend_back/pallas_call | solution.py:198
  292.2 4.6 %all-to-all-start.5 = ((bf16[4,256,1024]{2,1,0:T(8,128)(2,1)}), bf16[4,256,1024]{2,1,0:T(8,128)(2,1)}, u32[]{:S(2)}, u32[]{:S(2)}) async-start(bf16[4,256,1024]{2,1,0:T(8,128)(2,1)} %bitcast.286), calls=%async_computation.5 | async-start | bytes 4194304 | tf_op jit(solution)/shard_map/all_to_all | solution.py:114
  306.3 5.1 %fusion.88 = f32[1024,768]{1,0:T(8,128)} fusion(bf16[1024,1024]{1,0:T(8,128)(2,1)} %bitcast.20, bf16[768,1024]{1,0:T(8,128)(2,1)S(1)} %copy-done.1), kind=kOutput, calls=%fused_computation.222 | convolution fusion | flops 1610612736 | bytes 6815744 | tf_op jit(solution)/shard_map/dot_general | solution.py:22
  311.4 21.5 %attend_back.3 = bf16[768,1024]{1,0:T(8,128)(2,1)S(1)} custom-call(bf16[768,1024]{1,0:T(8,128)(2,1)S(1)} %add_convert_fusion.1.q_ref.k_ref.v_ref, bf16[768,1024]{1,0:T(8,128)(2,1)S(1)} %add_convert_fusion.1.q_ref.k_ref.v_ref, bf16[768,1024]{1,0:T(8,128)(2,1)S(1)} %add_convert_fusion.1.q_ref.k_ref.v_ref, bf16[4,256,512]{2,1,0:T(8,128)(2,1)} %all-to-all-done.4.do_ref, ...), custom_call_target="tpu_custom_call" | custom-call | flops 1048576 | bytes 1048576 | tf_op jit(solution)/shard_map/attend_back/pallas_call | solution.py:198
  336.1 4.5 %add_convert_fusion = bf16[1024,768]{1,0:T(8,128)(2,1)S(1)} fusion(f32[1024,768]{1,0:T(8,128)} %fusion.88, bf16[1024,1024]{1,0:T(8,128)(2,1)} %bitcast.28, bf16[768,1024]{1,0:T(8,128)(2,1)S(1)} %attend_back.3), kind=kOutput, calls=%fused_computation.16 | convolution fusion | flops 1612185600 | bytes 8388608 | tf_op jit(solution)/shard_map/dot_general | solution.py:22
  342.5 3.3 convolution_convert_fusion.2
  356.9 9.3 %reduce-scatter.10.cloned.1.call-done = bf16[1,640,1024]{2,1,0:T(8,128)(2,1)} async-done(((bf16[4,640,1024]{2,1,0:T(8,128)(2,1)}), bf16[1,640,1024]{2,1,0:T(8,128)(2,1)}) %reduce-scatter.10.cloned.1.call-update) | async-done | bytes 1310736
  366.3 4.7 %collective-permute-start.26 = (bf16[4,40,768]{2,1,0:T(8,128)(2,1)S(1)}, bf16[4,40,768]{2,1,0:T(8,128)(2,1)S(1)}, u32[]{:S(2)}, u32[]{:S(2)}) collective-permute-start(bf16[4,40,768]{2,1,0:T(8,128)(2,1)S(1)} %get-tuple-element.194), channel_id=1, source_target_pairs={{0,2},{1,3},{2,0},{3,1},{4,6},{5,7},{6,4},{7,5},{8,10},{9,11},{10,... | collective-permute-start | bytes 737288 | tf_op jit(solution)/shard_map/ppermute | solution.py:27
  376.0 16.4 %collective-permute-done.26 = bf16[4,40,768]{2,1,0:T(8,128)(2,1)S(1)} collective-permute-done((bf16[4,40,768]{2,1,0:T(8,128)(2,1)S(1)}, bf16[4,40,768]{2,1,0:T(8,128)(2,1)S(1)}, u32[]{:S(2)}, u32[]{:S(2)}) %collective-permute-start.26) | collective-permute-done | bytes 245792 | tf_op jit(solution)/shard_map/ppermute | solution.py:27
  (343 shorter events, 156.0 us)
Async XLA Ops:
  7.2 158.9 %all-gather.3.cloned.1.call-start = ((), (), s32[]{:S(2)}) async-start(), calls=%async_computation.11 | async-start | bytes 8912896 | tf_op jit(solution)/shard_map/all_gather | solution.py:314
  21.7 10.2 %collective-permute-start.3 = (bf16[4,40,768]{2,1,0:T(8,128)(2,1)S(1)}, bf16[4,40,768]{2,1,0:T(8,128)(2,1)S(1)}, u32[]{:S(2)}, u32[]{:S(2)}) collective-permute-start(bf16[4,40,768]{2,1,0:T(8,128)(2,1)S(1)} %bitcast_dynamic-update-slice_fusion.12), channel_id=1, source_target_pairs={{0,2},{1,3},{2,0},{3,1},{4,6},{5,7},{6,4},{7,5},{8,10},{9,11},{10,... | collective-permute-start | bytes 737288 | tf_op jit(solution)/shard_map/ppermute | solution.py:27
  23.1 17.5 %collective-permute-start.4 = (bf16[4,40,768]{2,1,0:T(8,128)(2,1)S(1)}, bf16[4,40,768]{2,1,0:T(8,128)(2,1)S(1)}, u32[]{:S(2)}, u32[]{:S(2)}) collective-permute-start(bf16[4,40,768]{2,1,0:T(8,128)(2,1)S(1)} %bitcast_dynamic-update-slice_fusion.12), channel_id=1, source_target_pairs={{0,4},{1,5},{2,6},{3,7},{4,0},{5,1},{6,2},{7,3},{8,12},{9,13},{10,... | collective-permute-start | bytes 737288 | tf_op jit(solution)/shard_map/ppermute | solution.py:27
  25.5 25.7 %collective-permute-start.5 = (bf16[4,40,768]{2,1,0:T(8,128)(2,1)S(1)}, bf16[4,40,768]{2,1,0:T(8,128)(2,1)S(1)}, u32[]{:S(2)}, u32[]{:S(2)}) collective-permute-start(bf16[4,40,768]{2,1,0:T(8,128)(2,1)S(1)} %bitcast_dynamic-update-slice_fusion.12), channel_id=1, source_target_pairs={{0,6},{1,7},{2,4},{3,5},{4,2},{5,3},{6,0},{7,1},{8,14},{9,15},{10,... | collective-permute-start | bytes 737288 | tf_op jit(solution)/shard_map/ppermute | solution.py:27
  27.1 32.9 %all-to-all-start = ((bf16[4,256,1024]{2,1,0:T(8,128)(2,1)}), bf16[4,256,1024]{2,1,0:T(8,128)(2,1)}, u32[]{:S(2)}, u32[]{:S(2)}) async-start(bf16[4,256,1024]{2,1,0:T(8,128)(2,1)} %broadcast_in_dim.147), calls=%async_computation | async-start | bytes 4194304 | tf_op jit(solution)/shard_map/all_to_all | solution.py:114
  51.3 6.6 %collective-permute-start.6 = (bf16[4,4,40,768]{3,2,0,1:T(8,128)(2,1)S(1)}, bf16[4,4,40,768]{3,2,0,1:T(8,128)(2,1)S(1)}, u32[]{:S(2)}, u32[]{:S(2)}) collective-permute-start(bf16[4,4,40,768]{3,2,0,1:T(8,128)(2,1)S(1)} %bitcast_dynamic-update-slice_fusion.7), channel_id=1, source_target_pairs={{0,1},{1,0},{2,3},{3,2},{4,5},{5,4},{6,7},{7,6},{8,9},{9,8},{10,11... | collective-permute-start | bytes 2949128 | tf_op jit(solution)/shard_map/ppermute | solution.py:27
  61.7 39.5 %all-to-all-start.2 = ((bf16[4,256,1024]{2,1,0:T(8,128)(2,1)}), bf16[4,256,1024]{2,1,0:T(8,128)(2,1)}, u32[]{:S(2)}, u32[]{:S(2)}) async-start(bf16[4,256,1024]{2,1,0:T(8,128)(2,1)} %broadcast_in_dim.149), calls=%async_computation.2 | async-start | bytes 4194304 | tf_op jit(solution)/shard_map/all_to_all | solution.py:114
  83.3 8.8 %collective-permute-start.7 = (bf16[32,1024]{1,0:T(8,128)(2,1)S(1)}, bf16[32,1024]{1,0:T(8,128)(2,1)S(1)}, u32[]{:S(2)}, u32[]{:S(2)}) collective-permute-start(bf16[32,1024]{1,0:T(8,128)(2,1)S(1)} %copy-done.40), channel_id=1, source_target_pairs={{0,2},{1,3},{2,0},{3,1},{4,6},{5,7},{6,4},{7,5},{8,10},{9,11},{10,... | collective-permute-start | bytes 196616 | tf_op jit(solution)/shard_map/ppermute | solution.py:27
  88.1 9.9 %collective-permute-start.9 = (bf16[32,1024]{1,0:T(8,128)(2,1)S(1)}, bf16[32,1024]{1,0:T(8,128)(2,1)S(1)}, u32[]{:S(2)}, u32[]{:S(2)}) collective-permute-start(bf16[32,1024]{1,0:T(8,128)(2,1)S(1)} %copy-done.40), channel_id=1, source_target_pairs={{0,6},{1,7},{2,4},{3,5},{4,2},{5,3},{6,0},{7,1},{8,14},{9,15},{10,... | collective-permute-start | bytes 196616 | tf_op jit(solution)/shard_map/ppermute | solution.py:27
  98.0 19.4 %collective-permute-start.10 = (bf16[4,32,1024]{2,1,0:T(8,128)(2,1)S(1)}, bf16[4,32,1024]{2,1,0:T(8,128)(2,1)}, u32[]{:S(2)}, u32[]{:S(2)}) collective-permute-start(bf16[4,32,1024]{2,1,0:T(8,128)(2,1)S(1)} %bitcast_dynamic-update-slice_fusion.8), channel_id=1, source_target_pairs={{0,8},{8,0},{16,24},{24,16},{1,9},{9,1},{17,25},{25,17},{2,10},{10... | collective-permute-start | bytes 786440 | tf_op jit(solution)/shard_map/ppermute | solution.py:27
  99.9 17.6 %collective-permute-start.11 = (bf16[4,32,1024]{2,1,0:T(8,128)(2,1)S(1)}, bf16[4,32,1024]{2,1,0:T(8,128)(2,1)}, u32[]{:S(2)}, u32[]{:S(2)}) collective-permute-start(bf16[4,32,1024]{2,1,0:T(8,128)(2,1)S(1)} %bitcast_dynamic-update-slice_fusion.8), channel_id=1, source_target_pairs={{0,16},{8,24},{16,0},{24,8},{1,17},{9,25},{17,1},{25,9},{2,18},{10... | collective-permute-start | bytes 786440 | tf_op jit(solution)/shard_map/ppermute | solution.py:27
  101.2 16.3 %collective-permute-start.12 = (bf16[4,32,1024]{2,1,0:T(8,128)(2,1)S(1)}, bf16[4,32,1024]{2,1,0:T(8,128)(2,1)}, u32[]{:S(2)}, u32[]{:S(2)}) collective-permute-start(bf16[4,32,1024]{2,1,0:T(8,128)(2,1)S(1)} %bitcast_dynamic-update-slice_fusion.8), channel_id=1, source_target_pairs={{0,24},{8,16},{16,8},{24,0},{1,25},{9,17},{17,9},{25,1},{2,26},{10... | collective-permute-start | bytes 786440 | tf_op jit(solution)/shard_map/ppermute | solution.py:27
  124.3 26.1 %collective-permute-start.13 = (bf16[4,4,32,1024]{3,2,1,0:T(8,128)(2,1)}, bf16[4,4,32,1024]{3,2,1,0:T(8,128)(2,1)}, u32[]{:S(2)}, u32[]{:S(2)}) collective-permute-start(bf16[4,4,32,1024]{3,2,1,0:T(8,128)(2,1)} %bitcast_dynamic-update-slice_fusion), channel_id=1, source_target_pairs={{0,1},{1,0},{2,3},{3,2},{4,5},{5,4},{6,7},{7,6},{8,9},{9,8},{10,11... | collective-permute-start | bytes 3145736 | tf_op jit(solution)/shard_map/ppermute | solution.py:27
  145.9 11.7 %all-to-all-start.3 = ((bf16[4,256,256]{2,1,0:T(8,128)(2,1)}), bf16[4,256,256]{2,1,0:T(8,128)(2,1)}, u32[]{:S(2)}, u32[]{:S(2)}) async-start(bf16[4,256,256]{2,1,0:T(8,128)(2,1)} %copy-done.9), calls=%async_computation.3 | async-start | bytes 1048576 | tf_op jit(solution)/shard_map/all_to_all | solution.py:114
  150.1 150.7 %reduce-scatter.6.cloned.1.call-start = ((), (), s32[]{:S(2)}) async-start(), calls=%async_computation.9 | async-start | bytes 5242880 | tf_op jit(solution)/shard_map/reduce_scatter | solution.py:368
  162.9 8.6 %collective-permute-start.14 = (bf16[512,1024]{1,0:T(8,128)(2,1)}, bf16[512,1024]{1,0:T(8,128)(2,1)}, u32[]{:S(2)}, u32[]{:S(2)}) collective-permute-start(bf16[512,1024]{1,0:T(8,128)(2,1)} %fusion.32), channel_id=1, source_target_pairs={{0,1},{1,0},{2,3},{3,2},{4,5},{5,4},{6,7},{7,6},{8,9},{9,8},{10,11... | collective-permute-start | bytes 3145736 | tf_op jit(solution)/shard_map/ppermute | solution.py:27
  232.9 20.7 %all-to-all-start.4 = ((bf16[4,256,512]{2,1,0:T(8,128)(2,1)}), bf16[4,256,512]{2,1,0:T(8,128)(2,1)}, u32[]{:S(2)}, u32[]{:S(2)}) async-start(bf16[4,256,512]{2,1,0:T(8,128)(2,1)} %bitcast.306), calls=%async_computation.4 | async-start | bytes 2097152 | tf_op jit(solution)/shard_map/all_to_all | solution.py:114
  237.2 129.0 %reduce-scatter.10.cloned.1.call-start = ((), (), s32[]{:S(2)}) async-start(), calls=%async_computation.12 | async-start | bytes 6553600
  256.7 6.3 %collective-permute-start.32 = (bf16[4,4,32,1024]{3,2,1,0:T(8,128)(2,1)S(1)}, bf16[4,4,32,1024]{3,2,1,0:T(8,128)(2,1)S(1)}, u32[]{:S(2)}, u32[]{:S(2)}) collective-permute-start(bf16[4,4,32,1024]{3,2,1,0:T(8,128)(2,1)S(1)} %dynamic-slice_bitcast_fusion), channel_id=1, source_target_pairs={{0,1},{1,0},{2,3},{3,2},{4,5},{5,4},{6,7},{7,6},{8,9},{9,8},{10,11... | collective-permute-start | bytes 3145736 | tf_op jit(solution)/shard_map/ppermute | solution.py:27
  292.2 43.0 %all-to-all-start.5 = ((bf16[4,256,1024]{2,1,0:T(8,128)(2,1)}), bf16[4,256,1024]{2,1,0:T(8,128)(2,1)}, u32[]{:S(2)}, u32[]{:S(2)}) async-start(bf16[4,256,1024]{2,1,0:T(8,128)(2,1)} %bitcast.286), calls=%async_computation.5 | async-start | bytes 4194304 | tf_op jit(solution)/shard_map/all_to_all | solution.py:114
  296.8 107.2 %reduce-scatter.8.cloned.1.call-start = ((), (), s32[]{:S(2)}) async-start(), calls=%async_computation.10 | async-start | bytes 1638400 | tf_op jit(solution)/shard_map/reduce_scatter | solution.py:438
  302.8 32.4 %collective-permute-start.19 = (bf16[128,1024]{1,0:T(8,128)(2,1)}, bf16[128,1024]{1,0:T(8,128)(2,1)}, u32[]{:S(2)}, u32[]{:S(2)}) collective-permute-start(bf16[128,1024]{1,0:T(8,128)(2,1)} %get-tuple-element.191), channel_id=1, source_target_pairs={{0,2},{1,3},{2,0},{3,1},{4,6},{5,7},{6,4},{7,5},{8,10},{9,11},{10,... | collective-permute-start | bytes 786440 | tf_op jit(solution)/shard_map/ppermute | solution.py:27
  304.0 31.2 %collective-permute-start.20 = (bf16[128,1024]{1,0:T(8,128)(2,1)}, bf16[128,1024]{1,0:T(8,128)(2,1)}, u32[]{:S(2)}, u32[]{:S(2)}) collective-permute-start(bf16[128,1024]{1,0:T(8,128)(2,1)} %get-tuple-element.190), channel_id=1, source_target_pairs={{0,4},{1,5},{2,6},{3,7},{4,0},{5,1},{6,2},{7,3},{8,12},{9,13},{10,... | collective-permute-start | bytes 786440 | tf_op jit(solution)/shard_map/ppermute | solution.py:27
  306.1 29.1 %collective-permute-start.21 = (bf16[128,1024]{1,0:T(8,128)(2,1)S(1)}, bf16[128,1024]{1,0:T(8,128)(2,1)}, u32[]{:S(2)}, u32[]{:S(2)}) collective-permute-start(bf16[128,1024]{1,0:T(8,128)(2,1)S(1)} %get-tuple-element.189), channel_id=1, source_target_pairs={{0,6},{1,7},{2,4},{3,5},{4,2},{5,3},{6,0},{7,1},{8,14},{9,15},{10,... | collective-permute-start | bytes 786440 | tf_op jit(solution)/shard_map/ppermute | solution.py:27
  341.7 7.9 %collective-permute-start.25 = (bf16[4,4,40,768]{3,2,0,1:T(8,128)(2,1)}, bf16[4,4,40,768]{3,2,0,1:T(8,128)(2,1)}, u32[]{:S(2)}, u32[]{:S(2)}) collective-permute-start(bf16[4,4,40,768]{3,2,0,1:T(8,128)(2,1)} %bitcast.259), channel_id=1, source_target_pairs={{0,1},{1,0},{2,3},{3,2},{4,5},{5,4},{6,7},{7,6},{8,9},{9,8},{10,11... | collective-permute-start | bytes 2949128 | tf_op jit(solution)/shard_map/ppermute | solution.py:27
  347.0 46.6 %collective-permute-start.22 = (bf16[256,1024]{1,0:T(8,128)(2,1)}, bf16[256,1024]{1,0:T(8,128)(2,1)S(1)}, u32[]{:S(2)}, u32[]{:S(2)}) collective-permute-start(bf16[256,1024]{1,0:T(8,128)(2,1)} %get-tuple-element.185), channel_id=1, source_target_pairs={{0,8},{8,0},{16,24},{24,16},{1,9},{9,1},{17,25},{25,17},{2,10},{10... | collective-permute-start | bytes 1572872 | tf_op jit(solution)/shard_map/ppermute | solution.py:27
  348.2 45.4 %collective-permute-start.23 = (bf16[256,1024]{1,0:T(8,128)(2,1)}, bf16[256,1024]{1,0:T(8,128)(2,1)}, u32[]{:S(2)}, u32[]{:S(2)}) collective-permute-start(bf16[256,1024]{1,0:T(8,128)(2,1)} %get-tuple-element.184), channel_id=1, source_target_pairs={{0,16},{8,24},{16,0},{24,8},{1,17},{9,25},{17,1},{25,9},{2,18},{10... | collective-permute-start | bytes 1572872 | tf_op jit(solution)/shard_map/ppermute | solution.py:27
  349.0 44.6 %collective-permute-start.24 = (bf16[256,1024]{1,0:T(8,128)(2,1)}, bf16[256,1024]{1,0:T(8,128)(2,1)}, u32[]{:S(2)}, u32[]{:S(2)}) collective-permute-start(bf16[256,1024]{1,0:T(8,128)(2,1)} %get-tuple-element.183), channel_id=1, source_target_pairs={{0,24},{8,16},{16,8},{24,0},{1,25},{9,17},{17,9},{25,1},{2,26},{10... | collective-permute-start | bytes 1572872 | tf_op jit(solution)/shard_map/ppermute | solution.py:27
  351.9 14.3 %collective-permute-start.28 = (bf16[4,40,768]{2,1,0:T(8,128)(2,1)}, bf16[4,40,768]{2,1,0:T(8,128)(2,1)}, u32[]{:S(2)}, u32[]{:S(2)}) collective-permute-start(bf16[4,40,768]{2,1,0:T(8,128)(2,1)} %get-tuple-element.195), channel_id=1, source_target_pairs={{0,6},{1,7},{2,4},{3,5},{4,2},{5,3},{6,0},{7,1},{8,14},{9,15},{10,... | collective-permute-start | bytes 737288 | tf_op jit(solution)/shard_map/ppermute | solution.py:27
  356.9 19.2 %collective-permute-start.27 = (bf16[4,40,768]{2,1,0:T(8,128)(2,1)}, bf16[4,40,768]{2,1,0:T(8,128)(2,1)}, u32[]{:S(2)}, u32[]{:S(2)}) collective-permute-start(bf16[4,40,768]{2,1,0:T(8,128)(2,1)} %get-tuple-element.196), channel_id=1, source_target_pairs={{0,4},{1,5},{2,6},{3,7},{4,0},{5,1},{6,2},{7,3},{8,12},{9,13},{10,... | collective-permute-start | bytes 737288 | tf_op jit(solution)/shard_map/ppermute | solution.py:27
  366.3 26.1 %collective-permute-start.26 = (bf16[4,40,768]{2,1,0:T(8,128)(2,1)S(1)}, bf16[4,40,768]{2,1,0:T(8,128)(2,1)S(1)}, u32[]{:S(2)}, u32[]{:S(2)}) collective-permute-start(bf16[4,40,768]{2,1,0:T(8,128)(2,1)S(1)} %get-tuple-element.194), channel_id=1, source_target_pairs={{0,2},{1,3},{2,0},{3,1},{4,6},{5,7},{6,4},{7,5},{8,10},{9,11},{10,... | collective-permute-start | bytes 737288 | tf_op jit(solution)/shard_map/ppermute | solution.py:27
  393.7 6.0 %collective-permute-start.29 = (bf16[40,768]{1,0:T(8,128)(2,1)S(1)}, bf16[40,768]{1,0:T(8,128)(2,1)S(1)}, u32[]{:S(2)}, u32[]{:S(2)}) collective-permute-start(bf16[40,768]{1,0:T(8,128)(2,1)S(1)} %get-tuple-element.216), channel_id=1, source_target_pairs={{0,8},{8,0},{16,24},{24,16},{1,9},{9,1},{17,25},{25,17},{2,10},{10... | collective-permute-start | bytes 184328 | tf_op jit(solution)/shard_map/ppermute | solution.py:27
  (66 other events, 386.8 us)
Sparse Core Ops, SparseCore 0:
  12.6 153.4 all-gather.2
  212.7 60.0 reduce-scatter.5
  276.1 90.0 reduce-scatter.9
  368.5 35.4 reduce-scatter.7

commit v7 on v6

--- a/solution.py
+++ b/solution.py
@@ -323,7 +323,7 @@
             lax.dynamic_slice_in_dim(value_bias, me * cols, cols),
         ]
     ).astype(F32)[:, None]
-    segs, qkvs, lses, mixed = [], [], [], []
+    segs, qkvs, lses = [], [], []
     outs = []
     for g in range(groups):
         segs.append(segment_ids(lengths[g], key_pos))
@@ -332,12 +332,12 @@
         o, lse = attend(qkvs[g], segs[g], ctx_rows)
         outs.append(o)
         lses.append(lse)
-        mixed.append(exchange_ctx(o if g == 0 else after(o, mixed[-1])))
     out_c = send_ctx([place(gather_z(after(w_out, outs[0])), me_z)] * nc)
     out_mat = place(after(out_c, outs[-1]), me_c)
     out_mat = in_order(out_mat, core_swap(out_mat), core, 2).reshape(width, width)
-    own = after(own, mixed[-1])
-    mixed = jnp.concatenate([t.reshape(width, ctx_rows) for t in mixed], axis=1)
+    mixed = exchange_ctx(jnp.concatenate(outs, axis=2))
+    own = after(own, mixed)
+    mixed = mixed.reshape(width, flat_rows)
     n_up = 2 * rows_w * parts
     up_mat = jnp.concatenate(
         [own[:, j * 2 * rows_w : (j + 1) * 2 * rows_w].reshape(width, width) for j in range(parts)], axis=1
@@ -376,7 +376,7 @@
     grad_out_bias = jnp.sum(grad_attended.astype(F32), axis=0)
     do_all = exchange_ctx(dot(out_mat, grad_attended, 1, 1).astype(BF).reshape(nc, cols, flat_rows))
     later = after((both_first, grad_hidden, mixed, grad_attended), do_all)
-    grad_out = dot(later[2], later[3], 1, 0).astype(BF).reshape(nc, nz, 2, rows_w, width)
+    grad_out = dot(mixed, grad_attended, 1, 0).astype(BF).reshape(nc, nz, 2, rows_w, width)
     grad_ups = [
         dot(later[0], later[1][:, j * width : (j + 1) * width], 0, 0).astype(BF) for j in range(parts)
     ]

time: 422 us -> 427 us (1.012)
  waiting for transfers between devices: 81 us -> 101 us
  blocking collectives: 18.3 us -> 0 us
    all_to_all x1 -> x0, blocking collectives: 18.3 us -> none  [exchange_ctx(): return lax.all_to_all(x, 'ctx', 0, 0)]
    all_gather x1, waiting for transfers between devices: 0.97 us -> 11.6 us  [body(): own = lax.all_gather(own, BOTH, axis=0, axis_index_groups=core_groups())]
    all_to_all x5, waiting for transfers between devices: 13.1 us -> 22.3 us  [exchange_ctx(): return lax.all_to_all(x, 'ctx', 0, 0)]
  transfers between devices with their start and end apart: 43 -> 43, of which waited for: 21 -> 21; matrix products, arithmetic and copies ran while one was open for 28% -> 29% of each run, Pallas kernels for 16% -> 16%
where the time goes in v7:
time: 427 us; the launch traced here: 421 us
  waiting for transfers between devices  101 us (24%)
  matrix products  85.2 us (20%)
  starting transfers between devices  68.5 us (16%)
  Pallas kernels  67.2 us (16%)
  other arithmetic  42.1 us (10%)
  local copies, waits for them, and re-layouts  41.3 us (10%)
  between operations  15.7 us (4%)
    dot_general x20, matrix products, dot(): lax.dot_general(a, b, (((ca,), (cb,)), ((), ())), preferred_element_type=...  85.2 us
    ppermute x34, waiting for transfers between devices, swap(): return lax.ppermute(x, axis, [(i, i ^ r) for i in range(n)])  56 us
    ppermute x34, starting transfers between devices, swap(): return lax.ppermute(x, axis, [(i, i ^ r) for i in range(n)])  45.7 us
    pallas_call x2, Pallas kernels, attend_back(): pl.pallas_call(functools.partial(attend_back_kernel, heads, nq, block), g...  42.9 us
    pallas_call x2, Pallas kernels, attend(): pl.pallas_call(attend_kernel, grid=(heads, nq), in_specs=[pl.BlockSpec((H...  24.3 us
    all_to_all x5, waiting for transfers between devices, exchange_ctx(): return lax.all_to_all(x, 'ctx', 0, 0)  22.3 us
    all_to_all x5, starting transfers between devices, exchange_ctx(): return lax.all_to_all(x, 'ctx', 0, 0)  22.2 us
    all_gather x1, waiting for transfers between devices, body(): own = lax.all_gather(own, BOTH, axis=0, axis_index_groups=core_groups())  11.6 us
  transfers between devices with their start and end apart: 43, of which 21 were waited for; matrix products, arithmetic and copies ran while one was open for 29% of the time, Pallas kernels for 16%

profile of v7, /device:TPU:1, one launch (start us, length us, event | category | flops | bytes accessed | tf_op | source)
XLA Modules:
  0.0 420.7 jit_solution(11421144164573650248)
XLA Ops:
  27.1 4.5 %all-to-all-start = ((bf16[4,256,1024]{2,1,0:T(8,128)(2,1)}), bf16[4,256,1024]{2,1,0:T(8,128)(2,1)}, u32[]{:S(2)}, u32[]{:S(2)}) async-start(bf16[4,256,1024]{2,1,0:T(8,128)(2,1)} %broadcast_in_dim.147), calls=%async_computation | async-start | bytes 4194304 | tf_op jit(solution)/shard_map/all_to_all | solution.py:114
  31.8 8.8 %collective-permute-done.4 = bf16[4,40,768]{2,1,0:T(8,128)(2,1)S(1)} collective-permute-done((bf16[4,40,768]{2,1,0:T(8,128)(2,1)S(1)}, bf16[4,40,768]{2,1,0:T(8,128)(2,1)S(1)}, u32[]{:S(2)}, u32[]{:S(2)}) %collective-permute-start.4) | collective-permute-done | bytes 245792 | tf_op jit(solution)/shard_map/ppermute | solution.py:27
  40.6 10.6 %collective-permute-done.5 = bf16[4,40,768]{2,1,0:T(8,128)(2,1)S(1)} collective-permute-done((bf16[4,40,768]{2,1,0:T(8,128)(2,1)S(1)}, bf16[4,40,768]{2,1,0:T(8,128)(2,1)S(1)}, u32[]{:S(2)}, u32[]{:S(2)}) %collective-permute-start.5) | collective-permute-done | bytes 245792 | tf_op jit(solution)/shard_map/ppermute | solution.py:27
  51.3 4.4 %collective-permute-start.6 = (bf16[4,4,40,768]{3,2,0,1:T(8,128)(2,1)S(1)}, bf16[4,4,40,768]{3,2,0,1:T(8,128)(2,1)S(1)}, u32[]{:S(2)}, u32[]{:S(2)}) collective-permute-start(bf16[4,4,40,768]{3,2,0,1:T(8,128)(2,1)S(1)} %bitcast_dynamic-update-slice_fusion.7), channel_id=1, source_target_pairs={{0,1},{1,0},{2,3},{3,2},{4,5},{5,4},{6,7},{7,6},{8,9},{9,8},{10,11... | collective-permute-start | bytes 2949128 | tf_op jit(solution)/shard_map/ppermute | solution.py:27
  61.7 4.7 %all-to-all-start.1 = ((bf16[4,256,1024]{2,1,0:T(8,128)(2,1)}), bf16[4,256,1024]{2,1,0:T(8,128)(2,1)}, u32[]{:S(2)}, u32[]{:S(2)}) async-start(bf16[4,256,1024]{2,1,0:T(8,128)(2,1)} %broadcast_in_dim.149), calls=%async_computation.1 | async-start | bytes 4194304 | tf_op jit(solution)/shard_map/all_to_all | solution.py:114
  66.3 4.0 add_convert_fusion.2.q_ref.k_ref.v_ref
  70.4 12.1 %attend.2 = (bf16[4,256,256]{2,1,0:T(8,128)(2,1)S(1)}, f32[4,1,1024]{2,1,0:T(1,128)S(1)}) custom-call(bf16[768,1024]{1,0:T(8,128)(2,1)S(1)} %add_convert_fusion.2.q_ref.k_ref.v_ref, bf16[768,1024]{1,0:T(8,128)(2,1)S(1)} %add_convert_fusion.2.q_ref.k_ref.v_ref, bf16[768,1024]{1,0:T(8,128)(2,1)S(1)} %add_convert_fusion.2.q_ref.k_ref.v_ref, ...), custom_call_target="tpu_custom_call" | custom-call | flops 12582912000 | bytes 1048576 | tf_op jit(solution)/shard_map/attend/pallas_call | solution.py:134
  83.3 4.2 collective-permute-start.7
  93.3 4.7 %collective-permute-done.9 = bf16[32,1024]{1,0:T(8,128)(2,1)S(1)} collective-permute-done((bf16[32,1024]{1,0:T(8,128)(2,1)S(1)}, bf16[32,1024]{1,0:T(8,128)(2,1)S(1)}, u32[]{:S(2)}, u32[]{:S(2)}) %collective-permute-start.9) | collective-permute-done | bytes 65568 | tf_op jit(solution)/shard_map/ppermute | solution.py:27
  101.2 4.0 add_convert_fusion.1.q_ref.k_ref.v_ref
  105.2 12.2 %attend.3 = (bf16[4,256,256]{2,1,0:T(8,128)(2,1)S(1)}, f32[4,1,1024]{2,1,0:T(1,128)S(1)}) custom-call(bf16[768,1024]{1,0:T(8,128)(2,1)S(1)} %add_convert_fusion.1.q_ref.k_ref.v_ref, bf16[768,1024]{1,0:T(8,128)(2,1)S(1)} %add_convert_fusion.1.q_ref.k_ref.v_ref, bf16[768,1024]{1,0:T(8,128)(2,1)S(1)} %add_convert_fusion.1.q_ref.k_ref.v_ref, ...), custom_call_target="tpu_custom_call" | custom-call | flops 12582912000 | bytes 1048576 | tf_op jit(solution)/shard_map/attend/pallas_call | solution.py:134
  128.8 4.3 %all-to-all-start.2 = ((bf16[4,256,512]{2,1,0:T(8,128)(2,1)}), bf16[4,256,512]{2,1,0:T(8,128)(2,1)}, u32[]{:S(2)}, u32[]{:S(2)}) async-start(bf16[4,256,512]{2,1,0:T(8,128)(2,1)} %pad_maximum_fusion.9), calls=%async_computation.2 | async-start | bytes 2097152 | tf_op jit(solution)/shard_map/all_to_all | solution.py:114
  133.4 4.0 maximum_select_fusion
  137.4 16.3 %all-to-all-done.2 = bf16[4,256,512]{2,1,0:T(8,128)(2,1)} async-done(((bf16[4,256,512]{2,1,0:T(8,128)(2,1)}), bf16[4,256,512]{2,1,0:T(8,128)(2,1)}, u32[]{:S(2)}, u32[]{:S(2)}) %all-to-all-start.2) | async-done | bytes 1048608 | tf_op jit(solution)/shard_map/all_to_all | solution.py:114
  153.6 3.5 fusion.85
  160.2 11.6 %all-gather.3.cloned.1.call-done = bf16[4096,1024]{1,0:T(8,128)(2,1)} async-done(((bf16[256,1024]{1,0:T(8,128)(2,1)}), bf16[4096,1024]{1,0:T(8,128)(2,1)}) %all-gather.3.cloned.1.call-update) | async-done | bytes 8388624 | tf_op jit(solution)/shard_map/all_gather | solution.py:314
  177.1 12.6 %fusion.4 = (bf16[1024,2048]{1,0:T(8,128)(2,1)}, bf16[1024,2048]{1,0:T(8,128)(2,1)S(1)}) fusion(f32[2048]{0:T(1024)S(1)} %bitcast.320, bf16[1024,1024]{1,0:T(8,128)(2,1)S(1)} %bitcast.289, bf16[1024,1024]{1,0:T(8,128)(2,1)S(1)} %bitcast.286, bf16[512,1024]{1,0:T(8,128)(2,1)} %collective-permute-done.14, bf16[512,1024]{1,0:T(8,128)(2,1)} %fusion.32), kind=kOutput, calls=%fused_computation.5 | convolution fusion | flops 4332716032 | bytes 14688256 | tf_op jit(solution)/shard_map/dot_general | solution.py:22
  196.6 6.5 %fusion.80 = (f32[512]{0:T(512)S(1)}, f32[512,1024]{1,0:T(8,128)S(1)}) fusion(f32[1024]{0:T(1024)S(1)} %reshape.595, bf16[512,1024]{1,0:T(8,128)(2,1)} %collective-permute-done.16, f32[1024]{0:T(1024)S(1)} %reshape.593, f32[1024]{0:T(1024)S(1)} %reshape.592, f32[512]{0:T(512)S(1)} %add_rsqrt_fusion.1, f32[512,1024]{1,0:T(8,128)} %copy-done.9, ...), kind=kOutput, calls=%fused_computation.216 | convolution fusion | flops 2152201728 | bytes 11552768 | tf_op jit(solution)/shard_map/dot_general | solution.py:22
  211.8 6.4 %convolution_convert_fusion = bf16[2048,1024]{1,0:T(8,128)(2,1)} fusion(bf16[1024,2048]{1,0:T(8,128)(2,1)S(1)} %copy-done.53, bf16[512,1024]{1,0:T(8,128)(2,1)S(1)} %collective-permute-done.17, bf16[512,1024]{1,0:T(8,128)(2,1)S(1)} %get-tuple-element.165), kind=kOutput, calls=%fused_computation.13 | convolution fusion | flops 4301258752 | bytes 10485760 | tf_op jit(solution)/shard_map/dot_general | solution.py:22
  218.3 5.7 %multiply_convert_fusion.1 = bf16[512,2048]{1,0:T(8,128)(2,1)S(1)} fusion(bf16[512,1024]{1,0:T(8,128)(2,1)} %copy-done.51, bf16[2048,1024]{1,0:T(8,128)(2,1)} %bitcast.275, bf16[1024,2048]{1,0:T(8,128)(2,1)} %get-tuple-element.172), kind=kOutput, calls=%fused_computation.11 | convolution fusion | flops 2150629376 | bytes 9437184 | tf_op jit(solution)/shard_map/dot_general | solution.py:22
  240.3 4.2 %all-to-all-start.3 = ((bf16[4,256,512]{2,1,0:T(8,128)(2,1)}), bf16[4,256,512]{2,1,0:T(8,128)(2,1)}, u32[]{:S(2)}, u32[]{:S(2)}) async-start(bf16[4,256,512]{2,1,0:T(8,128)(2,1)} %bitcast.304), calls=%async_computation.3 | async-start | bytes 2097152 | tf_op jit(solution)/shard_map/all_to_all | solution.py:114
  244.8 4.9 %pad_maximum_fusion.2 = bf16[1024,2048]{1,0:T(8,128)(2,1)} fusion(bf16[512,2048]{1,0:T(8,128)(2,1)} %copy-done.24, bf16[512,2048]{1,0:T(8,128)(2,1)} %copy-done.25), kind=kLoop, calls=%fused_computation.10 | loop fusion | flops 8388608 | bytes 8388608 | tf_op jit(solution)/shard_map/concatenate | solution.py:370
  254.7 4.7 %all-to-all-done.3.do_ref = bf16[4,256,512]{2,1,0:T(8,128)(2,1)} async-done(((bf16[4,256,512]{2,1,0:T(8,128)(2,1)}), bf16[4,256,512]{2,1,0:T(8,128)(2,1)}, u32[]{:S(2)}, u32[]{:S(2)}) %all-to-all-start.3) | async-done | bytes 1048608 | tf_op jit(solution)/shard_map/all_to_all | solution.py:114
  259.3 4.8 %fusion.29 = bf16[1024,1024]{1,0:T(8,128)(2,1)S(1)} fusion(bf16[1024,1024]{1,0:T(8,128)(2,1)} %pad_maximum_fusion.3, bf16[1024,2048]{1,0:T(8,128)(2,1)} %pad_maximum_fusion.2), kind=kOutput, calls=%fused_computation.66 | convolution fusion | flops 2148532224 | bytes 6291456 | tf_op jit(solution)/shard_map/dot_general | solution.py:22
  272.4 21.4 %attend_back.2 = bf16[768,1024]{1,0:T(8,128)(2,1)S(1)} custom-call(bf16[768,1024]{1,0:T(8,128)(2,1)S(1)} %add_convert_fusion.2.q_ref.k_ref.v_ref, bf16[768,1024]{1,0:T(8,128)(2,1)S(1)} %add_convert_fusion.2.q_ref.k_ref.v_ref, bf16[768,1024]{1,0:T(8,128)(2,1)S(1)} %add_convert_fusion.2.q_ref.k_ref.v_ref, bf16[4,256,512]{2,1,0:T(8,128)(2,1)} %all-to-all-done.3.do_ref, ...), custom_call_target="tpu_custom_call" | custom-call | flops 1048576 | bytes 1048576 | tf_op jit(solution)/shard_map/attend_back/pallas_call | solution.py:198
  297.0 4.6 %all-to-all-start.4 = ((bf16[4,256,1024]{2,1,0:T(8,128)(2,1)}), bf16[4,256,1024]{2,1,0:T(8,128)(2,1)}, u32[]{:S(2)}, u32[]{:S(2)}) async-start(bf16[4,256,1024]{2,1,0:T(8,128)(2,1)} %bitcast.284), calls=%async_computation.4 | async-start | bytes 4194304 | tf_op jit(solution)/shard_map/all_to_all | solution.py:114
  311.1 5.3 %fusion.88 = f32[1024,768]{1,0:T(8,128)} fusion(bf16[1024,1024]{1,0:T(8,128)(2,1)} %bitcast.20, bf16[768,1024]{1,0:T(8,128)(2,1)S(1)} %copy-done.1), kind=kOutput, calls=%fused_computation.222 | convolution fusion | flops 1610612736 | bytes 6815744 | tf_op jit(solution)/shard_map/dot_general | solution.py:22
  316.4 21.5 %attend_back.3 = bf16[768,1024]{1,0:T(8,128)(2,1)S(1)} custom-call(bf16[768,1024]{1,0:T(8,128)(2,1)S(1)} %add_convert_fusion.1.q_ref.k_ref.v_ref, bf16[768,1024]{1,0:T(8,128)(2,1)S(1)} %add_convert_fusion.1.q_ref.k_ref.v_ref, bf16[768,1024]{1,0:T(8,128)(2,1)S(1)} %add_convert_fusion.1.q_ref.k_ref.v_ref, bf16[4,256,512]{2,1,0:T(8,128)(2,1)} %all-to-all-done.3.do_ref, ...), custom_call_target="tpu_custom_call" | custom-call | flops 1048576 | bytes 1048576 | tf_op jit(solution)/shard_map/attend_back/pallas_call | solution.py:198
  340.4 4.5 %add_convert_fusion = bf16[1024,768]{1,0:T(8,128)(2,1)S(1)} fusion(f32[1024,768]{1,0:T(8,128)} %fusion.88, bf16[1024,1024]{1,0:T(8,128)(2,1)} %bitcast.27, bf16[768,1024]{1,0:T(8,128)(2,1)S(1)} %attend_back.3), kind=kOutput, calls=%fused_computation.16 | convolution fusion | flops 1612185600 | bytes 8388608 | tf_op jit(solution)/shard_map/dot_general | solution.py:22
  361.2 9.3 %reduce-scatter.10.cloned.1.call-done = bf16[1,640,1024]{2,1,0:T(8,128)(2,1)} async-done(((bf16[4,640,1024]{2,1,0:T(8,128)(2,1)}), bf16[1,640,1024]{2,1,0:T(8,128)(2,1)}) %reduce-scatter.10.cloned.1.call-update) | async-done | bytes 1310736
  370.5 4.7 %collective-permute-start.26 = (bf16[4,40,768]{2,1,0:T(8,128)(2,1)S(1)}, bf16[4,40,768]{2,1,0:T(8,128)(2,1)S(1)}, u32[]{:S(2)}, u32[]{:S(2)}) collective-permute-start(bf16[4,40,768]{2,1,0:T(8,128)(2,1)S(1)} %get-tuple-element.188), channel_id=1, source_target_pairs={{0,2},{1,3},{2,0},{3,1},{4,6},{5,7},{6,4},{7,5},{8,10},{9,11},{10,... | collective-permute-start | bytes 737288 | tf_op jit(solution)/shard_map/ppermute | solution.py:27
  380.3 16.4 %collective-permute-done.26 = bf16[4,40,768]{2,1,0:T(8,128)(2,1)S(1)} collective-permute-done((bf16[4,40,768]{2,1,0:T(8,128)(2,1)S(1)}, bf16[4,40,768]{2,1,0:T(8,128)(2,1)S(1)}, u32[]{:S(2)}, u32[]{:S(2)}) %collective-permute-start.26) | collective-permute-done | bytes 245792 | tf_op jit(solution)/shard_map/ppermute | solution.py:27
  (342 shorter events, 153.9 us)
Async XLA Ops:
  7.2 164.5 %all-gather.3.cloned.1.call-start = ((), (), s32[]{:S(2)}) async-start(), calls=%async_computation.10 | async-start | bytes 8912896 | tf_op jit(solution)/shard_map/all_gather | solution.py:314
  21.7 10.2 %collective-permute-start.3 = (bf16[4,40,768]{2,1,0:T(8,128)(2,1)S(1)}, bf16[4,40,768]{2,1,0:T(8,128)(2,1)S(1)}, u32[]{:S(2)}, u32[]{:S(2)}) collective-permute-start(bf16[4,40,768]{2,1,0:T(8,128)(2,1)S(1)} %bitcast_dynamic-update-slice_fusion.12), channel_id=1, source_target_pairs={{0,2},{1,3},{2,0},{3,1},{4,6},{5,7},{6,4},{7,5},{8,10},{9,11},{10,... | collective-permute-start | bytes 737288 | tf_op jit(solution)/shard_map/ppermute | solution.py:27
  23.1 17.5 %collective-permute-start.4 = (bf16[4,40,768]{2,1,0:T(8,128)(2,1)S(1)}, bf16[4,40,768]{2,1,0:T(8,128)(2,1)S(1)}, u32[]{:S(2)}, u32[]{:S(2)}) collective-permute-start(bf16[4,40,768]{2,1,0:T(8,128)(2,1)S(1)} %bitcast_dynamic-update-slice_fusion.12), channel_id=1, source_target_pairs={{0,4},{1,5},{2,6},{3,7},{4,0},{5,1},{6,2},{7,3},{8,12},{9,13},{10,... | collective-permute-start | bytes 737288 | tf_op jit(solution)/shard_map/ppermute | solution.py:27
  25.5 25.7 %collective-permute-start.5 = (bf16[4,40,768]{2,1,0:T(8,128)(2,1)S(1)}, bf16[4,40,768]{2,1,0:T(8,128)(2,1)S(1)}, u32[]{:S(2)}, u32[]{:S(2)}) collective-permute-start(bf16[4,40,768]{2,1,0:T(8,128)(2,1)S(1)} %bitcast_dynamic-update-slice_fusion.12), channel_id=1, source_target_pairs={{0,6},{1,7},{2,4},{3,5},{4,2},{5,3},{6,0},{7,1},{8,14},{9,15},{10,... | collective-permute-start | bytes 737288 | tf_op jit(solution)/shard_map/ppermute | solution.py:27
  27.1 32.9 %all-to-all-start = ((bf16[4,256,1024]{2,1,0:T(8,128)(2,1)}), bf16[4,256,1024]{2,1,0:T(8,128)(2,1)}, u32[]{:S(2)}, u32[]{:S(2)}) async-start(bf16[4,256,1024]{2,1,0:T(8,128)(2,1)} %broadcast_in_dim.147), calls=%async_computation | async-start | bytes 4194304 | tf_op jit(solution)/shard_map/all_to_all | solution.py:114
  51.3 6.6 %collective-permute-start.6 = (bf16[4,4,40,768]{3,2,0,1:T(8,128)(2,1)S(1)}, bf16[4,4,40,768]{3,2,0,1:T(8,128)(2,1)S(1)}, u32[]{:S(2)}, u32[]{:S(2)}) collective-permute-start(bf16[4,4,40,768]{3,2,0,1:T(8,128)(2,1)S(1)} %bitcast_dynamic-update-slice_fusion.7), channel_id=1, source_target_pairs={{0,1},{1,0},{2,3},{3,2},{4,5},{5,4},{6,7},{7,6},{8,9},{9,8},{10,11... | collective-permute-start | bytes 2949128 | tf_op jit(solution)/shard_map/ppermute | solution.py:27
  61.7 39.5 %all-to-all-start.1 = ((bf16[4,256,1024]{2,1,0:T(8,128)(2,1)}), bf16[4,256,1024]{2,1,0:T(8,128)(2,1)}, u32[]{:S(2)}, u32[]{:S(2)}) async-start(bf16[4,256,1024]{2,1,0:T(8,128)(2,1)} %broadcast_in_dim.149), calls=%async_computation.1 | async-start | bytes 4194304 | tf_op jit(solution)/shard_map/all_to_all | solution.py:114
  83.3 8.9 %collective-permute-start.7 = (bf16[32,1024]{1,0:T(8,128)(2,1)S(1)}, bf16[32,1024]{1,0:T(8,128)(2,1)S(1)}, u32[]{:S(2)}, u32[]{:S(2)}) collective-permute-start(bf16[32,1024]{1,0:T(8,128)(2,1)S(1)} %copy-done.40), channel_id=1, source_target_pairs={{0,2},{1,3},{2,0},{3,1},{4,6},{5,7},{6,4},{7,5},{8,10},{9,11},{10,... | collective-permute-start | bytes 196616 | tf_op jit(solution)/shard_map/ppermute | solution.py:27
  88.1 9.9 %collective-permute-start.9 = (bf16[32,1024]{1,0:T(8,128)(2,1)S(1)}, bf16[32,1024]{1,0:T(8,128)(2,1)S(1)}, u32[]{:S(2)}, u32[]{:S(2)}) collective-permute-start(bf16[32,1024]{1,0:T(8,128)(2,1)S(1)} %copy-done.40), channel_id=1, source_target_pairs={{0,6},{1,7},{2,4},{3,5},{4,2},{5,3},{6,0},{7,1},{8,14},{9,15},{10,... | collective-permute-start | bytes 196616 | tf_op jit(solution)/shard_map/ppermute | solution.py:27
  98.1 19.4 %collective-permute-start.10 = (bf16[4,32,1024]{2,1,0:T(8,128)(2,1)S(1)}, bf16[4,32,1024]{2,1,0:T(8,128)(2,1)}, u32[]{:S(2)}, u32[]{:S(2)}) collective-permute-start(bf16[4,32,1024]{2,1,0:T(8,128)(2,1)S(1)} %bitcast_dynamic-update-slice_fusion.8), channel_id=1, source_target_pairs={{0,8},{8,0},{16,24},{24,16},{1,9},{9,1},{17,25},{25,17},{2,10},{10... | collective-permute-start | bytes 786440 | tf_op jit(solution)/shard_map/ppermute | solution.py:27
  99.9 17.6 %collective-permute-start.11 = (bf16[4,32,1024]{2,1,0:T(8,128)(2,1)S(1)}, bf16[4,32,1024]{2,1,0:T(8,128)(2,1)}, u32[]{:S(2)}, u32[]{:S(2)}) collective-permute-start(bf16[4,32,1024]{2,1,0:T(8,128)(2,1)S(1)} %bitcast_dynamic-update-slice_fusion.8), channel_id=1, source_target_pairs={{0,16},{8,24},{16,0},{24,8},{1,17},{9,25},{17,1},{25,9},{2,18},{10... | collective-permute-start | bytes 786440 | tf_op jit(solution)/shard_map/ppermute | solution.py:27
  101.2 16.3 %collective-permute-start.12 = (bf16[4,32,1024]{2,1,0:T(8,128)(2,1)S(1)}, bf16[4,32,1024]{2,1,0:T(8,128)(2,1)}, u32[]{:S(2)}, u32[]{:S(2)}) collective-permute-start(bf16[4,32,1024]{2,1,0:T(8,128)(2,1)S(1)} %bitcast_dynamic-update-slice_fusion.8), channel_id=1, source_target_pairs={{0,24},{8,16},{16,8},{24,0},{1,25},{9,17},{17,9},{25,1},{2,26},{10... | collective-permute-start | bytes 786440 | tf_op jit(solution)/shard_map/ppermute | solution.py:27
  124.4 9.0 %collective-permute-start.13 = (bf16[4,4,32,1024]{3,2,1,0:T(8,128)(2,1)}, bf16[4,4,32,1024]{3,2,1,0:T(8,128)(2,1)}, u32[]{:S(2)}, u32[]{:S(2)}) collective-permute-start(bf16[4,4,32,1024]{3,2,1,0:T(8,128)(2,1)} %bitcast_dynamic-update-slice_fusion), channel_id=1, source_target_pairs={{0,1},{1,0},{2,3},{3,2},{4,5},{5,4},{6,7},{7,6},{8,9},{9,8},{10,11... | collective-permute-start | bytes 3145736 | tf_op jit(solution)/shard_map/ppermute | solution.py:27
  128.8 24.8 %all-to-all-start.2 = ((bf16[4,256,512]{2,1,0:T(8,128)(2,1)}), bf16[4,256,512]{2,1,0:T(8,128)(2,1)}, u32[]{:S(2)}, u32[]{:S(2)}) async-start(bf16[4,256,512]{2,1,0:T(8,128)(2,1)} %pad_maximum_fusion.9), calls=%async_computation.2 | async-start | bytes 2097152 | tf_op jit(solution)/shard_map/all_to_all | solution.py:114
  133.1 172.5 %reduce-scatter.6.cloned.1.call-start = ((), (), s32[]{:S(2)}) async-start(), calls=%async_computation.8 | async-start | bytes 5242880 | tf_op jit(solution)/shard_map/reduce_scatter | solution.py:368
  159.0 18.1 %collective-permute-start.14 = (bf16[512,1024]{1,0:T(8,128)(2,1)}, bf16[512,1024]{1,0:T(8,128)(2,1)}, u32[]{:S(2)}, u32[]{:S(2)}) collective-permute-start(bf16[512,1024]{1,0:T(8,128)(2,1)} %fusion.32), channel_id=1, source_target_pairs={{0,1},{1,0},{2,3},{3,2},{4,5},{5,4},{6,7},{7,6},{8,9},{9,8},{10,11... | collective-permute-start | bytes 3145736 | tf_op jit(solution)/shard_map/ppermute | solution.py:27
  226.5 6.2 %collective-permute-start.18 = (bf16[512,1024]{1,0:T(8,128)(2,1)S(1)}, bf16[512,1024]{1,0:T(8,128)(2,1)S(1)}, u32[]{:S(2)}, u32[]{:S(2)}) collective-permute-start(bf16[512,1024]{1,0:T(8,128)(2,1)S(1)} %convolution_convert_fusion.5), channel_id=1, source_target_pairs={{0,1},{1,0},{2,3},{3,2},{4,5},{5,4},{6,7},{7,6},{8,9},{9,8},{10,11... | collective-permute-start | bytes 3145736 | tf_op jit(solution)/shard_map/ppermute | solution.py:27
  240.3 19.0 %all-to-all-start.3 = ((bf16[4,256,512]{2,1,0:T(8,128)(2,1)}), bf16[4,256,512]{2,1,0:T(8,128)(2,1)}, u32[]{:S(2)}, u32[]{:S(2)}) async-start(bf16[4,256,512]{2,1,0:T(8,128)(2,1)} %bitcast.304), calls=%async_computation.3 | async-start | bytes 2097152 | tf_op jit(solution)/shard_map/all_to_all | solution.py:114
  244.6 125.9 %reduce-scatter.10.cloned.1.call-start = ((), (), s32[]{:S(2)}) async-start(), calls=%async_computation.11 | async-start | bytes 6553600
  254.7 11.9 %collective-permute-start.32 = (bf16[4,4,32,1024]{3,2,1,0:T(8,128)(2,1)}, bf16[4,4,32,1024]{3,2,1,0:T(8,128)(2,1)}, u32[]{:S(2)}, u32[]{:S(2)}) collective-permute-start(bf16[4,4,32,1024]{3,2,1,0:T(8,128)(2,1)} %dynamic-slice_bitcast_fusion), channel_id=1, source_target_pairs={{0,1},{1,0},{2,3},{3,2},{4,5},{5,4},{6,7},{7,6},{8,9},{9,8},{10,11... | collective-permute-start | bytes 3145736 | tf_op jit(solution)/shard_map/ppermute | solution.py:27
  297.0 42.5 %all-to-all-start.4 = ((bf16[4,256,1024]{2,1,0:T(8,128)(2,1)}), bf16[4,256,1024]{2,1,0:T(8,128)(2,1)}, u32[]{:S(2)}, u32[]{:S(2)}) async-start(bf16[4,256,1024]{2,1,0:T(8,128)(2,1)} %bitcast.284), calls=%async_computation.4 | async-start | bytes 4194304 | tf_op jit(solution)/shard_map/all_to_all | solution.py:114
  301.6 106.7 %reduce-scatter.8.cloned.1.call-start = ((), (), s32[]{:S(2)}) async-start(), calls=%async_computation.9 | async-start | bytes 1638400 | tf_op jit(solution)/shard_map/reduce_scatter | solution.py:438
  307.6 31.9 %collective-permute-start.19 = (bf16[128,1024]{1,0:T(8,128)(2,1)}, bf16[128,1024]{1,0:T(8,128)(2,1)}, u32[]{:S(2)}, u32[]{:S(2)}) collective-permute-start(bf16[128,1024]{1,0:T(8,128)(2,1)} %get-tuple-element.185), channel_id=1, source_target_pairs={{0,2},{1,3},{2,0},{3,1},{4,6},{5,7},{6,4},{7,5},{8,10},{9,11},{10,... | collective-permute-start | bytes 786440 | tf_op jit(solution)/shard_map/ppermute | solution.py:27
  308.7 30.8 %collective-permute-start.20 = (bf16[128,1024]{1,0:T(8,128)(2,1)}, bf16[128,1024]{1,0:T(8,128)(2,1)}, u32[]{:S(2)}, u32[]{:S(2)}) collective-permute-start(bf16[128,1024]{1,0:T(8,128)(2,1)} %get-tuple-element.184), channel_id=1, source_target_pairs={{0,4},{1,5},{2,6},{3,7},{4,0},{5,1},{6,2},{7,3},{8,12},{9,13},{10,... | collective-permute-start | bytes 786440 | tf_op jit(solution)/shard_map/ppermute | solution.py:27
  310.9 28.6 %collective-permute-start.21 = (bf16[128,1024]{1,0:T(8,128)(2,1)S(1)}, bf16[128,1024]{1,0:T(8,128)(2,1)}, u32[]{:S(2)}, u32[]{:S(2)}) collective-permute-start(bf16[128,1024]{1,0:T(8,128)(2,1)S(1)} %get-tuple-element.183), channel_id=1, source_target_pairs={{0,6},{1,7},{2,4},{3,5},{4,2},{5,3},{6,0},{7,1},{8,14},{9,15},{10,... | collective-permute-start | bytes 786440 | tf_op jit(solution)/shard_map/ppermute | solution.py:27
  346.0 7.9 %collective-permute-start.25 = (bf16[4,4,40,768]{3,2,0,1:T(8,128)(2,1)}, bf16[4,4,40,768]{3,2,0,1:T(8,128)(2,1)}, u32[]{:S(2)}, u32[]{:S(2)}) collective-permute-start(bf16[4,4,40,768]{3,2,0,1:T(8,128)(2,1)} %bitcast.259), channel_id=1, source_target_pairs={{0,1},{1,0},{2,3},{3,2},{4,5},{5,4},{6,7},{7,6},{8,9},{9,8},{10,11... | collective-permute-start | bytes 2949128 | tf_op jit(solution)/shard_map/ppermute | solution.py:27
  351.2 46.6 %collective-permute-start.22 = (bf16[256,1024]{1,0:T(8,128)(2,1)}, bf16[256,1024]{1,0:T(8,128)(2,1)S(1)}, u32[]{:S(2)}, u32[]{:S(2)}) collective-permute-start(bf16[256,1024]{1,0:T(8,128)(2,1)} %get-tuple-element.179), channel_id=1, source_target_pairs={{0,8},{8,0},{16,24},{24,16},{1,9},{9,1},{17,25},{25,17},{2,10},{10... | collective-permute-start | bytes 1572872 | tf_op jit(solution)/shard_map/ppermute | solution.py:27
  352.4 45.4 %collective-permute-start.23 = (bf16[256,1024]{1,0:T(8,128)(2,1)}, bf16[256,1024]{1,0:T(8,128)(2,1)}, u32[]{:S(2)}, u32[]{:S(2)}) collective-permute-start(bf16[256,1024]{1,0:T(8,128)(2,1)} %get-tuple-element.178), channel_id=1, source_target_pairs={{0,16},{8,24},{16,0},{24,8},{1,17},{9,25},{17,1},{25,9},{2,18},{10... | collective-permute-start | bytes 1572872 | tf_op jit(solution)/shard_map/ppermute | solution.py:27
  353.7 44.2 %collective-permute-start.24 = (bf16[256,1024]{1,0:T(8,128)(2,1)}, bf16[256,1024]{1,0:T(8,128)(2,1)}, u32[]{:S(2)}, u32[]{:S(2)}) collective-permute-start(bf16[256,1024]{1,0:T(8,128)(2,1)} %get-tuple-element.177), channel_id=1, source_target_pairs={{0,24},{8,16},{16,8},{24,0},{1,25},{9,17},{17,9},{25,1},{2,26},{10... | collective-permute-start | bytes 1572872 | tf_op jit(solution)/shard_map/ppermute | solution.py:27
  356.2 14.3 %collective-permute-start.28 = (bf16[4,40,768]{2,1,0:T(8,128)(2,1)}, bf16[4,40,768]{2,1,0:T(8,128)(2,1)}, u32[]{:S(2)}, u32[]{:S(2)}) collective-permute-start(bf16[4,40,768]{2,1,0:T(8,128)(2,1)} %get-tuple-element.189), channel_id=1, source_target_pairs={{0,6},{1,7},{2,4},{3,5},{4,2},{5,3},{6,0},{7,1},{8,14},{9,15},{10,... | collective-permute-start | bytes 737288 | tf_op jit(solution)/shard_map/ppermute | solution.py:27
  361.1 19.2 %collective-permute-start.27 = (bf16[4,40,768]{2,1,0:T(8,128)(2,1)}, bf16[4,40,768]{2,1,0:T(8,128)(2,1)}, u32[]{:S(2)}, u32[]{:S(2)}) collective-permute-start(bf16[4,40,768]{2,1,0:T(8,128)(2,1)} %get-tuple-element.190), channel_id=1, source_target_pairs={{0,4},{1,5},{2,6},{3,7},{4,0},{5,1},{6,2},{7,3},{8,12},{9,13},{10,... | collective-permute-start | bytes 737288 | tf_op jit(solution)/shard_map/ppermute | solution.py:27
  370.5 26.2 %collective-permute-start.26 = (bf16[4,40,768]{2,1,0:T(8,128)(2,1)S(1)}, bf16[4,40,768]{2,1,0:T(8,128)(2,1)S(1)}, u32[]{:S(2)}, u32[]{:S(2)}) collective-permute-start(bf16[4,40,768]{2,1,0:T(8,128)(2,1)S(1)} %get-tuple-element.188), channel_id=1, source_target_pairs={{0,2},{1,3},{2,0},{3,1},{4,6},{5,7},{6,4},{7,5},{8,10},{9,11},{10,... | collective-permute-start | bytes 737288 | tf_op jit(solution)/shard_map/ppermute | solution.py:27
  (66 other events, 386.2 us)
Sparse Core Ops, SparseCore 0:
  12.6 159.0 all-gather.2
  218.4 58.5 reduce-scatter.5
  280.3 90.1 reduce-scatter.9
  372.7 35.4 reduce-scatter.7
